TPU v7x, 32 devices: a whole 2x2x4 slice. The times are simulated.
32 devices in a mesh: wide: 8 (over z, core), narrow: 4 (over y, x).
Axes of the slice: x: 2, y: 2, z: 4, core: 2. Of those that a mesh axis runs over, the one named last changes fastest.
Arguments:
- tokens: bfloat16 [4, 8, 4, 256, 768], P('narrow', 'wide'), may hold values from -6 to 6
- segment_ids: int32 [4, 8, 4, 256], P('narrow', 'wide'), may hold values from -1 to 7, as said below
- cotangent: bfloat16 [4, 8, 4, 256, 768], P('narrow', 'wide'), may hold values from -6 to 6
- w_qkv: bfloat16 [768, 2304], replicated, may hold values from -0.21875 to 0.21875
- b_qv: float32 [1536], replicated, may hold values from -3 to 3
- w_out: bfloat16 [768, 768], replicated, may hold values from -0.875 to 0.875
- b_out: float32 [768], replicated, may hold values from -3 to 3
- ls_attn: float32 [768], replicated, may hold values from 0.25 to 1.75
- ln1_gain: float32 [768], replicated, may hold values from 0.25 to 1.75
- ln1_bias: float32 [768], replicated, may hold values from -3 to 3
- ln2_gain: float32 [768], replicated, may hold values from 0.25 to 1.75
- ln2_bias: float32 [768], replicated, may hold values from -3 to 3
- w_fc1: bfloat16 [768, 3072], replicated, may hold values from -0.21875 to 0.21875
- b_fc1: float32 [3072], replicated, may hold values from -3 to 3
- w_fc2: bfloat16 [3072, 768], replicated, may hold values from -0.109375 to 0.109375
- b_fc2: float32 [768], replicated, may hold values from -3 to 3
- ls_mlp: float32 [768], replicated, may hold values from 0.25 to 1.75
Outputs:
- output: bfloat16 [4, 8, 4, 256, 768], P('narrow', 'wide')
- grad_tokens: bfloat16 [4, 8, 4, 256, 768], P('narrow', 'wide')
- grad_w_qkv: float32 [768, 2304], P('narrow')
- grad_b_qv: float32 [1536], P('narrow')
- grad_w_out: float32 [768, 768], P('narrow')
- grad_b_out: float32 [768], P('narrow')
- grad_ls_attn: float32 [768], P('narrow')
- grad_ln1_gain: float32 [768], P('narrow')
- grad_ln1_bias: float32 [768], P('narrow')
- grad_ln2_gain: float32 [768], P('narrow')
- grad_ln2_bias: float32 [768], P('narrow')
- grad_w_fc1: float32 [768, 3072], P('narrow')
- grad_b_fc1: float32 [3072], P('narrow')
- grad_w_fc2: float32 [3072, 768], P('narrow')
- grad_b_fc2: float32 [768], P('narrow')
- grad_ls_mlp: float32 [768], P('narrow')
Inputs may be any that keep to these rules, and one draw needn't show every extreme that they name: `segment_ids`: in each block, images take consecutive slots from the block's first slot on; the slots of one image share an id of 0 to 7 and different images of a block have different ids; -1 marks the padding after the last image. An image holds k * k + 5 slots for a whole k, at most 1374 and at most 2048; the first image of block 0 is the longest such image.
All inputs are finite; a program needn't handle non-finite values.
Results may differ from a plain program's by a relative error of at most 0.018.
Values may be sent and summed in bfloat16 or wider, within the bound.
A program may use at most 256 MiB of HBM per device.

v0:
```python
import jax
import jax.numpy as jnp
from jax import lax
from jax.sharding import PartitionSpec as P

D = 768
HEADS = 12
HEAD = 64
GROUPS = 4
QROWS = 512


EPSILON = 1e-06
ROOT_HALF = 0.7071067811865476


def layer_norm(values, gain, bias):
    average = jnp.mean(values, -1, keepdims=True)
    centred = values - average
    variance = jnp.mean(centred * centred, -1, keepdims=True)
    return centred * lax.rsqrt(variance + EPSILON) * gain + bias


def gelu_exact(values):
    return 0.5 * values * (1.0 + lax.erf(values * ROOT_HALF))


def per_device(
    tokens,
    segment_ids,
    cotangent,
    w_qkv,
    b_qv,
    w_out,
    b_out,
    ls_attn,
    ln1_gain,
    ln1_bias,
    ln2_gain,
    ln2_bias,
    w_fc1,
    b_fc1,
    w_fc2,
    b_fc2,
    ls_mlp,
):
    span_count = lax.axis_size("wide")
    head_groups = span_count // GROUPS
    group_heads = HEADS // head_groups
    head_cols = group_heads * HEAD
    piece_rows = tokens.shape[3]
    local_rows = GROUPS * piece_rows
    block_rows = span_count * piece_rows
    query_blocks = block_rows // QROWS
    score_scale = HEAD ** (-0.5)
    slot_ids = segment_ids.reshape(GROUPS, piece_rows)
    valid_rows = (slot_ids >= 0).astype(jnp.float32).reshape(local_rows, 1)
    inputs = tokens.reshape(local_rows, D).astype(jnp.float32)
    normed, norm_first_back = jax.vjp(layer_norm, inputs, ln1_gain, ln1_bias)
    normed_low = normed.astype(jnp.bfloat16)
    bias_all = jnp.concatenate([b_qv[:D], jnp.zeros((D,), jnp.float32), b_qv[D:]])
    qkv_low = (jnp.dot(normed_low, w_qkv, preferred_element_type=jnp.float32) + bias_all).astype(
        jnp.bfloat16
    )
    outgoing = qkv_low.reshape(GROUPS, piece_rows, 3, head_groups, head_cols).transpose(
        0, 3, 1, 2, 4
    )
    outgoing = outgoing.reshape(GROUPS * head_groups, piece_rows * 3 * head_cols)
    id_outgoing = jnp.broadcast_to(slot_ids[:, None, :], (GROUPS, head_groups, piece_rows))
    id_outgoing = id_outgoing.reshape(GROUPS * head_groups, piece_rows)
    arrived, block_ids = (
        lax.all_to_all(outgoing, "wide", split_axis=0, concat_axis=0, tiled=True),
        lax.all_to_all(id_outgoing, "wide", split_axis=0, concat_axis=0, tiled=True),
    )
    triples = arrived.reshape(block_rows, 3, group_heads, HEAD)
    query_all = triples[:, 0]
    key_all = triples[:, 1]
    value_all = triples[:, 2]
    block_ids = block_ids.reshape(block_rows)
    query_split = query_all.reshape(query_blocks, QROWS, group_heads, HEAD)
    id_split = block_ids.reshape(query_blocks, QROWS)

    def masked_scores(query_block, id_block):
        raw_scores = (
            jnp.einsum("qhd,khd->hqk", query_block, key_all, preferred_element_type=jnp.float32)
            * score_scale
        )
        same_image = id_block[:, None] == block_ids[None, :]
        return jnp.where(same_image[None], raw_scores, -1e30)

    def attend_rows(pair):
        scores = masked_scores(pair[0], pair[1])
        row_max = jnp.max(scores, -1, keepdims=True)
        shifted = jnp.exp(scores - row_max)
        row_total = jnp.sum(shifted, -1, keepdims=True)
        soft_low = (shifted / row_total).astype(jnp.bfloat16)
        mixed_block = jnp.einsum(
            "hqk,khd->qhd", soft_low, value_all, preferred_element_type=jnp.float32
        )
        return (mixed_block.astype(jnp.bfloat16), (row_max + jnp.log(row_total))[:, :, 0])

    mixed_heads, log_totals = lax.map(attend_rows, (query_split, id_split))
    homeward = mixed_heads.reshape(span_count, piece_rows * head_cols)
    returned = lax.all_to_all(homeward, "wide", split_axis=0, concat_axis=0, tiled=True)
    mixed_rows = (
        returned.reshape(GROUPS, head_groups, piece_rows, head_cols)
        .transpose(0, 2, 1, 3)
        .reshape(local_rows, D)
    )
    projected = jnp.dot(mixed_rows, w_out, preferred_element_type=jnp.float32) + b_out
    hidden = inputs + ls_attn * projected
    second, norm_second_back = jax.vjp(layer_norm, hidden, ln2_gain, ln2_bias)
    second_low = second.astype(jnp.bfloat16)
    pre_act = jnp.dot(second_low, w_fc1, preferred_element_type=jnp.float32) + b_fc1
    activation, gelu_back = jax.vjp(gelu_exact, pre_act)
    act_low = activation.astype(jnp.bfloat16)
    mlp_out = jnp.dot(act_low, w_fc2, preferred_element_type=jnp.float32) + b_fc2
    result = ((hidden + ls_mlp * mlp_out) * valid_rows).astype(jnp.bfloat16).reshape(tokens.shape)
    grad_out = cotangent.reshape(local_rows, D).astype(jnp.float32) * valid_rows
    grad_ls_mlp = jnp.sum(grad_out * mlp_out, 0)
    grad_mlp = (ls_mlp * grad_out).astype(jnp.bfloat16)
    grad_b_fc2 = jnp.sum(grad_mlp.astype(jnp.float32), 0)
    grad_w_fc2 = jnp.einsum("tf,td->fd", act_low, grad_mlp, preferred_element_type=jnp.float32)
    grad_act = jnp.dot(grad_mlp, w_fc2.T, preferred_element_type=jnp.float32)
    grad_pre = gelu_back(grad_act)[0].astype(jnp.bfloat16)
    grad_b_fc1 = jnp.sum(grad_pre.astype(jnp.float32), 0)
    grad_w_fc1 = jnp.einsum("td,tf->df", second_low, grad_pre, preferred_element_type=jnp.float32)
    grad_second = jnp.dot(grad_pre, w_fc1.T, preferred_element_type=jnp.float32)
    grad_hidden_norm, grad_ln2_gain, grad_ln2_bias = norm_second_back(grad_second)
    grad_hidden = grad_out + grad_hidden_norm
    grad_ls_attn = jnp.sum(grad_hidden * projected, 0)
    grad_proj = (ls_attn * grad_hidden).astype(jnp.bfloat16)
    grad_b_out = jnp.sum(grad_proj.astype(jnp.float32), 0)
    grad_w_out = jnp.einsum("td,te->de", mixed_rows, grad_proj, preferred_element_type=jnp.float32)
    grad_mixed = jnp.dot(grad_proj, w_out.T, preferred_element_type=jnp.float32).astype(
        jnp.bfloat16
    )
    outward = grad_mixed.reshape(GROUPS, piece_rows, head_groups, head_cols).transpose(0, 2, 1, 3)
    outward = outward.reshape(GROUPS * head_groups, piece_rows * head_cols)
    grad_heads = lax.all_to_all(outward, "wide", split_axis=0, concat_axis=0, tiled=True).reshape(
        query_blocks, QROWS, group_heads, HEAD
    )

    def attend_back(sums, inputs_block):
        grad_keys, grad_values = sums
        query_block, id_block, lse_block, grad_block = inputs_block
        scores = masked_scores(query_block, id_block)
        soft = jnp.exp(scores - lse_block[:, :, None])
        grad_soft = jnp.einsum(
            "qhd,khd->hqk", grad_block, value_all, preferred_element_type=jnp.float32
        )
        grad_values = grad_values + jnp.einsum(
            "hqk,qhd->khd",
            soft.astype(jnp.bfloat16),
            grad_block,
            preferred_element_type=jnp.float32,
        )
        inner_sum = jnp.sum(soft * grad_soft, -1, keepdims=True)
        grad_scores = (soft * (grad_soft - inner_sum)).astype(jnp.bfloat16)
        grad_query = (
            jnp.einsum("hqk,khd->qhd", grad_scores, key_all, preferred_element_type=jnp.float32)
            * score_scale
        )
        grad_keys = (
            grad_keys
            + jnp.einsum(
                "hqk,qhd->khd", grad_scores, query_block, preferred_element_type=jnp.float32
            )
            * score_scale
        )
        return ((grad_keys, grad_values), grad_query)

    zeros_block = jnp.zeros((block_rows, group_heads, HEAD), jnp.float32)
    (grad_keys, grad_values), grad_queries = lax.scan(
        attend_back, (zeros_block, zeros_block), (query_split, id_split, log_totals, grad_heads)
    )
    grad_triples = jnp.stack(
        [grad_queries.reshape(block_rows, group_heads, HEAD), grad_keys, grad_values], 1
    )
    grad_triples = grad_triples.astype(jnp.bfloat16).reshape(span_count, piece_rows * 3 * head_cols)
    back_home = lax.all_to_all(grad_triples, "wide", split_axis=0, concat_axis=0, tiled=True)
    grad_qkv = back_home.reshape(GROUPS, head_groups, piece_rows, 3, head_cols).transpose(
        0, 2, 3, 1, 4
    )
    grad_qkv = grad_qkv.reshape(local_rows, 3 * D)
    qkv_sums = jnp.sum(grad_qkv.astype(jnp.float32), 0)
    grad_b_qv = jnp.concatenate([qkv_sums[:D], qkv_sums[2 * D :]])
    grad_w_qkv = jnp.einsum("td,te->de", normed_low, grad_qkv, preferred_element_type=jnp.float32)
    grad_normed = jnp.dot(grad_qkv, w_qkv.T, preferred_element_type=jnp.float32)
    grad_inputs_norm, grad_ln1_gain, grad_ln1_bias = norm_first_back(grad_normed)
    grad_tokens = (grad_hidden + grad_inputs_norm).astype(jnp.bfloat16).reshape(tokens.shape)
    shares = (
        lax.psum_scatter(
            grad_w_qkv.astype(jnp.bfloat16), "narrow", scatter_dimension=0, tiled=True
        ).astype(jnp.float32),
        lax.psum_scatter(
            grad_b_qv.astype(jnp.bfloat16), "narrow", scatter_dimension=0, tiled=True
        ).astype(jnp.float32),
        lax.psum_scatter(
            grad_w_out.astype(jnp.bfloat16), "narrow", scatter_dimension=0, tiled=True
        ).astype(jnp.float32),
        lax.psum_scatter(
            grad_b_out.astype(jnp.bfloat16), "narrow", scatter_dimension=0, tiled=True
        ).astype(jnp.float32),
        lax.psum_scatter(
            grad_ls_attn.astype(jnp.bfloat16), "narrow", scatter_dimension=0, tiled=True
        ).astype(jnp.float32),
        lax.psum_scatter(
            grad_ln1_gain.astype(jnp.bfloat16), "narrow", scatter_dimension=0, tiled=True
        ).astype(jnp.float32),
        lax.psum_scatter(
            grad_ln1_bias.astype(jnp.bfloat16), "narrow", scatter_dimension=0, tiled=True
        ).astype(jnp.float32),
        lax.psum_scatter(
            grad_ln2_gain.astype(jnp.bfloat16), "narrow", scatter_dimension=0, tiled=True
        ).astype(jnp.float32),
        lax.psum_scatter(
            grad_ln2_bias.astype(jnp.bfloat16), "narrow", scatter_dimension=0, tiled=True
        ).astype(jnp.float32),
        lax.psum_scatter(
            grad_w_fc1.astype(jnp.bfloat16), "narrow", scatter_dimension=0, tiled=True
        ).astype(jnp.float32),
        lax.psum_scatter(
            grad_b_fc1.astype(jnp.bfloat16), "narrow", scatter_dimension=0, tiled=True
        ).astype(jnp.float32),
        lax.psum_scatter(
            grad_w_fc2.astype(jnp.bfloat16), "narrow", scatter_dimension=0, tiled=True
        ).astype(jnp.float32),
        lax.psum_scatter(
            grad_b_fc2.astype(jnp.bfloat16), "narrow", scatter_dimension=0, tiled=True
        ).astype(jnp.float32),
        lax.psum_scatter(
            grad_ls_mlp.astype(jnp.bfloat16), "narrow", scatter_dimension=0, tiled=True
        ).astype(jnp.float32),
    )
    outputs = (
        lax.psum(shares[0].astype(jnp.bfloat16), "wide").astype(jnp.float32),
        lax.psum(shares[1].astype(jnp.bfloat16), "wide").astype(jnp.float32),
        lax.psum(shares[2].astype(jnp.bfloat16), "wide").astype(jnp.float32),
        lax.psum(shares[3].astype(jnp.bfloat16), "wide").astype(jnp.float32),
        lax.psum(shares[4].astype(jnp.bfloat16), "wide").astype(jnp.float32),
        lax.psum(shares[5].astype(jnp.bfloat16), "wide").astype(jnp.float32),
        lax.psum(shares[6].astype(jnp.bfloat16), "wide").astype(jnp.float32),
        lax.psum(shares[7].astype(jnp.bfloat16), "wide").astype(jnp.float32),
        lax.psum(shares[8].astype(jnp.bfloat16), "wide").astype(jnp.float32),
        lax.psum(shares[9].astype(jnp.bfloat16), "wide").astype(jnp.float32),
        lax.psum(shares[10].astype(jnp.bfloat16), "wide").astype(jnp.float32),
        lax.psum(shares[11].astype(jnp.bfloat16), "wide").astype(jnp.float32),
        lax.psum(shares[12].astype(jnp.bfloat16), "wide").astype(jnp.float32),
        lax.psum(shares[13].astype(jnp.bfloat16), "wide").astype(jnp.float32),
    )
    return (
        result,
        grad_tokens,
        outputs[0],
        outputs[1],
        outputs[2],
        outputs[3],
        outputs[4],
        outputs[5],
        outputs[6],
        outputs[7],
        outputs[8],
        outputs[9],
        outputs[10],
        outputs[11],
        outputs[12],
        outputs[13],
    )


def solution(mesh):
    placed = (
        P("narrow", "wide", None, None, None),
        P("narrow", "wide", None, None),
        P("narrow", "wide", None, None, None),
        P(),
        P(),
        P(),
        P(),
        P(),
        P(),
        P(),
        P(),
        P(),
        P(),
        P(),
        P(),
        P(),
        P(),
    )
    return jax.shard_map(
        per_device,
        mesh=mesh,
        in_specs=placed,
        out_specs=(
            P("narrow", "wide", None, None, None),
            P("narrow", "wide", None, None, None),
            P("narrow", None),
            P("narrow"),
            P("narrow", None),
            P("narrow"),
            P("narrow"),
            P("narrow"),
            P("narrow"),
            P("narrow"),
            P("narrow"),
            P("narrow", None),
            P("narrow"),
            P("narrow", None),
            P("narrow"),
            P("narrow"),
        ),
        check_vma=False,
    )
```

profile of v0, /device:TPU:0, one launch (start us, length us, event | category | flops | bytes accessed | tf_op | source)
XLA Modules:
  0.0 1497.4 jit_solution(13206768497569784228)
XLA Ops:
  54.3 30.7 %reduce.18 = bf16[8,294912]{1,0:T(8,128)(2,1)} reduce(bf16[8,1,294912]{2,1,0:T(2,128)(2,1)} %all_to_all.40, bf16[]{:T(256)} %broadcast.266), dimensions={1}, to_apply=%all_to_all.40.reduce_sub_computation | reduce | bytes 9437186 | tf_op jit(solution)/shard_map/all_to_all | solution.py:72
  100.2 104.1 %all-to-all-done.1 = bf16[8,2,147456]{2,1,0:T(2,128)(2,1)} async-done(((bf16[8,2,147456]{2,1,0:T(2,128)(2,1)}), bf16[8,2,147456]{2,1,0:T(2,128)(2,1)}, u32[]{:S(2)}, u32[]{:S(2)}) %all-to-all-start.1) | async-done | bytes 4718624 | tf_op jit(solution)/shard_map/all_to_all | solution.py:72
  213.6 29.6 %reduce.9 = bf16[8,294912]{1,0:T(8,128)(2,1)} reduce(bf16[8,1,294912]{2,1,0:T(2,128)(2,1)} %reshape.375, bf16[]{:T(256)} %constant.122), dimensions={1}, to_apply=%all_to_all.34.reduce_sub_computation | reduce | bytes 9437186 | tf_op jit(solution)/shard_map/all_to_all | solution.py:72
  249.8 15.1 %reshape.341 = bf16[2048,3,6,64]{3,2,1,0:T(8,128)(2,1)} reshape(bf16[2359296]{0:T(1024)(128)(2,1)} %reshape.370) | data formatting | bytes 9437184 | tf_op jit(solution)/shard_map/reshape | solution.py:75
  289.0 165.4 %while.27 = (s32[]{:T(128)}, bf16[4,512,6,64]{1,3,2,0:T(8,128)(2,1)}, f32[4,6,512]{2,1,0:T(8,128)}, s32[4,512]{1,0:T(4,128)}, s32[8,256]{1,0:T(8,128)}, /*index=...) while((s32[]{:T(128)}, ...), condition=%wide.region_5.6_spmd, body=%wide.region_2.5_spmd.sunk | while | flops 1687352320 | bytes 90050176 | solution.py:102
  491.8 34.7 %all-to-all-done.2 = bf16[8,2,49152]{2,1,0:T(2,128)(2,1)} async-done(((bf16[8,2,49152]{2,1,0:T(2,128)(2,1)}), bf16[8,2,49152]{2,1,0:T(2,128)(2,1)}, u32[]{:S(2)}, u32[]{:S(2)}) %all-to-all-start.2) | async-done | bytes 1572896 | tf_op jit(solution)/shard_map/all_to_all | solution.py:104
  565.0 14.4 fusion.63
  651.6 28.3 %all-to-all-done.3 = bf16[8,2,49152]{2,1,0:T(2,128)(2,1)} async-done(((bf16[8,2,49152]{2,1,0:T(2,128)(2,1)}), bf16[8,2,49152]{2,1,0:T(2,128)(2,1)}, u32[]{:S(2)}, u32[]{:S(2)}) %all-to-all-start.3) | async-done | bytes 1572896 | tf_op jit(solution)/shard_map/all_to_all | solution.py:140
  713.1 365.3 %while.28 = (s32[]{:T(128)}, f32[2048,6,64]{0,2,1:T(8,128)}, f32[2048,6,64]{0,2,1:T(8,128)}, bf16[4,512,6,64]{1,3,2,0:T(8,128)(2,1)}, bf16[4,512,6,64]{1,3,2,0:T...) while((s32[]{:T(128)}, f32[2048,6,64]{0,2,1:T(8,128)}, ...), condition=%wide.region_12.13_spmd.clone, body=%wide.region_10.12_spmd.clone.sunk | while | flops 4126077952 | bytes 212718224 | solution.py:174
  731.3 18.9 %multiply_reduce_fusion.7 = (f32[6,512]{1,0:T(8,128)}, f32[6,512,2048]{2,1,0:T(8,128)}) fusion(f32[6,512,2048]{2,1,0:T(8,128)} %fusion.123, f32[6,512]{1,0:T(8,128)S(1)} %dynamic-slice_bitcast_fusion.2, pred[512,2048]{1,0:T(8,128)(4,1)} %broadcast_compare_fusion.5, bf16[2048,6,64]{0,2,1:T(8,128)(2,1)} %get-tuple-element.506, ...), kind=kOutput, calls=%fused_computation.19.clone.1 | convolution fusion | flops 836760576 | bytes 53371392 | tf_op jit(solution)/shard_map/while/body/eval_jaxpr/qhd,khd->hqk/dot_general | solution.py:149
  750.3 22.2 %multiply_convert_fusion.8 = bf16[6,512,2048]{2,1,0:T(8,128)(2,1)} fusion(f32[6,512,2048]{2,1,0:T(8,128)} %get-tuple-element.441, f32[6,512,2048]{2,1,0:T(8,128)} %fusion.123, f32[6,512]{1,0:T(8,128)} %get-tuple-element.442, f32[6,512]{1,0:T(8,128)S(1)} %dynamic-slice_bitcast_fusion.2, pred[512,2048]{1,0:T(8,128)(4,1)} %broadcast_compare_fusion.5), kind=kLoop, calls=%fused_computation.18.clone.1 | loop fusion | flops 37748736 | bytes 63987712 | tf_op jit(solution)/shard_map/while/body/eval_jaxpr/convert_element_type | solution.py:159
  821.0 18.8 %multiply_reduce_fusion.7 = (f32[6,512]{1,0:T(8,128)}, f32[6,512,2048]{2,1,0:T(8,128)}) fusion(f32[6,512,2048]{2,1,0:T(8,128)} %fusion.123, f32[6,512]{1,0:T(8,128)S(1)} %dynamic-slice_bitcast_fusion.2, pred[512,2048]{1,0:T(8,128)(4,1)} %broadcast_compare_fusion.5, bf16[2048,6,64]{0,2,1:T(8,128)(2,1)} %get-tuple-element.506, ...), kind=kOutput, calls=%fused_computation.19.clone.1 | convolution fusion | flops 836760576 | bytes 53371392 | tf_op jit(solution)/shard_map/while/body/eval_jaxpr/qhd,khd->hqk/dot_general | solution.py:149
  839.8 22.2 %multiply_convert_fusion.8 = bf16[6,512,2048]{2,1,0:T(8,128)(2,1)} fusion(f32[6,512,2048]{2,1,0:T(8,128)} %get-tuple-element.441, f32[6,512,2048]{2,1,0:T(8,128)} %fusion.123, f32[6,512]{1,0:T(8,128)} %get-tuple-element.442, f32[6,512]{1,0:T(8,128)S(1)} %dynamic-slice_bitcast_fusion.2, pred[512,2048]{1,0:T(8,128)(4,1)} %broadcast_compare_fusion.5), kind=kLoop, calls=%fused_computation.18.clone.1 | loop fusion | flops 37748736 | bytes 63987712 | tf_op jit(solution)/shard_map/while/body/eval_jaxpr/convert_element_type | solution.py:159
  912.4 18.8 %multiply_reduce_fusion.7 = (f32[6,512]{1,0:T(8,128)}, f32[6,512,2048]{2,1,0:T(8,128)}) fusion(f32[6,512,2048]{2,1,0:T(8,128)} %fusion.123, f32[6,512]{1,0:T(8,128)S(1)} %dynamic-slice_bitcast_fusion.2, pred[512,2048]{1,0:T(8,128)(4,1)} %broadcast_compare_fusion.5, bf16[2048,6,64]{0,2,1:T(8,128)(2,1)} %get-tuple-element.506, ...), kind=kOutput, calls=%fused_computation.19.clone.1 | convolution fusion | flops 836760576 | bytes 53371392 | tf_op jit(solution)/shard_map/while/body/eval_jaxpr/qhd,khd->hqk/dot_general | solution.py:149
  931.2 22.2 %multiply_convert_fusion.8 = bf16[6,512,2048]{2,1,0:T(8,128)(2,1)} fusion(f32[6,512,2048]{2,1,0:T(8,128)} %get-tuple-element.441, f32[6,512,2048]{2,1,0:T(8,128)} %fusion.123, f32[6,512]{1,0:T(8,128)} %get-tuple-element.442, f32[6,512]{1,0:T(8,128)S(1)} %dynamic-slice_bitcast_fusion.2, pred[512,2048]{1,0:T(8,128)(4,1)} %broadcast_compare_fusion.5), kind=kLoop, calls=%fused_computation.18.clone.1 | loop fusion | flops 37748736 | bytes 63987712 | tf_op jit(solution)/shard_map/while/body/eval_jaxpr/convert_element_type | solution.py:159
  1003.9 18.8 %multiply_reduce_fusion.7 = (f32[6,512]{1,0:T(8,128)}, f32[6,512,2048]{2,1,0:T(8,128)}) fusion(f32[6,512,2048]{2,1,0:T(8,128)} %fusion.123, f32[6,512]{1,0:T(8,128)S(1)} %dynamic-slice_bitcast_fusion.2, pred[512,2048]{1,0:T(8,128)(4,1)} %broadcast_compare_fusion.5, bf16[2048,6,64]{0,2,1:T(8,128)(2,1)} %get-tuple-element.506, ...), kind=kOutput, calls=%fused_computation.19.clone.1 | convolution fusion | flops 836760576 | bytes 53371392 | tf_op jit(solution)/shard_map/while/body/eval_jaxpr/qhd,khd->hqk/dot_general | solution.py:149
  1022.7 22.2 %multiply_convert_fusion.8 = bf16[6,512,2048]{2,1,0:T(8,128)(2,1)} fusion(f32[6,512,2048]{2,1,0:T(8,128)} %get-tuple-element.441, f32[6,512,2048]{2,1,0:T(8,128)} %fusion.123, f32[6,512]{1,0:T(8,128)} %get-tuple-element.442, f32[6,512]{1,0:T(8,128)S(1)} %dynamic-slice_bitcast_fusion.2, pred[512,2048]{1,0:T(8,128)(4,1)} %broadcast_compare_fusion.5), kind=kLoop, calls=%fused_computation.18.clone.1 | loop fusion | flops 37748736 | bytes 63987712 | tf_op jit(solution)/shard_map/while/body/eval_jaxpr/convert_element_type | solution.py:159
  1118.5 30.1 %reduce.21 = bf16[8,294912]{1,0:T(8,128)(2,1)} reduce(bf16[8,1,294912]{2,1,0:T(2,128)(2,1)} %convert_element_type.262, bf16[]{:T(256)} %broadcast.266), dimensions={1}, to_apply=%convert_element_type.262.reduce_sub_computation | reduce | bytes 9437186 | tf_op jit(solution)/shard_map/convert_element_type | solution.py:180
  1165.5 101.9 %all-to-all-done.4 = bf16[8,2,147456]{2,1,0:T(2,128)(2,1)} async-done(((bf16[8,2,147456]{2,1,0:T(2,128)(2,1)}), bf16[8,2,147456]{2,1,0:T(2,128)(2,1)}, u32[]{:S(2)}, u32[]{:S(2)}) %all-to-all-start.4) | async-done | bytes 4718624 | tf_op jit(solution)/shard_map/all_to_all | solution.py:181
  1276.8 29.8 %reduce.12 = bf16[8,294912]{1,0:T(8,128)(2,1)} reduce(bf16[8,1,294912]{2,1,0:T(2,128)(2,1)} %reshape.381, bf16[]{:T(256)} %constant.122), dimensions={1}, to_apply=%all_to_all.39.reduce_sub_computation | reduce | bytes 9437186 | tf_op jit(solution)/shard_map/all_to_all | solution.py:181
  1374.4 22.6 %reduce-scatter.5.cloned.1.call-done = bf16[192,2304]{1,0:T(8,128)(2,1)} async-done(((bf16[768,2304]{1,0:T(8,128)(2,1)}), bf16[192,2304]{1,0:T(8,128)(2,1)}) %reduce-scatter.5.cloned.1.call-update) | async-done | bytes 884752 | tf_op jit(solution)/shard_map/reduce_scatter | solution.py:193
  1411.0 16.5 %all-reduce.12 = (bf16[1536]{0:T(1024)(128)(2,1)S(1)}, bf16[768]{0:T(1024)(128)(2,1)}, bf16[768]{0:T(1024)(128)(2,1)}, bf16[768]{0:T(1024)(128)(2,1)}, bf16[768]...) all-reduce(bf16[1536]{0:T(1024)(128)(2,1)} %pad_maximum_fusion.2, ...), channel_id=3, replica_groups=mesh['wide'=8,'narrow'=4] {'narrow'}, use_global_device_ids=true, to_apply=%region_18.19.clone | all-reduce | flops 10752 | bytes 43008
  1437.1 14.6 all-reduce.10
  1462.7 21.2 %all-reduce.15.cloned.1.call-done = (bf16[192,2304]{1,0:T(8,128)(2,1)}, bf16[192,768]{1,0:T(8,128)(2,1)}, bf16[192,3072]{1,0:T(8,128)(2,1)}, bf16[768,768]{1,0:T(8,128)(2,1)}) async-done(((bf16[192,2304]{1,0:T(8,128)(2,1)}, bf16[192,768]{1,0:T(8,128)(2,1)}, bf16[192,3072]{1,0:T(8,128)(2,1)}, bf16[768,768]{1,0:T(8,128)(2,1)}), (bf16[192,2304]{1,0:T(8,128)(2,1)}, bf16[192,768]{1,0:T(8,128)(2,1)}, ...) | async-done | bytes 3538960 | tf_op jit(solution)/shard_map/psum | solution.py:237
  (306 shorter events, 822.0 us)
Async XLA Ops:
  7.2 13.6 copy-start
  7.2 12.9 copy-start.16
  7.2 12.9 copy-start.31
  8.7 85.2 %all-to-all-start = ((s32[8,1,256]{2,1,0:T(1,128)}), s32[8,1,256]{2,1,0:T(1,128)S(1)}, u32[]{:S(2)}, u32[]{:S(2)}) async-start(s32[8,1,256]{2,1,0:T(1,128)} %all_to_all.30), calls=%async_computation | async-start | bytes 16384 | tf_op jit(solution)/shard_map/all_to_all | solution.py:73
  93.9 110.4 %all-to-all-start.1 = ((bf16[8,2,147456]{2,1,0:T(2,128)(2,1)}), bf16[8,2,147456]{2,1,0:T(2,128)(2,1)}, u32[]{:S(2)}, u32[]{:S(2)}) async-start(bf16[8,2,147456]{2,1,0:T(2,128)(2,1)} %reshape.374), calls=%async_computation.1 | async-start | bytes 9437184 | tf_op jit(solution)/shard_map/all_to_all | solution.py:72
  305.5 12.7 copy-start.1
  346.8 12.7 copy-start.1
  388.1 12.7 copy-start.1
  429.4 12.7 copy-start.1
  480.4 8.3 copy-start.33
  484.3 42.1 %all-to-all-start.2 = ((bf16[8,2,49152]{2,1,0:T(2,128)(2,1)}), bf16[8,2,49152]{2,1,0:T(2,128)(2,1)}, u32[]{:S(2)}, u32[]{:S(2)}) async-start(bf16[8,2,49152]{2,1,0:T(2,128)(2,1)} %reshape.376), calls=%async_computation.2 | async-start | bytes 3145728 | tf_op jit(solution)/shard_map/all_to_all | solution.py:104
  488.6 885.8 %reduce-scatter.7.cloned.1.call-start = ((), (), s32[]{:S(2)}) async-start(), calls=%async_computation.10 | async-start | bytes 1474560 | tf_op jit(solution)/shard_map/reduce_scatter | solution.py:199
  488.7 98.4 %copy-start.24 = (f32[1,2,4,128]{3,1,2,0:T(2,128)}, f32[1,2,4,128]{3,1,2,0:T(2,128)S(1)}, u32[]{:S(2)}) copy-start(f32[1,2,4,128]{3,1,2,0:T(2,128)S(1)} %copy.96) | copy-start | bytes 12292
  552.6 33.0 %copy-start.5 = (f32[1024,768]{1,0:T(8,128)}, f32[1024,768]{1,0:T(8,128)S(1)}, u32[]{:S(2)}) copy-start(f32[1024,768]{1,0:T(8,128)S(1)} %get-tuple-element.294) | copy-start | bytes 9437188
  552.6 12.4 slice-start.2
  553.4 11.6 copy-start.10
  553.4 11.6 slice-start.3
  592.4 782.0 %reduce-scatter.9.cloned.1.call-start = ((), (), s32[]{:S(2)}) async-start(), calls=%async_computation.11 | async-start | bytes 5898240 | tf_op jit(solution)/shard_map/reduce_scatter | solution.py:220
  637.7 42.2 %all-to-all-start.3 = ((bf16[8,2,49152]{2,1,0:T(2,128)(2,1)}), bf16[8,2,49152]{2,1,0:T(2,128)(2,1)}, u32[]{:S(2)}, u32[]{:S(2)}) async-start(bf16[8,2,49152]{2,1,0:T(2,128)(2,1)} %reshape.378), calls=%async_computation.3 | async-start | bytes 3145728 | tf_op jit(solution)/shard_map/all_to_all | solution.py:140
  642.1 732.4 %reduce-scatter.11.cloned.1.call-start = ((), (), s32[]{:S(2)}) async-start(), calls=%async_computation.12 | async-start | bytes 5898240 | tf_op jit(solution)/shard_map/reduce_scatter | solution.py:226
  1157.5 110.0 %all-to-all-start.4 = ((bf16[8,2,147456]{2,1,0:T(2,128)(2,1)}), bf16[8,2,147456]{2,1,0:T(2,128)(2,1)}, u32[]{:S(2)}, u32[]{:S(2)}) async-start(bf16[8,2,147456]{2,1,0:T(2,128)(2,1)} %reshape.380), calls=%async_computation.4 | async-start | bytes 9437184 | tf_op jit(solution)/shard_map/all_to_all | solution.py:181
  1162.3 234.7 %reduce-scatter.5.cloned.1.call-start = ((), (), s32[]{:S(2)}) async-start(), calls=%async_computation.9 | async-start | bytes 4423680 | tf_op jit(solution)/shard_map/reduce_scatter | solution.py:193
  1350.7 133.1 %all-reduce.15.cloned.1.call-start = ((), (), s32[]{:S(2)}) async-start(), calls=%async_computation.13 | async-start | bytes 7077888 | tf_op jit(solution)/shard_map/psum | solution.py:237
  1371.5 25.5 %copy-start.25 = (f32[1,2,4,128]{3,1,2,0:T(2,128)S(1)}, f32[1,2,4,128]{3,1,2,0:T(2,128)}, u32[]{:S(2)}) copy-start(f32[1,2,4,128]{3,1,2,0:T(2,128)} %copy-done.24) | copy-start | bytes 12292
  (39 other events, 131.9 us)
Sparse Core Ops, SparseCore 0:
  592.6 27.5 reduce-scatter.6
  623.2 56.9 reduce-scatter.8
  683.1 56.9 reduce-scatter.10
  1350.8 46.1 reduce-scatter.4
  1399.5 84.2 all-reduce.14
where the time goes:
time: 1510 us; the launch traced here: 1500 us
  matrix products  465 us (31%)
  other arithmetic  369 us (24%)
  waiting for transfers between devices  313 us (21%)
  local copies, waits for them, and re-layouts  277 us (18%)
  blocking collectives  31.2 us (2%)
  starting transfers between devices  25.2 us (2%)
  between operations  16.6 us (1%)
    dot_general x8, matrix products, masked_scores(): jnp.einsum('qhd,khd->hqk', query_block, key_all, preferred_element_type=j...  111 us
    all_to_all x1, waiting for transfers between devices, per_device(): lax.all_to_all(outgoing, 'wide', split_axis=0, concat_axis=0, tiled=True)  104 us
    all_to_all x1, waiting for transfers between devices, per_device(): lax.all_to_all(grad_triples, 'wide', split_axis=0, concat_axis=0, tiled=T...  102 us
    convert_element_type x4, other arithmetic, attend_back(): grad_scores = (soft * (grad_soft - inner_sum)).astype(jnp.bfloat16)  88.9 us
    unnamed x126, local copies, waits for them, and re-layouts  87.9 us
    dot_general x4, matrix products, attend_back(): jnp.einsum('qhd,khd->hqk', grad_block, value_all, preferred_element_type=...  75.4 us
    all_to_all x2, other arithmetic, per_device(): lax.all_to_all(outgoing, 'wide', split_axis=0, concat_axis=0, tiled=True)  60.2 us
    dot_general x4, matrix products, attend_back(): jnp.einsum('hqk,qhd->khd', soft.astype(jnp.bfloat16), grad_block, preferr...  55.1 us
  transfers between devices with their start and end apart: 10, of which 6 were waited for; matrix products, arithmetic and copies ran while one was open for 49% of the time, Pallas kernels for 0%

commit v1 on v0

v1 whole, which is shorter than its diff:
```python
import functools
import jax
import jax.numpy as jnp
from jax import lax
from jax.experimental import pallas as pl
from jax.experimental.pallas import tpu as pltpu
from jax.sharding import PartitionSpec as P

D = 768
HEADS = 12
HEAD = 64
GROUPS = 4
TILE = 256
LANES = 128
EPSILON = 1e-06
ROOT_HALF = 0.7071067811865476
FAR = -1e30
F32 = jnp.float32
BF16 = jnp.bfloat16


def layer_norm(values, gain, bias):
    average = jnp.mean(values, -1, keepdims=True)
    centred = values - average
    variance = jnp.mean(centred * centred, -1, keepdims=True)
    return centred * lax.rsqrt(variance + EPSILON) * gain + bias


def gelu_exact(values):
    return 0.5 * values * (1.0 + lax.erf(values * ROOT_HALF))


def dot_nt(a, b):
    return lax.dot_general(a, b, (((1,), (1,)), ((), ())), preferred_element_type=F32)


def dot_nn(a, b):
    return jnp.dot(a, b, preferred_element_type=F32)


class Geometry:
    def __init__(self, wide, piece):
        self.wide = wide
        self.piece = piece
        self.peers = wide // GROUPS
        self.chunk = piece // self.peers
        self.rows = wide * self.chunk
        self.slots = wide * piece
        heads = HEADS // self.peers
        self.real_cols = heads * HEAD
        self.pairs = (heads + 1) // 2
        self.cols = self.pairs * LANES
        self.tiles = self.slots // TILE


def gather_rows(geo, own, parts, column, fill):
    for back, part in enumerate(parts):
        source = lax.rem(own - back + geo.peers, geo.peers)
        for span in range(geo.wide):
            offset = pl.multiple_of(span * geo.piece + source * geo.chunk, geo.chunk)
            fill(offset, part[span, :, pl.ds(pl.multiple_of(column, LANES), LANES)])


def scatter_rows(geo, own, parts, column, source_ref):
    for back, part in enumerate(parts):
        source = lax.rem(own - back + geo.peers, geo.peers)
        for span in range(geo.wide):
            offset = pl.multiple_of(span * geo.piece + source * geo.chunk, geo.chunk)
            part[span, :, pl.ds(pl.multiple_of(column, LANES), LANES)] = source_ref[
                pl.ds(offset, geo.chunk), :
            ]


def attend_kernel(geo, table, *refs):
    peers = geo.peers
    qkv = refs[:peers]
    key_marks, query_marks = refs[peers : peers + 2]
    mixed = refs[peers + 2 : 2 * peers + 2]
    lse = refs[2 * peers + 2]
    ka, qa, vn, vt, ob = refs[2 * peers + 3 :]
    pair = pl.program_id(0)
    own = table[0]
    first = lax.broadcasted_iota(jnp.int32, (geo.chunk, LANES), 1) < HEAD

    def put_query(offset, values):
        marks = query_marks[pl.ds(offset, geo.chunk), :]
        scaled = values * 0.125
        qa[0, pl.ds(offset, geo.chunk), :] = jnp.where(first, scaled, marks)
        qa[1, pl.ds(offset, geo.chunk), :] = jnp.where(first, marks, scaled)

    def put_key(offset, values):
        marks = key_marks[pl.ds(offset, geo.chunk), :]
        ka[0, pl.ds(offset, geo.chunk), :] = jnp.where(first, values, marks)
        ka[1, pl.ds(offset, geo.chunk), :] = jnp.where(first, marks, values)

    def put_value(offset, values):
        vn[pl.ds(offset, geo.chunk), :] = values

    gather_rows(geo, own, qkv, pair * LANES, put_query)
    gather_rows(geo, own, qkv, geo.cols + pair * LANES, put_key)
    gather_rows(geo, own, qkv, 2 * geo.cols + pair * LANES, put_value)
    for tile in range(geo.tiles):
        vt[:, tile * TILE : (tile + 1) * TILE] = vn[tile * TILE : (tile + 1) * TILE, :].T

    def query_tile(tile, _):
        at = pl.multiple_of(tile * TILE, TILE)
        q0 = qa[0, pl.ds(at, TILE), :]
        q1 = qa[1, pl.ds(at, TILE), :]

        def one(q, which, step, m, l, acc):
            k = ka[which, pl.ds(step, TILE), :]
            s = dot_nt(k, q)
            m_new = jnp.maximum(m, jnp.max(s, 0, keepdims=True))
            p = jnp.exp(s - m_new)
            alpha = jnp.exp(m - m_new)
            l = l * alpha + jnp.sum(p, 0, keepdims=True)
            v = vt[which * HEAD : (which + 1) * HEAD, pl.ds(step, TILE)]
            acc = acc * alpha + dot_nn(v, p.astype(BF16))
            return m_new, l, acc

        def key_tile(index, carry):
            m0, l0, a0, m1, l1, a1 = carry
            step = pl.multiple_of(index * TILE, TILE)
            m0, l0, a0 = one(q0, 0, step, m0, l0, a0)
            m1, l1, a1 = one(q1, 1, step, m1, l1, a1)
            return m0, l0, a0, m1, l1, a1

        low = jnp.full((1, TILE), -2e30, F32)
        none = jnp.zeros((1, TILE), F32)
        blank = jnp.zeros((HEAD, TILE), F32)
        m0, l0, a0, m1, l1, a1 = lax.fori_loop(
            table[1 + tile],
            table[1 + geo.tiles + tile],
            key_tile,
            (low, none, blank, low, none, blank),
        )
        out = jnp.concatenate([a0 / l0, a1 / l1], 0)
        ob[pl.ds(at, TILE), :] = out.T.astype(BF16)
        lse[0, 0:1, pl.ds(at, TILE)] = m0 + jnp.log(l0)
        lse[0, 1:2, pl.ds(at, TILE)] = m1 + jnp.log(l1)
        return 0

    lax.fori_loop(0, geo.tiles, query_tile, 0)
    scatter_rows(geo, own, mixed, pair * LANES, ob)


def attend_back_kernel(geo, table, *refs):
    peers = geo.peers
    qkv = refs[:peers]
    grads = refs[peers : 2 * peers]
    mixed = refs[2 * peers : 3 * peers]
    lse, key_marks, query_marks, value_marks = refs[3 * peers : 3 * peers + 4]
    outs = refs[3 * peers + 4 : 4 * peers + 4]
    ka, qa, va, da, qm, dm, kn, kt, dk, dv, ob = refs[4 * peers + 4 :]
    pair = pl.program_id(0)
    own = table[0]
    lane = lax.broadcasted_iota(jnp.int32, (geo.chunk, LANES), 1)
    first = lane < HEAD
    zero = jnp.zeros((geo.chunk, LANES), BF16)

    def put_query(offset, values):
        marks = query_marks[pl.ds(offset, geo.chunk), :]
        scaled = values * 0.125
        qa[0, pl.ds(offset, geo.chunk), :] = jnp.where(first, scaled, marks)
        qa[1, pl.ds(offset, geo.chunk), :] = jnp.where(first, marks, scaled)
        qm[0, pl.ds(offset, geo.chunk), :] = jnp.where(first, scaled, zero)
        qm[1, pl.ds(offset, geo.chunk), :] = jnp.where(first, zero, scaled)

    def put_key(offset, values):
        marks = key_marks[pl.ds(offset, geo.chunk), :]
        ka[0, pl.ds(offset, geo.chunk), :] = jnp.where(first, values, marks)
        ka[1, pl.ds(offset, geo.chunk), :] = jnp.where(first, marks, values)
        kn[pl.ds(offset, geo.chunk), :] = values

    def put_value(offset, values):
        marks = value_marks[pl.ds(offset, geo.chunk), :]
        va[0, pl.ds(offset, geo.chunk), :] = jnp.where(first, values, marks)
        va[1, pl.ds(offset, geo.chunk), :] = jnp.where(first, marks, values)

    def put_mixed(offset, values):
        ob[pl.ds(offset, geo.chunk), :] = values

    def put_grad(offset, values):
        product = values.astype(F32) * ob[pl.ds(offset, geo.chunk), :].astype(F32)
        inner0 = jnp.sum(jnp.where(first, product, 0.0), 1, keepdims=True)
        inner1 = jnp.sum(jnp.where(first, 0.0, product), 1, keepdims=True)

        def digits(inner, base):
            high = (-inner).astype(BF16)
            rest = -inner - high.astype(F32)
            middle = rest.astype(BF16)
            last = (rest - middle.astype(F32)).astype(BF16)
            spread = jnp.where(
                lane == base,
                high.astype(F32),
                jnp.where(
                    lane == base + 1,
                    middle.astype(F32),
                    jnp.where(lane == base + 2, last.astype(F32), 0.0),
                ),
            )
            return spread.astype(BF16)

        da[0, pl.ds(offset, geo.chunk), :] = jnp.where(first, values, digits(inner0, HEAD))
        da[1, pl.ds(offset, geo.chunk), :] = jnp.where(first, digits(inner1, 0), values)
        dm[0, pl.ds(offset, geo.chunk), :] = jnp.where(first, values, zero)
        dm[1, pl.ds(offset, geo.chunk), :] = jnp.where(first, zero, values)

    gather_rows(geo, own, qkv, pair * LANES, put_query)
    gather_rows(geo, own, qkv, geo.cols + pair * LANES, put_key)
    gather_rows(geo, own, qkv, 2 * geo.cols + pair * LANES, put_value)
    gather_rows(geo, own, mixed, pair * LANES, put_mixed)
    gather_rows(geo, own, grads, pair * LANES, put_grad)
    for tile in range(geo.tiles):
        kt[:, tile * TILE : (tile + 1) * TILE] = kn[tile * TILE : (tile + 1) * TILE, :].T
    dk[...] = jnp.zeros_like(dk)
    dv[...] = jnp.zeros_like(dv)

    def query_tile(tile, _):
        at = pl.multiple_of(tile * TILE, TILE)

        def one(which, step):
            s = dot_nt(ka[which, pl.ds(step, TILE), :], qa[which, pl.ds(at, TILE), :])
            p = jnp.exp(s - lse[0, which : which + 1, pl.ds(at, TILE)])
            g = dot_nt(va[which, pl.ds(step, TILE), :], da[which, pl.ds(at, TILE), :])
            ds = (p * g).astype(BF16)
            return p.astype(BF16), ds

        def key_tile(index, carry):
            a0, a1 = carry
            step = pl.multiple_of(index * TILE, TILE)
            p0, s0 = one(0, step)
            p1, s1 = one(1, step)
            dv[pl.ds(step, TILE), :] += dot_nn(p0, dm[0, pl.ds(at, TILE), :]) + dot_nn(
                p1, dm[1, pl.ds(at, TILE), :]
            )
            dk[pl.ds(step, TILE), :] += dot_nn(s0, qm[0, pl.ds(at, TILE), :]) + dot_nn(
                s1, qm[1, pl.ds(at, TILE), :]
            )
            a0 = a0 + dot_nn(kt[:HEAD, pl.ds(step, TILE)], s0)
            a1 = a1 + dot_nn(kt[HEAD:, pl.ds(step, TILE)], s1)
            return a0, a1

        blank = jnp.zeros((HEAD, TILE), F32)
        a0, a1 = lax.fori_loop(
            table[1 + tile], table[1 + geo.tiles + tile], key_tile, (blank, blank)
        )
        ob[pl.ds(at, TILE), :] = (jnp.concatenate([a0, a1], 0) * 0.125).T.astype(BF16)
        return 0

    lax.fori_loop(0, geo.tiles, query_tile, 0)
    scatter_rows(geo, own, outs, pair * LANES, ob)
    ob[...] = dk[...].astype(BF16)
    scatter_rows(geo, own, outs, geo.cols + pair * LANES, ob)
    ob[...] = dv[...].astype(BF16)
    scatter_rows(geo, own, outs, 2 * geo.cols + pair * LANES, ob)


def whole_spec(shape):
    return pl.BlockSpec(shape, lambda pair, table: (0,) * len(shape))


def attend(geo, table, qkv_parts, key_marks, query_marks):
    out_shape = [
        jax.ShapeDtypeStruct((geo.wide, geo.chunk, geo.cols), BF16) for _ in range(geo.peers)
    ] + [jax.ShapeDtypeStruct((geo.pairs, 8, geo.slots), F32)]
    return pl.pallas_call(
        functools.partial(attend_kernel, geo),
        name="attend",
        out_shape=out_shape,
        grid_spec=pltpu.PrefetchScalarGridSpec(
            num_scalar_prefetch=1,
            grid=(geo.pairs,),
            in_specs=[whole_spec(a.shape) for a in qkv_parts]
            + [whole_spec((geo.slots, LANES))] * 2,
            out_specs=[whole_spec((geo.wide, geo.chunk, geo.cols))] * geo.peers
            + [pl.BlockSpec((1, 8, geo.slots), lambda pair, table: (pair, 0, 0))],
            scratch_shapes=[
                pltpu.VMEM((2, geo.slots, LANES), BF16),
                pltpu.VMEM((2, geo.slots, LANES), BF16),
                pltpu.VMEM((geo.slots, LANES), BF16),
                pltpu.VMEM((LANES, geo.slots), BF16),
                pltpu.VMEM((geo.slots, LANES), BF16),
            ],
        ),
        cost_estimate=pl.CostEstimate(
            flops=4 * geo.slots * geo.slots * geo.real_cols,
            transcendentals=geo.slots * geo.slots * 6,
            bytes_accessed=4 * geo.slots * geo.cols * 2,
        ),
    )(table, *qkv_parts, key_marks, query_marks)


def attend_back(geo, table, qkv_parts, grad_parts, mixed_parts, lse, key_marks, query_marks, value_marks):
    wide_shape = (geo.wide, geo.chunk, 3 * geo.cols)
    two = pltpu.VMEM((2, geo.slots, LANES), BF16)
    return pl.pallas_call(
        functools.partial(attend_back_kernel, geo),
        name="attend_back",
        out_shape=[jax.ShapeDtypeStruct(wide_shape, BF16) for _ in range(geo.peers)],
        grid_spec=pltpu.PrefetchScalarGridSpec(
            num_scalar_prefetch=1,
            grid=(geo.pairs,),
            in_specs=[whole_spec(a.shape) for a in (*qkv_parts, *grad_parts, *mixed_parts)]
            + [pl.BlockSpec((1, 8, geo.slots), lambda pair, table: (pair, 0, 0))]
            + [whole_spec((geo.slots, LANES))] * 3,
            out_specs=[whole_spec(wide_shape)] * geo.peers,
            scratch_shapes=[two] * 6
            + [
                pltpu.VMEM((geo.slots, LANES), BF16),
                pltpu.VMEM((LANES, geo.slots), BF16),
                pltpu.VMEM((geo.slots, LANES), F32),
                pltpu.VMEM((geo.slots, LANES), F32),
                pltpu.VMEM((geo.slots, LANES), BF16),
            ],
        ),
        cost_estimate=pl.CostEstimate(
            flops=10 * geo.slots * geo.slots * geo.real_cols,
            transcendentals=geo.slots * geo.slots * 6,
            bytes_accessed=12 * geo.slots * geo.cols * 2,
        ),
    )(table, *qkv_parts, *grad_parts, *mixed_parts, lse, key_marks, query_marks, value_marks)


def marks_of(block_ids, geo):
    lane = lax.broadcasted_iota(jnp.int32, (geo.slots, LANES), 1) % HEAD
    number = block_ids[:, None] + 1
    key_marks = (lane == number).astype(BF16)
    query_marks = jnp.where((lane < 9) & (lane != number), FAR, 0.0).astype(BF16)
    value_marks = (lane < 3).astype(BF16)
    return key_marks, query_marks, value_marks


def tile_table(block_ids, own, geo):
    ids = block_ids.reshape(geo.tiles, TILE, 1)
    present = jnp.any(ids == jnp.arange(-1, 8, dtype=jnp.int32), 1)
    shared = jnp.any(present[:, None] & present[None], -1)
    places = jnp.arange(geo.tiles, dtype=jnp.int32)
    low = jnp.min(jnp.where(shared, places, geo.tiles), 1)
    high = jnp.max(jnp.where(shared, places + 1, 0), 1)
    return jnp.concatenate([own[None], low, high]).astype(jnp.int32)


def pick(parts, own, target):
    peers = len(parts)
    result = parts[0]
    for step in range(1, peers):
        result = jnp.where((target - own + peers) % peers == step, parts[step], result)
    return result


def ahead(wide, peers, step):
    return [(w, w // peers * peers + (w % peers + step) % peers) for w in range(wide)]


def per_device(
    tokens,
    segment_ids,
    cotangent,
    w_qkv,
    b_qv,
    w_out,
    b_out,
    ls_attn,
    ln1_gain,
    ln1_bias,
    ln2_gain,
    ln2_bias,
    w_fc1,
    b_fc1,
    w_fc2,
    b_fc2,
    ls_mlp,
):
    geo = Geometry(lax.axis_size("wide"), tokens.shape[3])
    wide, peers, chunk, rows, cols = geo.wide, geo.peers, geo.chunk, geo.rows, geo.cols
    own = lax.axis_index("wide") % peers

    def regroup(array):
        return lax.all_to_all(array, "wide", split_axis=0, concat_axis=0, tiled=True)

    ids_out = jnp.broadcast_to(segment_ids.reshape(GROUPS, 1, geo.piece), (GROUPS, peers, geo.piece))
    block_ids = regroup(ids_out.reshape(wide, geo.piece)).reshape(geo.slots)
    token_rows = regroup(tokens.reshape(wide, chunk, D)).reshape(rows, D)
    cotangent, token_rows = lax.optimization_barrier((cotangent, token_rows))
    cotangent_rows = regroup(cotangent.reshape(wide, chunk, D)).reshape(rows, D)

    my_ids = lax.dynamic_index_in_dim(
        block_ids.reshape(wide, peers, chunk), own, 1, keepdims=False
    ).reshape(rows, 1)
    valid_rows = (my_ids >= 0).astype(F32)
    key_marks, query_marks, value_marks = marks_of(block_ids, geo)
    table = tile_table(block_ids, own, geo)

    bias_all = jnp.concatenate([b_qv[:D], jnp.zeros((D,), F32), b_qv[D:]])
    w_heads = w_qkv.reshape(D, 3, peers, geo.real_cols)
    b_heads = bias_all.reshape(3, peers, geo.real_cols)
    o_heads = w_out.reshape(peers, geo.real_cols, D)
    spare = cols - geo.real_cols

    def heads_of(step):
        group = (own + step) % peers
        w = lax.dynamic_index_in_dim(w_heads, group, 2, keepdims=False)
        b = lax.dynamic_index_in_dim(b_heads, group, 1, keepdims=False)
        o = lax.dynamic_index_in_dim(o_heads, group, 0, keepdims=False)
        w = jnp.pad(w, ((0, 0), (0, 0), (0, spare))).reshape(D, 3 * cols)
        b = jnp.pad(b, ((0, 0), (0, spare))).reshape(3 * cols)
        return w, b, jnp.pad(o, ((0, spare), (0, 0)))

    weights = [heads_of(step) for step in range(peers)]

    def send(array, step):
        return lax.ppermute(array, "wide", ahead(wide, peers, step % peers))

    inputs = token_rows.astype(F32)
    normed, norm_first_back = jax.vjp(layer_norm, inputs, ln1_gain, ln1_bias)
    normed_low = normed.astype(BF16)
    qkv_parts = [None] * peers
    for step in [*range(1, peers), 0]:
        w, b, _ = weights[step]
        made = (dot_nn(normed_low, w) + b).astype(BF16).reshape(wide, chunk, 3 * cols)
        qkv_parts[step] = send(made, step) if step else made
    *mixed_parts, lse = attend(geo, table, qkv_parts, key_marks, query_marks)
    mixed_home = [
        (send(part, -step) if step else part).reshape(rows, cols)
        for step, part in enumerate(mixed_parts)
    ]
    mixed_rows = jnp.concatenate(mixed_home, 1)
    w_out_rel = jnp.concatenate([o for _, _, o in weights], 0)
    projected = dot_nn(mixed_rows, w_out_rel) + b_out
    hidden = inputs + ls_attn * projected
    second, norm_second_back = jax.vjp(layer_norm, hidden, ln2_gain, ln2_bias)
    second_low = second.astype(BF16)
    pre_act = dot_nn(second_low, w_fc1) + b_fc1
    activation, gelu_back = jax.vjp(gelu_exact, pre_act)
    act_low = activation.astype(BF16)
    mlp_out = dot_nn(act_low, w_fc2) + b_fc2
    result = ((hidden + ls_mlp * mlp_out) * valid_rows).astype(BF16)
    output = regroup(result.reshape(wide, chunk, D)).reshape(tokens.shape)
    grad_out = cotangent_rows.astype(F32) * valid_rows
    grad_ls_mlp = jnp.sum(grad_out * mlp_out, 0)
    grad_mlp = (ls_mlp * grad_out).astype(BF16)
    grad_b_fc2 = jnp.sum(grad_mlp.astype(F32), 0)
    grad_w_fc2 = jnp.einsum("tf,td->fd", act_low, grad_mlp, preferred_element_type=F32)
    grad_act = jnp.dot(grad_mlp, w_fc2.T, preferred_element_type=F32)
    grad_pre = gelu_back(grad_act)[0].astype(BF16)
    grad_b_fc1 = jnp.sum(grad_pre.astype(F32), 0)
    grad_w_fc1 = jnp.einsum("td,tf->df", second_low, grad_pre, preferred_element_type=F32)
    grad_second = jnp.dot(grad_pre, w_fc1.T, preferred_element_type=F32)
    grad_hidden_norm, grad_ln2_gain, grad_ln2_bias = norm_second_back(grad_second)
    grad_hidden = grad_out + grad_hidden_norm
    grad_ls_attn = jnp.sum(grad_hidden * projected, 0)
    grad_proj = (ls_attn * grad_hidden).astype(BF16)
    grad_b_out = jnp.sum(grad_proj.astype(F32), 0)
    grad_parts = [None] * peers
    for step in [*range(1, peers), 0]:
        made = jnp.dot(grad_proj, weights[step][2].T, preferred_element_type=F32)
        made = made.astype(BF16).reshape(wide, chunk, cols)
        grad_parts[step] = send(made, step) if step else made
    grad_w_out_rel = jnp.einsum("td,te->de", mixed_rows, grad_proj, preferred_element_type=F32)
    grad_w_out_parts = [
        grad_w_out_rel[step * cols : step * cols + geo.real_cols].astype(BF16)
        for step in range(peers)
    ]
    grad_w_out = jnp.concatenate([pick(grad_w_out_parts, own, g) for g in range(peers)], 0)

    dqkv_parts = attend_back(
        geo, table, qkv_parts, grad_parts, mixed_parts, lse, key_marks, query_marks, value_marks
    )
    dqkv_home = [
        (send(part, -step) if step else part).reshape(rows, 3 * cols)
        for step, part in enumerate(dqkv_parts)
    ]
    grad_qkv = jnp.concatenate(dqkv_home, 1)
    w_qkv_rel = jnp.concatenate([w for w, _, _ in weights], 1)
    grad_normed = jnp.dot(grad_qkv, w_qkv_rel.T, preferred_element_type=F32)
    sums_rel = jnp.sum(grad_qkv.astype(F32), 0).reshape(peers, 3, cols)[:, :, : geo.real_cols]
    sums = jnp.stack([pick(list(sums_rel), own, g) for g in range(peers)], 1).reshape(3, D)
    grad_b_qv = jnp.concatenate([sums[0], sums[2]])
    grad_w_rel = jnp.einsum("td,te->de", normed_low, grad_qkv, preferred_element_type=F32)
    grad_w_rel = grad_w_rel.astype(BF16).reshape(D, peers, 3, cols)[..., : geo.real_cols]
    grad_w_qkv = jnp.stack(
        [pick([grad_w_rel[:, k] for k in range(peers)], own, g) for g in range(peers)], 2
    ).reshape(D, 3 * D)
    grad_inputs_norm, grad_ln1_gain, grad_ln1_bias = norm_first_back(grad_normed)
    grad_tokens = regroup(
        (grad_hidden + grad_inputs_norm).astype(BF16).reshape(wide, chunk, D)
    ).reshape(tokens.shape)

    def reduced(array):
        share = lax.psum_scatter(array.astype(BF16), "narrow", scatter_dimension=0, tiled=True)
        return lax.psum(share, "wide").astype(F32)

    narrow = lax.axis_size("narrow")
    vectors = [
        grad_b_qv,
        grad_b_out,
        grad_ls_attn,
        grad_ln1_gain,
        grad_ln1_bias,
        grad_ln2_gain,
        grad_ln2_bias,
        grad_b_fc1,
        grad_b_fc2,
        grad_ls_mlp,
    ]
    packed = jnp.concatenate([v.reshape(narrow, -1) for v in vectors], 1)
    packed = lax.psum_scatter(packed, "narrow", scatter_dimension=0, tiled=False)
    packed = lax.psum(packed, "wide")
    small, start = [], 0
    for v in vectors:
        size = v.shape[0] // narrow
        small.append(packed[start : start + size])
        start += size
    return (
        output,
        grad_tokens,
        reduced(grad_w_qkv),
        small[0],
        reduced(grad_w_out),
        small[1],
        small[2],
        small[3],
        small[4],
        small[5],
        small[6],
        reduced(grad_w_fc1),
        small[7],
        reduced(grad_w_fc2),
        small[8],
        small[9],
    )


def solution(mesh):
    rows = P("narrow", "wide", None, None, None)
    placed = (rows, P("narrow", "wide", None, None), rows) + (P(),) * 14
    matrix, vector = P("narrow", None), P("narrow")
    return jax.shard_map(
        per_device,
        mesh=mesh,
        in_specs=placed,
        out_specs=(
            rows,
            rows,
            matrix,
            vector,
            matrix,
            vector,
            vector,
            vector,
            vector,
            vector,
            vector,
            matrix,
            vector,
            matrix,
            vector,
            vector,
        ),
        check_vma=False,
    )
```

time: 1510 us -> 663 us (0.44)
  matrix products: 465 us -> 98.3 us
  other arithmetic: 369 us -> 22.8 us
  local copies, waits for them, and re-layouts: 277 us -> 43.2 us
  Pallas kernels: 0 us -> 183 us
  waiting for transfers between devices: 313 us -> 186 us
  blocking collectives: 31.2 us -> 85.6 us
    dot_general x40 -> x14, matrix products: 465 us -> 98.3 us  [the longest x5 36.7 us: dot_nn(): return jnp.dot(a, b, preferred_element_type=F32)]
    all_to_all x5 -> x4, waiting for transfers between devices: 269 us -> 27.1 us  [regroup(): lax.all_to_all(array, 'wide', split_axis=0, concat_axis=0, tiled=True)]
    pallas_call x0 -> x2, Pallas kernels: none -> 183 us  [the longest x1 100 us: attend(): pl.pallas_call(functools.partial(attend_kernel, geo), name='attend', out_...]
    all_to_all x8 -> x0, other arithmetic: 140 us -> none  [the longest x2 60.2 us: per_device(): lax.all_to_all(outgoing, 'wide', split_axis=0, concat_axis=0, tiled=True)]
    convert_element_type x23 -> x7, other arithmetic: 144 us -> 8.25 us  [the longest x3 5.37 us: reduced(): return lax.psum(share, 'wide').astype(F32)]
    reduce_scatter x4 -> x3, waiting for transfers between devices: 22.6 us -> 111 us  [reduced(): lax.psum_scatter(array.astype(BF16), 'narrow', scatter_dimension=0, tiled...]
    reshape x8 -> x9, local copies, waits for them, and re-layouts: 68.4 us -> 0.63 us  [per_device(): packed = jnp.concatenate([v.reshape(narrow, -1) for v in vectors], 1)]
    unnamed x126 -> x70, local copies, waits for them, and re-layouts: 87.9 us -> 24.9 us
  transfers between devices with their start and end apart: 10 -> 13, of which waited for: 6 -> 6; matrix products, arithmetic and copies ran while one was open for 49% -> 13% of each run, Pallas kernels for 0% -> 15%
where the time goes in v1:
time: 663 us; the launch traced here: 655 us
  waiting for transfers between devices  186 us (28%)
  Pallas kernels  183 us (28%)
  matrix products  98.3 us (15%)
  blocking collectives  85.6 us (13%)
  local copies, waits for them, and re-layouts  43.2 us (7%)
  other arithmetic  22.8 us (3%)
  starting transfers between devices  20.3 us (3%)
  between operations  14.5 us (2%)
    reduce_scatter x3, waiting for transfers between devices, reduced(): lax.psum_scatter(array.astype(BF16), 'narrow', scatter_dimension=0, tiled...  111 us
    pallas_call x1, Pallas kernels, attend(): pl.pallas_call(functools.partial(attend_kernel, geo), name='attend', out_...  100 us
    pallas_call x1, Pallas kernels, attend_back(): pl.pallas_call(functools.partial(attend_back_kernel, geo), name='attend_b...  83.1 us
    psum x1, waiting for transfers between devices, reduced(): return lax.psum(share, 'wide').astype(F32)  43.1 us
    all_to_all x1, blocking collectives, regroup(): lax.all_to_all(array, 'wide', split_axis=0, concat_axis=0, tiled=True)  42.3 us
    dot_general x5, matrix products, dot_nn(): return jnp.dot(a, b, preferred_element_type=F32)  36.7 us
    psum x1, blocking collectives, per_device(): packed = lax.psum(packed, 'wide')  27.5 us
    all_to_all x4, waiting for transfers between devices, regroup(): lax.all_to_all(array, 'wide', split_axis=0, concat_axis=0, tiled=True)  27.1 us
  transfers between devices with their start and end apart: 13, of which 6 were waited for; matrix products, arithmetic and copies ran while one was open for 13% of the time, Pallas kernels for 15%

profile of v1, /device:TPU:0, one launch (start us, length us, event | category | flops | bytes accessed | tf_op | source)
XLA Modules:
  0.0 654.6 jit_solution(13684346101681198459)
XLA Ops:
  7.2 6.4 all-to-all-start
  14.2 5.8 copy.48
  24.3 27.1 %all-to-all-done = bf16[8,128,768]{2,1,0:T(8,128)(2,1)S(1)} async-done(((bf16[8,128,768]{2,1,0:T(8,128)(2,1)}), bf16[8,128,768]{2,1,0:T(8,128)(2,1)S(1)}, u32[]{:S(2)}, u32[]{:S(2)}) %all-to-all-start) | async-done | bytes 1572896 | tf_op jit(solution)/shard_map/all_to_all | solution.py:380
  61.2 4.8 all-to-all-start.3
  69.2 5.4 add_convert_fusion.2
  74.7 100.4 %attend.1 = (bf16[8,128,384]{2,1,0:T(8,128)(2,1)}, bf16[8,128,384]{2,1,0:T(8,128)(2,1)}, f32[3,8,2048]{2,1,0:T(8,128)}) custom-call(s32[17]{0:T(128)} %pad_add_fusion.table, bf16[8,128,1152]{2,1,0:T(8,128)(2,1)} %bitcast.116, bf16[8,128,1152]{2,1,0:T(8,128)(2,1)} %collective-permute-done.refs_1_, bf16[2048,128]{1,0:T(8,128)(2,1)} %get-tuple-element.126.refs_2_.refs_7_, ...), custom_call_target="tpu_custom_call" | custom-call | flops 6442450944 | bytes 6291456 | tf_op jit(solution)/shard_map/attend/pallas_call | solution.py:267
  179.7 4.9 fusion.36
  185.4 11.8 %multiply_convert_fusion = (bf16[1024,3072]{1,0:T(8,128)(2,1)}, f32[1024,3072]{1,0:T(8,128)}) fusion(f32[3072]{0:T(1024)S(1)} %copy-done.18, bf16[768,3072]{1,0:T(8,128)(2,1)S(1)} %bitcast.112, f32[1024,768]{1,0:T(8,128)S(1)} %get-tuple-element.100, f32[768]{0:T(1024)S(1)} %copy-done.20, f32[768]{0:T(1024)S(1)} %copy-done.14, f32[1024]{0:T(1024)S(1)} %fusion.23, ...), kind=kOutput, calls=%fused_computation.2 | convolution fusion | flops 4854644736 | bytes 26765312 | tf_op jit(solution)/shard_map/dot_general | solution.py:38
  197.2 13.8 %convert_reduce_fusion = (f32[3072]{0:T(1024)S(1)}, bf16[1024,3072]{1,0:T(8,128)(2,1)S(1)}) fusion(bf16[1024,768]{1,0:T(8,128)(2,1)S(1)} %multiply_convert_fusion.3, bf16[3072,768]{1,0:T(8,128)(2,1)S(1)} %bitcast.114, f32[1024,3072]{1,0:T(8,128)} %get-tuple-element.129, f32[3072]{0:T(1024)S(1)} %copy-done.18), kind=kOutput, calls=%fused_computation | convolution fusion | flops 4882166784 | bytes 25190400 | tf_op jit(solution)/shard_map/dot_general | solution.py:445
  211.1 5.7 multiply_reduce_fusion.1
  224.7 83.1 %attend_back.1 = (bf16[8,128,1152]{2,1,0:T(8,128)(2,1)}, bf16[8,128,1152]{2,1,0:T(8,128)(2,1)}) custom-call(s32[17]{0:T(128)} %pad_add_fusion.table, bf16[8,128,1152]{2,1,0:T(8,128)(2,1)} %bitcast.117, bf16[8,128,1152]{2,1,0:T(8,128)(2,1)} %collective-permute-done.refs_1_, bf16[8,128,384]{2,1,0:T(8,128)(2,1)} %bitcast.120, bf16[8,128,384]{2,1,0:T(8,128)(2,1)} %copy-done.17, ...), custom_call_target="tpu_custom_call" | custom-call | flops 16106127360 | bytes 18874368 | tf_op jit(solution)/shard_map/attend_back/pallas_call | solution.py:297
  312.7 8.4 %convolution_convert_fusion.2 = bf16[768,2304]{1,0:T(8,128)(2,1)} fusion(bf16[1024,1152]{1,0:T(8,128)(2,1)} %bitcast.24, bf16[1024,1152]{1,0:T(8,128)(2,1)} %bitcast.90, bf16[1024,768]{1,0:T(8,128)(2,1)S(1)} %bitcast.82, f32[768]{0:T(1024)S(1)} %copy-done.19, f32[768]{0:T(1024)S(1)} %copy-done.15, f32[1024]{0:T(1024)S(1)} %fusion.22, ...), kind=kOutput, calls=%fused_computation.7 | convolution fusion | flops 3639803904 | bytes 9844736 | tf_op jit(solution)/shard_map/td,te->de/dot_general | solution.py:480
  321.0 5.8 copy.49
  331.4 5.8 copy.52
  341.9 10.5 %convolution_convert_fusion.1 = bf16[768,3072]{1,0:T(8,128)(2,1)} fusion(bf16[1024,3072]{1,0:T(8,128)(2,1)} %copy-done.26, f32[1024,768]{1,0:T(8,128)} %copy-done, f32[768]{0:T(1024)S(1)} %copy-done.20, f32[768]{0:T(1024)S(1)} %copy-done.14, f32[1024]{0:T(1024)S(1)} %fusion.23, f32[1024]{0:T(1024)S(1)} %broadcast_multiply_fusion), kind=kOutput, calls=%fused_computation.6 | convolution fusion | flops 4838129664 | bytes 14170112 | tf_op jit(solution)/shard_map/td,tf->df/dot_general | solution.py:448
  352.6 9.1 %convolution_convert_fusion = bf16[3072,768]{1,0:T(8,128)(2,1)} fusion(bf16[1024,3072]{1,0:T(8,128)(2,1)} %get-tuple-element.128, bf16[1024,768]{1,0:T(8,128)(2,1)} %copy-done.5), kind=kOutput, calls=%fused_computation.5 | convolution fusion | flops 4834197504 | bytes 12582912 | tf_op jit(solution)/shard_map/tf,td->fd/dot_general | solution.py:444
  361.8 7.9 %fusion.34 = (f32[768]{0:T(1024)S(1)}, f32[1024]{0:T(1024)S(1)}, f32[1024,768]{1,0:T(8,128)S(1)}) fusion(f32[768]{0:T(1024)S(1)} %copy-done.15, f32[1024]{0:T(1024)S(1)} %broadcast_multiply_fusion.1, bf16[1024,768]{1,0:T(8,128)(2,1)S(1)} %bitcast.83, bf16[768,1152]{0,1:T(8,128)(2,1)} %bitcast.93, bf16[768,1152]{0,1:T(8,128)(2,1)} %bitcast.96, ...), kind=kOutput, calls=%fused_computation.111 | convolution fusion | flops 3645110528 | bytes 12990464 | tf_op jit(solution)/shard_map/dot_general | solution.py:476
  371.6 10.6 %multiply_reduce_fusion = (f32[768]{0:T(1024)S(1)}, f32[768]{0:T(1024)S(1)}, bf16[1024,768]{1,0:T(8,128)(2,1)}, bf16[1024,768]{1,0:T(8,128)(2,1)S(1)}) fusion(bf16[8,128,768]{2,1,0:T(8,128)(2,1)S(1)} %all-to-all-done.3, f32[1024]{0:T(1024)S(1)} %bitcast.107, f32[768]{0:T(1024)S(1)} %copy-done.21, f32[1024,768]{1,0:T(8,128)S(1)} %copy-done.25, ...), kind=kOutput, calls=%fused_computation.33 | convolution fusion | flops 4850710528 | bytes 29927424 | tf_op jit(solution)/shard_map/dot_general | solution.py:38
  382.2 42.3 %all_to_all.29 = bf16[8,128,768]{2,1,0:T(8,128)(2,1)S(1)} all-to-all(bf16[8,128,768]{2,1,0:T(8,128)(2,1)S(1)} %bitcast.100), channel_id=1, replica_groups=mesh['wide'=8,'narrow'=4] {'wide'}, dimensions={0} | all-to-all | bytes 3145728 | tf_op jit(solution)/shard_map/all_to_all | solution.py:380
  431.2 51.1 %reduce-scatter.9.cloned.1.call-done = bf16[192,3072]{1,0:T(8,128)(2,1)} async-done(((bf16[768,3072]{1,0:T(8,128)(2,1)}), bf16[192,3072]{1,0:T(8,128)(2,1)}) %reduce-scatter.9.cloned.1.call-update) | async-done | bytes 1179664 | tf_op jit(solution)/shard_map/reduce_scatter | solution.py:491
  482.4 59.8 %reduce-scatter.11.cloned.1.call-done = bf16[768,768]{1,0:T(8,128)(2,1)} async-done(((bf16[3072,768]{1,0:T(8,128)(2,1)}), bf16[768,768]{1,0:T(8,128)(2,1)}) %reduce-scatter.11.cloned.1.call-update) | async-done | bytes 1179664 | tf_op jit(solution)/shard_map/reduce_scatter | solution.py:491
  547.2 15.7 %all-reduce = f32[4,2688]{1,0:T(4,128)S(1)} all-reduce(f32[4,2688]{1,0:T(4,128)S(1)} %concatenate.42), channel_id=3, replica_groups=mesh['wide'=8,'narrow'=4] {'narrow'}, use_global_device_ids=true, to_apply=%region_24.25.clone | all-reduce | flops 10752 | bytes 86016
  563.7 27.5 %psum.36 = f32[2688]{0:T(1024)S(1)} all-reduce(f32[2688]{0:T(1024)S(1)} %dynamic-slice_reduce_fusion), channel_id=1, replica_groups=mesh['wide'=8,'narrow'=4] {'wide'}, use_global_device_ids=true, to_apply=%region_25.26 | all-reduce | flops 2688 | bytes 21504 | tf_op jit(solution)/shard_map/psum | solution.py:509
  593.0 43.1 %all-reduce.4.cloned.1.call-done = (bf16[192,2304]{0,1:T(8,128)(2,1)}, bf16[192,768]{1,0:T(8,128)(2,1)}, bf16[192,3072]{1,0:T(8,128)(2,1)}, bf16[768,768]{1,0:T(8,128)(2,1)}) async-done(((bf16[192,2304]{0,1:T(8,128)(2,1)}, bf16[192,768]{1,0:T(8,128)(2,1)}, bf16[192,3072]{1,0:T(8,128)(2,1)}, bf16[768,768]{1,0:T(8,128)(2,1)}), (bf16[192,2304]{0,1:T(8,128)(2,1)}, bf16[192,768]{1,0:T(8,128)(2,1)}, ...) | async-done | bytes 3538960 | tf_op jit(solution)/shard_map/psum | solution.py:492
  (168 shorter events, 73.3 us)
Async XLA Ops:
  7.2 44.2 %all-to-all-start = ((bf16[8,128,768]{2,1,0:T(8,128)(2,1)}), bf16[8,128,768]{2,1,0:T(8,128)(2,1)S(1)}, u32[]{:S(2)}, u32[]{:S(2)}) async-start(bf16[8,128,768]{2,1,0:T(8,128)(2,1)} %bitcast.97), calls=%async_computation | async-start | bytes 3145728 | tf_op jit(solution)/shard_map/all_to_all | solution.py:380
  24.3 31.4 %copy-start.15 = (f32[768]{0:T(1024)S(1)}, f32[768]{0:T(1024)}, u32[]{:S(2)}) copy-start(f32[768]{0:T(1024)} %param.25) | copy-start | bytes 9220
  24.3 31.4 %copy-start.19 = (f32[768]{0:T(1024)S(1)}, f32[768]{0:T(1024)}, u32[]{:S(2)}) copy-start(f32[768]{0:T(1024)} %param.26) | copy-start | bytes 9220
  51.4 9.2 %all-to-all-start.1 = ((s32[8,1,256]{2,1,0:T(1,128)}), s32[8,1,256]{2,1,0:T(1,128)S(1)}, u32[]{:S(2)}, u32[]{:S(2)}) async-start(s32[8,1,256]{2,1,0:T(1,128)} %all_to_all.19), calls=%async_computation.1 | async-start | bytes 16384 | tf_op jit(solution)/shard_map/all_to_all | solution.py:380
  60.1 14.5 %collective-permute-start = (bf16[8,128,1152]{2,1,0:T(8,128)(2,1)}, bf16[8,128,1152]{2,1,0:T(8,128)(2,1)}, u32[]{:S(2)}, u32[]{:S(2)}) collective-permute-start(bf16[8,128,1152]{2,1,0:T(8,128)(2,1)} %bitcast.8), channel_id=1, source_target_pairs={{0,4},{4,0},{8,12},{12,8},{16,20},{20,16},{24,28},{28,24},{1,5},{5... | collective-permute-start | bytes 7077896 | tf_op jit(solution)/shard_map/ppermute | solution.py:413
  61.2 116.7 %all-to-all-start.3 = ((bf16[8,128,768]{2,1,0:T(8,128)(2,1)}), bf16[8,128,768]{2,1,0:T(8,128)(2,1)S(1)}, u32[]{:S(2)}, u32[]{:S(2)}) async-start(bf16[8,128,768]{2,1,0:T(8,128)(2,1)} %bitcast.98), calls=%async_computation.3 | async-start | bytes 3145728 | tf_op jit(solution)/shard_map/all_to_all | solution.py:380
  66.0 362.9 %reduce-scatter.13.cloned.1.call-start = ((), (), s32[]{:S(2)}) async-start(), calls=%async_computation.12 | async-start | bytes 4423680
  74.7 103.4 %copy-start.11 = (f32[768]{0:T(1024)S(1)}, f32[768]{0:T(1024)}, u32[]{:S(2)}) copy-start(f32[768]{0:T(1024)} %param.33) | copy-start | bytes 9220
  175.1 3.4 collective-permute-start.1
  178.4 18.8 %copy-start.5 = (bf16[1024,768]{1,0:T(8,128)(2,1)}, bf16[1024,768]{1,0:T(8,128)(2,1)S(1)}, u32[]{:S(2)}) copy-start(bf16[1024,768]{1,0:T(8,128)(2,1)S(1)} %multiply_convert_fusion.3) | copy-start | bytes 4718596
  178.5 6.7 %slice-start = ((s8[4718592]{0:T(1024)(128)(4,1)}), s8[4194304]{0:T(1024)(128)(4,1)S(1)}, s32[]{:S(2)}) async-start(s8[4718592]{0:T(1024)(128)(4,1)} %bitcast.111), calls=%async_computation.14 | async-start | bytes 8388608
  184.6 32.1 %copy-start = (f32[1024,768]{1,0:T(8,128)}, f32[1024,768]{1,0:T(8,128)S(1)}, u32[]{:S(2)}) copy-start(f32[1024,768]{1,0:T(8,128)S(1)} %get-tuple-element.100) | copy-start | bytes 9437188
  184.7 12.6 %slice-start.2 = ((s8[4718592]{0:T(1024)(128)(4,1)}), s8[4194304]{0:T(1024)(128)(4,1)S(1)}, s32[]{:S(2)}) async-start(s8[4718592]{0:T(1024)(128)(4,1)} %bitcast.113), calls=%async_computation.16 | async-start | bytes 8388608
  185.4 11.8 %slice-start.3 = ((s8[4718592]{0:T(1024)(128)(4,1)}), s8[524288]{0:T(1024)(128)(4,1)S(1)}, s32[]{:S(2)}) async-start(s8[4718592]{0:T(1024)(128)(4,1)} %bitcast.113), calls=%async_computation.17 | async-start | bytes 1048576
  221.5 2.4 collective-permute-start.2
  307.8 4.9 collective-permute-start.3
  337.2 94.0 %reduce-scatter.7.cloned.1.call-start = ((), (), s32[]{:S(2)}) async-start(), calls=%async_computation.9 | async-start | bytes 1474560 | tf_op jit(solution)/shard_map/reduce_scatter | solution.py:491
  341.8 140.6 %reduce-scatter.9.cloned.1.call-start = ((), (), s32[]{:S(2)}) async-start(), calls=%async_computation.10 | async-start | bytes 5898240 | tf_op jit(solution)/shard_map/reduce_scatter | solution.py:491
  352.4 189.8 %reduce-scatter.11.cloned.1.call-start = ((), (), s32[]{:S(2)}) async-start(), calls=%async_computation.11 | async-start | bytes 5898240 | tf_op jit(solution)/shard_map/reduce_scatter | solution.py:491
  361.7 9.7 %copy-start.3 = (f32[1024,768]{1,0:T(8,128)S(1)}, f32[1024,768]{1,0:T(8,128)}, u32[]{:S(2)}) copy-start(f32[1024,768]{1,0:T(8,128)} %copy-done.2) | copy-start | bytes 9437188
  361.8 9.7 %copy-start.25 = (f32[1024,768]{1,0:T(8,128)S(1)}, f32[1024,768]{1,0:T(8,128)}, u32[]{:S(2)}) copy-start(f32[1024,768]{1,0:T(8,128)} %get-tuple-element.127) | copy-start | bytes 9437188
  424.5 168.4 %all-to-all-start.4 = ((bf16[8,128,768]{2,1,0:T(8,128)(2,1)}), bf16[8,128,768]{2,1,0:T(8,128)(2,1)}, u32[]{:S(2)}, u32[]{:S(2)}) async-start(bf16[8,128,768]{2,1,0:T(8,128)(2,1)} %bitcast.99), calls=%async_computation.4 | async-start | bytes 3145728 | tf_op jit(solution)/shard_map/all_to_all | solution.py:380
  428.8 113.4 %copy-start.24 = (u32[32]{0:T(128)S(1)}, u32[32]{0:T(128)}, u32[]{:S(2)}) copy-start(u32[32]{0:T(128)} %constant.132) | copy-start | bytes 388
  428.8 207.3 %all-reduce.4.cloned.1.call-start = ((), (), s32[]{:S(2)}) async-start(), calls=%async_computation.13 | async-start | bytes 7667712 | tf_op jit(solution)/shard_map/psum | solution.py:492
  (20 other events, 56.4 us)
Sparse Core Ops, SparseCore 0:
  337.3 52.7 reduce-scatter.12
  393.6 28.6 reduce-scatter.6
  425.4 56.9 reduce-scatter.8
  485.2 56.9 reduce-scatter.10
  545.3 90.7 all-reduce.3

commit v2 on v1

--- a/solution.py
+++ b/solution.py
@@ -10,7 +10,8 @@
 HEADS = 12
 HEAD = 64
 GROUPS = 4
-TILE = 256
+TILE = 512
+KEYS = 512
 LANES = 128
 EPSILON = 1e-06
 ROOT_HALF = 0.7071067811865476
@@ -77,10 +78,15 @@
     key_marks, query_marks = refs[peers : peers + 2]
     mixed = refs[peers + 2 : 2 * peers + 2]
     lse = refs[2 * peers + 2]
-    ka, qa, vn, vt, ob = refs[2 * peers + 3 :]
+    ka, qa, va, ob, worst = refs[2 * peers + 3 :]
     pair = pl.program_id(0)
     own = table[0]
     first = lax.broadcasted_iota(jnp.int32, (geo.chunk, LANES), 1) < HEAD
+    left = lax.broadcasted_iota(jnp.int32, (TILE, LANES), 1) < HEAD
+    one = jnp.ones((geo.chunk, LANES), BF16)
+    picks = lax.broadcasted_iota(jnp.int32, (8, LANES), 1) == HEAD * lax.broadcasted_iota(
+        jnp.int32, (8, LANES), 0
+    )
 
     def put_query(offset, values):
         marks = query_marks[pl.ds(offset, geo.chunk), :]
@@ -94,53 +100,79 @@
         ka[1, pl.ds(offset, geo.chunk), :] = jnp.where(first, marks, values)
 
     def put_value(offset, values):
-        vn[pl.ds(offset, geo.chunk), :] = values
+        va[0, pl.ds(offset, geo.chunk), :] = jnp.where(first, values, one)
+        va[1, pl.ds(offset, geo.chunk), :] = jnp.where(first, one, values)
 
     gather_rows(geo, own, qkv, pair * LANES, put_query)
     gather_rows(geo, own, qkv, geo.cols + pair * LANES, put_key)
     gather_rows(geo, own, qkv, 2 * geo.cols + pair * LANES, put_value)
-    for tile in range(geo.tiles):
-        vt[:, tile * TILE : (tile + 1) * TILE] = vn[tile * TILE : (tile + 1) * TILE, :].T
-
-    def query_tile(tile, _):
+
+    def scores(which, step, at):
+        return dot_nt(qa[which, pl.ds(at, TILE), :], ka[which, pl.ds(step, KEYS), :])
+
+    def weighted(which, step, p):
+        return dot_nn(p.astype(BF16), va[which, pl.ds(step, KEYS), :])
+
+    def store(at, acc0, acc1, m0, m1):
+        totals = pltpu.roll(jnp.where(left, acc1, acc0), HEAD, 1)
+        ob[pl.ds(at, TILE), :] = (jnp.where(left, acc0, acc1) / totals).astype(BF16)
+        logs = jnp.log(totals) + jnp.where(left, m0, m1)
+        lse[0, :, pl.ds(at, TILE)] = lax.dot_general(
+            picks.astype(F32),
+            logs,
+            (((1,), (1,)), ((), ())),
+            precision=lax.Precision.HIGHEST,
+            preferred_element_type=F32,
+        )
+        return totals
+
+    def plain_tile(tile, _):
         at = pl.multiple_of(tile * TILE, TILE)
-        q0 = qa[0, pl.ds(at, TILE), :]
-        q1 = qa[1, pl.ds(at, TILE), :]
-
-        def one(q, which, step, m, l, acc):
-            k = ka[which, pl.ds(step, TILE), :]
-            s = dot_nt(k, q)
-            m_new = jnp.maximum(m, jnp.max(s, 0, keepdims=True))
-            p = jnp.exp(s - m_new)
-            alpha = jnp.exp(m - m_new)
-            l = l * alpha + jnp.sum(p, 0, keepdims=True)
-            v = vt[which * HEAD : (which + 1) * HEAD, pl.ds(step, TILE)]
-            acc = acc * alpha + dot_nn(v, p.astype(BF16))
-            return m_new, l, acc
 
         def key_tile(index, carry):
-            m0, l0, a0, m1, l1, a1 = carry
-            step = pl.multiple_of(index * TILE, TILE)
-            m0, l0, a0 = one(q0, 0, step, m0, l0, a0)
-            m1, l1, a1 = one(q1, 1, step, m1, l1, a1)
-            return m0, l0, a0, m1, l1, a1
-
-        low = jnp.full((1, TILE), -2e30, F32)
-        none = jnp.zeros((1, TILE), F32)
-        blank = jnp.zeros((HEAD, TILE), F32)
-        m0, l0, a0, m1, l1, a1 = lax.fori_loop(
-            table[1 + tile],
-            table[1 + geo.tiles + tile],
-            key_tile,
-            (low, none, blank, low, none, blank),
+            acc0, acc1 = carry
+            step = pl.multiple_of(index * KEYS, KEYS)
+            p0 = jnp.exp(scores(0, step, at))
+            p1 = jnp.exp(scores(1, step, at))
+            return acc0 + weighted(0, step, p0), acc1 + weighted(1, step, p1)
+
+        blank = jnp.zeros((TILE, LANES), F32)
+        acc0, acc1 = lax.fori_loop(
+            table[1 + tile], table[1 + geo.tiles + tile], key_tile, (blank, blank)
         )
-        out = jnp.concatenate([a0 / l0, a1 / l1], 0)
-        ob[pl.ds(at, TILE), :] = out.T.astype(BF16)
-        lse[0, 0:1, pl.ds(at, TILE)] = m0 + jnp.log(l0)
-        lse[0, 1:2, pl.ds(at, TILE)] = m1 + jnp.log(l1)
+        totals = store(at, acc0, acc1, 0.0, 0.0)
+        odd = jnp.where((totals > 1e-20) & (totals < 1e20), 0.0, 1.0)
+        worst[...] = jnp.maximum(worst[...], jnp.max(odd.reshape(TILE // 8, 8, LANES), 0))
         return 0
 
-    lax.fori_loop(0, geo.tiles, query_tile, 0)
+    def careful_tile(tile, _):
+        at = pl.multiple_of(tile * TILE, TILE)
+
+        def one_head(which, step, m, acc):
+            s = scores(which, step, at)
+            m_new = jnp.maximum(m, jnp.max(s, 1, keepdims=True))
+            acc = acc * jnp.exp(m - m_new) + weighted(which, step, jnp.exp(s - m_new))
+            return m_new, acc
+
+        def key_tile(index, carry):
+            step = pl.multiple_of(index * KEYS, KEYS)
+            return (*one_head(0, step, *carry[:2]), *one_head(1, step, *carry[2:]))
+
+        low = jnp.full((TILE, 1), -2e30, F32)
+        blank = jnp.zeros((TILE, LANES), F32)
+        m0, acc0, m1, acc1 = lax.fori_loop(
+            table[1 + tile], table[1 + geo.tiles + tile], key_tile, (low, blank, low, blank)
+        )
+        store(at, acc0, acc1, m0, m1)
+        return 0
+
+    worst[...] = jnp.zeros_like(worst)
+    lax.fori_loop(0, geo.tiles, plain_tile, 0)
+
+    @pl.when(jnp.max(worst[...]) > 0.0)
+    def _():
+        lax.fori_loop(0, geo.tiles, careful_tile, 0)
+
     scatter_rows(geo, own, mixed, pair * LANES, ob)
 
 
@@ -149,14 +181,18 @@
     qkv = refs[:peers]
     grads = refs[peers : 2 * peers]
     mixed = refs[2 * peers : 3 * peers]
-    lse, key_marks, query_marks, value_marks = refs[3 * peers : 3 * peers + 4]
-    outs = refs[3 * peers + 4 : 4 * peers + 4]
-    ka, qa, va, da, qm, dm, kn, kt, dk, dv, ob = refs[4 * peers + 4 :]
+    lse, key_marks, query_marks = refs[3 * peers : 3 * peers + 3]
+    outs = refs[3 * peers + 3 : 4 * peers + 3]
+    ka, qa, vn, qm, dm, kn, kt, dk, dv, ob, inner = refs[4 * peers + 3 :]
     pair = pl.program_id(0)
     own = table[0]
     lane = lax.broadcasted_iota(jnp.int32, (geo.chunk, LANES), 1)
     first = lane < HEAD
     zero = jnp.zeros((geo.chunk, LANES), BF16)
+    half = lax.broadcasted_iota(jnp.int32, (8, LANES), 1) // HEAD == lax.broadcasted_iota(
+        jnp.int32, (8, LANES), 0
+    )
+    half = half.astype(BF16)
 
     def put_query(offset, values):
         marks = query_marks[pl.ds(offset, geo.chunk), :]
@@ -173,46 +209,31 @@
         kn[pl.ds(offset, geo.chunk), :] = values
 
     def put_value(offset, values):
-        marks = value_marks[pl.ds(offset, geo.chunk), :]
-        va[0, pl.ds(offset, geo.chunk), :] = jnp.where(first, values, marks)
-        va[1, pl.ds(offset, geo.chunk), :] = jnp.where(first, marks, values)
+        vn[pl.ds(offset, geo.chunk), :] = values
 
     def put_mixed(offset, values):
         ob[pl.ds(offset, geo.chunk), :] = values
 
     def put_grad(offset, values):
-        product = values.astype(F32) * ob[pl.ds(offset, geo.chunk), :].astype(F32)
-        inner0 = jnp.sum(jnp.where(first, product, 0.0), 1, keepdims=True)
-        inner1 = jnp.sum(jnp.where(first, 0.0, product), 1, keepdims=True)
-
-        def digits(inner, base):
-            high = (-inner).astype(BF16)
-            rest = -inner - high.astype(F32)
-            middle = rest.astype(BF16)
-            last = (rest - middle.astype(F32)).astype(BF16)
-            spread = jnp.where(
-                lane == base,
-                high.astype(F32),
-                jnp.where(
-                    lane == base + 1,
-                    middle.astype(F32),
-                    jnp.where(lane == base + 2, last.astype(F32), 0.0),
-                ),
-            )
-            return spread.astype(BF16)
-
-        da[0, pl.ds(offset, geo.chunk), :] = jnp.where(first, values, digits(inner0, HEAD))
-        da[1, pl.ds(offset, geo.chunk), :] = jnp.where(first, digits(inner1, 0), values)
         dm[0, pl.ds(offset, geo.chunk), :] = jnp.where(first, values, zero)
         dm[1, pl.ds(offset, geo.chunk), :] = jnp.where(first, zero, values)
-
+        product = values.astype(F32) * ob[pl.ds(offset, geo.chunk), :].astype(F32)
+        high = product.astype(BF16)
+        rest = (product - high.astype(F32)).astype(BF16)
+        kn[pl.ds(offset, geo.chunk), :] = high
+        vn[pl.ds(offset, geo.chunk), :] = rest
+
+    gather_rows(geo, own, mixed, pair * LANES, put_mixed)
+    gather_rows(geo, own, grads, pair * LANES, put_grad)
+    for tile in range(geo.tiles):
+        rows = slice(tile * TILE, (tile + 1) * TILE)
+        inner[:, rows] = dot_nt(half, kn[rows, :]) + dot_nt(half, vn[rows, :])
     gather_rows(geo, own, qkv, pair * LANES, put_query)
     gather_rows(geo, own, qkv, geo.cols + pair * LANES, put_key)
     gather_rows(geo, own, qkv, 2 * geo.cols + pair * LANES, put_value)
-    gather_rows(geo, own, mixed, pair * LANES, put_mixed)
-    gather_rows(geo, own, grads, pair * LANES, put_grad)
     for tile in range(geo.tiles):
-        kt[:, tile * TILE : (tile + 1) * TILE] = kn[tile * TILE : (tile + 1) * TILE, :].T
+        rows = slice(tile * TILE, (tile + 1) * TILE)
+        kt[:, rows] = kn[rows, :].T
     dk[...] = jnp.zeros_like(dk)
     dv[...] = jnp.zeros_like(dv)
 
@@ -220,25 +241,25 @@
         at = pl.multiple_of(tile * TILE, TILE)
 
         def one(which, step):
-            s = dot_nt(ka[which, pl.ds(step, TILE), :], qa[which, pl.ds(at, TILE), :])
+            s = dot_nt(ka[which, pl.ds(step, KEYS), :], qa[which, pl.ds(at, TILE), :])
             p = jnp.exp(s - lse[0, which : which + 1, pl.ds(at, TILE)])
-            g = dot_nt(va[which, pl.ds(step, TILE), :], da[which, pl.ds(at, TILE), :])
-            ds = (p * g).astype(BF16)
+            g = dot_nt(vn[pl.ds(step, KEYS), :], dm[which, pl.ds(at, TILE), :])
+            ds = (p * (g - inner[which : which + 1, pl.ds(at, TILE)])).astype(BF16)
             return p.astype(BF16), ds
 
         def key_tile(index, carry):
             a0, a1 = carry
-            step = pl.multiple_of(index * TILE, TILE)
+            step = pl.multiple_of(index * KEYS, KEYS)
             p0, s0 = one(0, step)
             p1, s1 = one(1, step)
-            dv[pl.ds(step, TILE), :] += dot_nn(p0, dm[0, pl.ds(at, TILE), :]) + dot_nn(
+            dv[pl.ds(step, KEYS), :] += dot_nn(p0, dm[0, pl.ds(at, TILE), :]) + dot_nn(
                 p1, dm[1, pl.ds(at, TILE), :]
             )
-            dk[pl.ds(step, TILE), :] += dot_nn(s0, qm[0, pl.ds(at, TILE), :]) + dot_nn(
+            dk[pl.ds(step, KEYS), :] += dot_nn(s0, qm[0, pl.ds(at, TILE), :]) + dot_nn(
                 s1, qm[1, pl.ds(at, TILE), :]
             )
-            a0 = a0 + dot_nn(kt[:HEAD, pl.ds(step, TILE)], s0)
-            a1 = a1 + dot_nn(kt[HEAD:, pl.ds(step, TILE)], s1)
+            a0 = a0 + dot_nn(kt[:HEAD, pl.ds(step, KEYS)], s0)
+            a1 = a1 + dot_nn(kt[HEAD:, pl.ds(step, KEYS)], s1)
             return a0, a1
 
         blank = jnp.zeros((HEAD, TILE), F32)
@@ -278,9 +299,9 @@
             scratch_shapes=[
                 pltpu.VMEM((2, geo.slots, LANES), BF16),
                 pltpu.VMEM((2, geo.slots, LANES), BF16),
+                pltpu.VMEM((2, geo.slots, LANES), BF16),
                 pltpu.VMEM((geo.slots, LANES), BF16),
-                pltpu.VMEM((LANES, geo.slots), BF16),
-                pltpu.VMEM((geo.slots, LANES), BF16),
+                pltpu.VMEM((8, LANES), F32),
             ],
         ),
         cost_estimate=pl.CostEstimate(
@@ -291,9 +312,10 @@
     )(table, *qkv_parts, key_marks, query_marks)
 
 
-def attend_back(geo, table, qkv_parts, grad_parts, mixed_parts, lse, key_marks, query_marks, value_marks):
+def attend_back(geo, table, qkv_parts, grad_parts, mixed_parts, lse, key_marks, query_marks):
     wide_shape = (geo.wide, geo.chunk, 3 * geo.cols)
     two = pltpu.VMEM((2, geo.slots, LANES), BF16)
+    one = pltpu.VMEM((geo.slots, LANES), BF16)
     return pl.pallas_call(
         functools.partial(attend_back_kernel, geo),
         name="attend_back",
@@ -303,15 +325,15 @@
             grid=(geo.pairs,),
             in_specs=[whole_spec(a.shape) for a in (*qkv_parts, *grad_parts, *mixed_parts)]
             + [pl.BlockSpec((1, 8, geo.slots), lambda pair, table: (pair, 0, 0))]
-            + [whole_spec((geo.slots, LANES))] * 3,
+            + [whole_spec((geo.slots, LANES))] * 2,
             out_specs=[whole_spec(wide_shape)] * geo.peers,
-            scratch_shapes=[two] * 6
+            scratch_shapes=[two, two, one, two, two, one]
             + [
-                pltpu.VMEM((geo.slots, LANES), BF16),
                 pltpu.VMEM((LANES, geo.slots), BF16),
                 pltpu.VMEM((geo.slots, LANES), F32),
                 pltpu.VMEM((geo.slots, LANES), F32),
-                pltpu.VMEM((geo.slots, LANES), BF16),
+                one,
+                pltpu.VMEM((8, geo.slots), F32),
             ],
         ),
         cost_estimate=pl.CostEstimate(
@@ -319,7 +341,7 @@
             transcendentals=geo.slots * geo.slots * 6,
             bytes_accessed=12 * geo.slots * geo.cols * 2,
         ),
-    )(table, *qkv_parts, *grad_parts, *mixed_parts, lse, key_marks, query_marks, value_marks)
+    )(table, *qkv_parts, *grad_parts, *mixed_parts, lse, key_marks, query_marks)
 
 
 def marks_of(block_ids, geo):
@@ -327,15 +349,15 @@
     number = block_ids[:, None] + 1
     key_marks = (lane == number).astype(BF16)
     query_marks = jnp.where((lane < 9) & (lane != number), FAR, 0.0).astype(BF16)
-    value_marks = (lane < 3).astype(BF16)
-    return key_marks, query_marks, value_marks
+    return key_marks, query_marks
 
 
 def tile_table(block_ids, own, geo):
-    ids = block_ids.reshape(geo.tiles, TILE, 1)
-    present = jnp.any(ids == jnp.arange(-1, 8, dtype=jnp.int32), 1)
-    shared = jnp.any(present[:, None] & present[None], -1)
-    places = jnp.arange(geo.tiles, dtype=jnp.int32)
+    def present(size):
+        return jnp.any(block_ids.reshape(-1, size, 1) == jnp.arange(-1, 8, dtype=jnp.int32), 1)
+
+    shared = jnp.any(present(TILE)[:, None] & present(KEYS)[None], -1)
+    places = jnp.arange(geo.slots // KEYS, dtype=jnp.int32)
     low = jnp.min(jnp.where(shared, places, geo.tiles), 1)
     high = jnp.max(jnp.where(shared, places + 1, 0), 1)
     return jnp.concatenate([own[None], low, high]).astype(jnp.int32)
@@ -389,7 +411,7 @@
         block_ids.reshape(wide, peers, chunk), own, 1, keepdims=False
     ).reshape(rows, 1)
     valid_rows = (my_ids >= 0).astype(F32)
-    key_marks, query_marks, value_marks = marks_of(block_ids, geo)
+    key_marks, query_marks = marks_of(block_ids, geo)
     table = tile_table(block_ids, own, geo)
 
     bias_all = jnp.concatenate([b_qv[:D], jnp.zeros((D,), F32), b_qv[D:]])
@@ -465,7 +487,7 @@
     grad_w_out = jnp.concatenate([pick(grad_w_out_parts, own, g) for g in range(peers)], 0)
 
     dqkv_parts = attend_back(
-        geo, table, qkv_parts, grad_parts, mixed_parts, lse, key_marks, query_marks, value_marks
+        geo, table, qkv_parts, grad_parts, mixed_parts, lse, key_marks, query_marks
     )
     dqkv_home = [
         (send(part, -step) if step else part).reshape(rows, 3 * cols)

time: 663 us -> 590 us (0.89); the launches traced: 655 us -> 598 us
  Pallas kernels: 183 us -> 106 us
  waiting for transfers between devices: 186 us -> 209 us
    pallas_call x1, Pallas kernels: 100 us -> 40.5 us  [attend(): pl.pallas_call(functools.partial(attend_kernel, geo), name='attend', out_...]
    reduce_scatter x3, waiting for transfers between devices: 111 us -> 133 us  [reduced(): lax.psum_scatter(array.astype(BF16), 'narrow', scatter_dimension=0, tiled...]
    pallas_call x1, Pallas kernels: 83.1 us -> 65.7 us  [attend_back(): pl.pallas_call(functools.partial(attend_back_kernel, geo), name='attend_b...]
    unnamed x70 -> x69, local copies, waits for them, and re-layouts: 24.9 us -> 25.2 us
  transfers between devices with their start and end apart: 13 -> 13, of which waited for: 6 -> 7; matrix products, arithmetic and copies ran while one was open for 13% -> 14% of each run, Pallas kernels for 15% -> 7%
where the time goes in v2:
time: 590 us; the launch traced here: 598 us
  waiting for transfers between devices  209 us (35%)
  Pallas kernels  106 us (18%)
  matrix products  98.5 us (17%)
  blocking collectives  83.5 us (14%)
  local copies, waits for them, and re-layouts  43.6 us (7%)
  other arithmetic  22.1 us (4%)
  starting transfers between devices  20.7 us (4%)
  between operations  14.8 us (3%)
    reduce_scatter x3, waiting for transfers between devices, reduced(): lax.psum_scatter(array.astype(BF16), 'narrow', scatter_dimension=0, tiled...  133 us
    pallas_call x1, Pallas kernels, attend_back(): pl.pallas_call(functools.partial(attend_back_kernel, geo), name='attend_b...  65.7 us
    psum x1, waiting for transfers between devices, reduced(): return lax.psum(share, 'wide').astype(F32)  43.1 us
    pallas_call x1, Pallas kernels, attend(): pl.pallas_call(functools.partial(attend_kernel, geo), name='attend', out_...  40.5 us
    all_to_all x1, blocking collectives, regroup(): lax.all_to_all(array, 'wide', split_axis=0, concat_axis=0, tiled=True)  40.2 us
    dot_general x5, matrix products, dot_nn(): return jnp.dot(a, b, preferred_element_type=F32)  36.7 us
    psum x1, blocking collectives, per_device(): packed = lax.psum(packed, 'wide')  27.5 us
    all_to_all x4, waiting for transfers between devices, regroup(): lax.all_to_all(array, 'wide', split_axis=0, concat_axis=0, tiled=True)  27.1 us
  transfers between devices with their start and end apart: 13, of which 7 were waited for; matrix products, arithmetic and copies ran while one was open for 14% of the time, Pallas kernels for 7%

profile of v2, /device:TPU:0, one launch (start us, length us, event | category | flops | bytes accessed | tf_op | source)
XLA Modules:
  0.0 598.1 jit_solution(1169879711478915158)
XLA Ops:
  7.2 6.4 %all-to-all-start = ((bf16[8,128,768]{2,1,0:T(8,128)(2,1)}), bf16[8,128,768]{2,1,0:T(8,128)(2,1)S(1)}, u32[]{:S(2)}, u32[]{:S(2)}) async-start(bf16[8,128,768]{2,1,0:T(8,128)(2,1)} %bitcast.94), calls=%async_computation | async-start | bytes 3145728 | tf_op jit(solution)/shard_map/all_to_all | solution.py:402
  14.2 5.8 copy.48
  24.3 27.1 %all-to-all-done = bf16[8,128,768]{2,1,0:T(8,128)(2,1)S(1)} async-done(((bf16[8,128,768]{2,1,0:T(8,128)(2,1)}), bf16[8,128,768]{2,1,0:T(8,128)(2,1)S(1)}, u32[]{:S(2)}, u32[]{:S(2)}) %all-to-all-start) | async-done | bytes 1572896 | tf_op jit(solution)/shard_map/all_to_all | solution.py:402
  69.5 5.4 add_convert_fusion.2
  74.9 40.5 %attend.1 = (bf16[8,128,384]{2,1,0:T(8,128)(2,1)}, bf16[8,128,384]{2,1,0:T(8,128)(2,1)}, f32[3,8,2048]{2,1,0:T(8,128)}) custom-call(s32[9]{0:T(128)} %pad_add_fusion.table, bf16[8,128,1152]{2,1,0:T(8,128)(2,1)} %bitcast.112, bf16[8,128,1152]{2,1,0:T(8,128)(2,1)} %collective-permute-done.refs_1_, bf16[2048,128]{1,0:T(8,128)(2,1)} %fusion.19.refs_2_.refs_7_, ...), custom_call_target="tpu_custom_call" | custom-call | flops 6442450944 | bytes 6291456 | tf_op jit(solution)/shard_map/attend/pallas_call | solution.py:288
  120.0 4.9 fusion.35
  125.7 11.8 %multiply_convert_fusion = (bf16[1024,3072]{1,0:T(8,128)(2,1)}, f32[1024,3072]{1,0:T(8,128)}) fusion(f32[3072]{0:T(1024)S(1)} %copy-done.18, bf16[768,3072]{1,0:T(8,128)(2,1)S(1)} %bitcast.108, f32[1024,768]{1,0:T(8,128)S(1)} %get-tuple-element.100, f32[768]{0:T(1024)S(1)} %copy-done.20, f32[768]{0:T(1024)S(1)} %copy-done.14, f32[1024]{0:T(1024)S(1)} %fusion.22, ...), kind=kOutput, calls=%fused_computation.2 | convolution fusion | flops 4854644736 | bytes 26765312 | tf_op jit(solution)/shard_map/dot_general | solution.py:39
  137.6 14.0 %convert_reduce_fusion = (f32[3072]{0:T(1024)S(1)}, bf16[1024,3072]{1,0:T(8,128)(2,1)S(1)}) fusion(bf16[1024,768]{1,0:T(8,128)(2,1)S(1)} %multiply_convert_fusion.3, bf16[3072,768]{1,0:T(8,128)(2,1)S(1)} %bitcast.110, f32[1024,3072]{1,0:T(8,128)} %get-tuple-element.129, f32[3072]{0:T(1024)S(1)} %copy-done.18), kind=kOutput, calls=%fused_computation | convolution fusion | flops 4882166784 | bytes 25190400 | tf_op jit(solution)/shard_map/dot_general | solution.py:467
  151.6 5.7 multiply_reduce_fusion.1
  164.8 65.7 %attend_back.1 = (bf16[8,128,1152]{2,1,0:T(8,128)(2,1)}, bf16[8,128,1152]{2,1,0:T(8,128)(2,1)}) custom-call(s32[9]{0:T(128)} %pad_add_fusion.table, bf16[8,128,1152]{2,1,0:T(8,128)(2,1)} %bitcast.113, bf16[8,128,1152]{2,1,0:T(8,128)(2,1)} %collective-permute-done.refs_1_, bf16[8,128,384]{2,1,0:T(8,128)(2,1)} %bitcast.116, bf16[8,128,384]{2,1,0:T(8,128)(2,1)} %copy-done.17, ...), custom_call_target="tpu_custom_call" | custom-call | flops 16106127360 | bytes 18874368 | tf_op jit(solution)/shard_map/attend_back/pallas_call | solution.py:319
  235.4 8.4 %convolution_convert_fusion.2 = bf16[768,2304]{1,0:T(8,128)(2,1)} fusion(bf16[1024,1152]{1,0:T(8,128)(2,1)} %bitcast.24, bf16[1024,1152]{1,0:T(8,128)(2,1)} %bitcast.87, bf16[1024,768]{1,0:T(8,128)(2,1)S(1)} %bitcast.79, f32[768]{0:T(1024)S(1)} %copy-done.19, f32[768]{0:T(1024)S(1)} %copy-done.15, f32[1024]{0:T(1024)S(1)} %fusion.21, ...), kind=kOutput, calls=%fused_computation.7 | convolution fusion | flops 3639803904 | bytes 9844736 | tf_op jit(solution)/shard_map/td,te->de/dot_general | solution.py:502
  243.8 5.8 copy.49
  254.1 5.8 copy.52
  264.6 10.5 %convolution_convert_fusion.1 = bf16[768,3072]{1,0:T(8,128)(2,1)} fusion(bf16[1024,3072]{1,0:T(8,128)(2,1)} %copy-done.26, f32[1024,768]{1,0:T(8,128)} %copy-done, f32[768]{0:T(1024)S(1)} %copy-done.20, f32[768]{0:T(1024)S(1)} %copy-done.14, f32[1024]{0:T(1024)S(1)} %fusion.22, f32[1024]{0:T(1024)S(1)} %broadcast_multiply_fusion), kind=kOutput, calls=%fused_computation.6 | convolution fusion | flops 4838129664 | bytes 14170112 | tf_op jit(solution)/shard_map/td,tf->df/dot_general | solution.py:470
  275.2 9.4 %convolution_convert_fusion = bf16[3072,768]{1,0:T(8,128)(2,1)} fusion(bf16[1024,3072]{1,0:T(8,128)(2,1)} %get-tuple-element.128, bf16[1024,768]{1,0:T(8,128)(2,1)} %copy-done.5), kind=kOutput, calls=%fused_computation.5 | convolution fusion | flops 4834197504 | bytes 12582912 | tf_op jit(solution)/shard_map/tf,td->fd/dot_general | solution.py:466
  284.6 7.6 %fusion.33 = (f32[768]{0:T(1024)S(1)}, f32[1024]{0:T(1024)S(1)}, f32[1024,768]{1,0:T(8,128)S(1)}) fusion(f32[768]{0:T(1024)S(1)} %copy-done.15, f32[1024]{0:T(1024)S(1)} %broadcast_multiply_fusion.1, bf16[1024,768]{1,0:T(8,128)(2,1)S(1)} %bitcast.80, bf16[768,1152]{0,1:T(8,128)(2,1)} %bitcast.90, bf16[768,1152]{0,1:T(8,128)(2,1)} %bitcast.93, ...), kind=kOutput, calls=%fused_computation.108 | convolution fusion | flops 3645110528 | bytes 12990464 | tf_op jit(solution)/shard_map/dot_general | solution.py:498
  294.5 10.6 %multiply_reduce_fusion = (f32[768]{0:T(1024)S(1)}, f32[768]{0:T(1024)S(1)}, bf16[1024,768]{1,0:T(8,128)(2,1)}, bf16[1024,768]{1,0:T(8,128)(2,1)S(1)}) fusion(bf16[8,128,768]{2,1,0:T(8,128)(2,1)S(1)} %all-to-all-done.3, f32[1024]{0:T(1024)S(1)} %bitcast.103, f32[768]{0:T(1024)S(1)} %copy-done.21, f32[1024,768]{1,0:T(8,128)S(1)} %copy-done.25, ...), kind=kOutput, calls=%fused_computation.33 | convolution fusion | flops 4850710528 | bytes 29927424 | tf_op jit(solution)/shard_map/dot_general | solution.py:39
  305.1 40.2 %all_to_all.29 = bf16[8,128,768]{2,1,0:T(8,128)(2,1)S(1)} all-to-all(bf16[8,128,768]{2,1,0:T(8,128)(2,1)S(1)} %bitcast.97), channel_id=1, replica_groups=mesh['wide'=8,'narrow'=4] {'wide'}, dimensions={0} | all-to-all | bytes 3145728 | tf_op jit(solution)/shard_map/all_to_all | solution.py:402
  352.0 13.6 %reduce-scatter.7.cloned.1.call-done = bf16[192,768]{1,0:T(8,128)(2,1)} async-done(((bf16[768,768]{1,0:T(8,128)(2,1)}), bf16[192,768]{1,0:T(8,128)(2,1)}) %reduce-scatter.7.cloned.1.call-update) | async-done | bytes 294928 | tf_op jit(solution)/shard_map/reduce_scatter | solution.py:513
  365.6 60.0 %reduce-scatter.9.cloned.1.call-done = bf16[192,3072]{1,0:T(8,128)(2,1)} async-done(((bf16[768,3072]{1,0:T(8,128)(2,1)}), bf16[192,3072]{1,0:T(8,128)(2,1)}) %reduce-scatter.9.cloned.1.call-update) | async-done | bytes 1179664 | tf_op jit(solution)/shard_map/reduce_scatter | solution.py:513
  425.6 59.8 %reduce-scatter.11.cloned.1.call-done = bf16[768,768]{1,0:T(8,128)(2,1)} async-done(((bf16[3072,768]{1,0:T(8,128)(2,1)}), bf16[768,768]{1,0:T(8,128)(2,1)}) %reduce-scatter.11.cloned.1.call-update) | async-done | bytes 1179664 | tf_op jit(solution)/shard_map/reduce_scatter | solution.py:513
  490.4 15.7 %all-reduce = f32[4,2688]{1,0:T(4,128)S(1)} all-reduce(f32[4,2688]{1,0:T(4,128)S(1)} %concatenate.42), channel_id=3, replica_groups=mesh['wide'=8,'narrow'=4] {'narrow'}, use_global_device_ids=true, to_apply=%region_24.25.clone | all-reduce | flops 10752 | bytes 86016
  506.9 27.5 %psum.36 = f32[2688]{0:T(1024)S(1)} all-reduce(f32[2688]{0:T(1024)S(1)} %dynamic-slice_reduce_fusion), channel_id=1, replica_groups=mesh['wide'=8,'narrow'=4] {'wide'}, use_global_device_ids=true, to_apply=%region_25.26 | all-reduce | flops 2688 | bytes 21504 | tf_op jit(solution)/shard_map/psum | solution.py:531
  536.2 43.1 %all-reduce.4.cloned.1.call-done = (bf16[192,2304]{0,1:T(8,128)(2,1)}, bf16[192,768]{1,0:T(8,128)(2,1)}, bf16[192,3072]{1,0:T(8,128)(2,1)}, bf16[768,768]{1,0:T(8,128)(2,1)}) async-done(((bf16[192,2304]{0,1:T(8,128)(2,1)}, bf16[192,768]{1,0:T(8,128)(2,1)}, bf16[192,3072]{1,0:T(8,128)(2,1)}, bf16[768,768]{1,0:T(8,128)(2,1)}), (bf16[192,2304]{0,1:T(8,128)(2,1)}, bf16[192,768]{1,0:T(8,128)(2,1)}, ...) | async-done | bytes 3538960 | tf_op jit(solution)/shard_map/psum | solution.py:514
  (168 shorter events, 78.1 us)
Async XLA Ops:
  7.2 44.2 %all-to-all-start = ((bf16[8,128,768]{2,1,0:T(8,128)(2,1)}), bf16[8,128,768]{2,1,0:T(8,128)(2,1)S(1)}, u32[]{:S(2)}, u32[]{:S(2)}) async-start(bf16[8,128,768]{2,1,0:T(8,128)(2,1)} %bitcast.94), calls=%async_computation | async-start | bytes 3145728 | tf_op jit(solution)/shard_map/all_to_all | solution.py:402
  24.3 31.4 %copy-start.15 = (f32[768]{0:T(1024)S(1)}, f32[768]{0:T(1024)}, u32[]{:S(2)}) copy-start(f32[768]{0:T(1024)} %param.25) | copy-start | bytes 9220
  24.3 31.4 %copy-start.19 = (f32[768]{0:T(1024)S(1)}, f32[768]{0:T(1024)}, u32[]{:S(2)}) copy-start(f32[768]{0:T(1024)} %param.26) | copy-start | bytes 9220
  51.4 9.2 %all-to-all-start.1 = ((s32[8,1,256]{2,1,0:T(1,128)}), s32[8,1,256]{2,1,0:T(1,128)S(1)}, u32[]{:S(2)}, u32[]{:S(2)}) async-start(s32[8,1,256]{2,1,0:T(1,128)} %all_to_all.19), calls=%async_computation.1 | async-start | bytes 16384 | tf_op jit(solution)/shard_map/all_to_all | solution.py:402
  60.1 14.8 %collective-permute-start = (bf16[8,128,1152]{2,1,0:T(8,128)(2,1)}, bf16[8,128,1152]{2,1,0:T(8,128)(2,1)}, u32[]{:S(2)}, u32[]{:S(2)}) collective-permute-start(bf16[8,128,1152]{2,1,0:T(8,128)(2,1)} %bitcast.8), channel_id=1, source_target_pairs={{0,4},{4,0},{8,12},{12,8},{16,20},{20,16},{24,28},{28,24},{1,5},{5... | collective-permute-start | bytes 7077896 | tf_op jit(solution)/shard_map/ppermute | solution.py:435
  61.2 57.1 %all-to-all-start.3 = ((bf16[8,128,768]{2,1,0:T(8,128)(2,1)}), bf16[8,128,768]{2,1,0:T(8,128)(2,1)S(1)}, u32[]{:S(2)}, u32[]{:S(2)}) async-start(bf16[8,128,768]{2,1,0:T(8,128)(2,1)} %bitcast.95), calls=%async_computation.3 | async-start | bytes 3145728 | tf_op jit(solution)/shard_map/all_to_all | solution.py:402
  65.9 283.7 %reduce-scatter.13.cloned.1.call-start = ((), (), s32[]{:S(2)}) async-start(), calls=%async_computation.12 | async-start | bytes 4423680
  74.9 43.4 %copy-start.11 = (f32[768]{0:T(1024)S(1)}, f32[768]{0:T(1024)}, u32[]{:S(2)}) copy-start(f32[768]{0:T(1024)} %param.33) | copy-start | bytes 9220
  115.4 3.4 collective-permute-start.1
  118.8 18.8 %copy-start.5 = (bf16[1024,768]{1,0:T(8,128)(2,1)}, bf16[1024,768]{1,0:T(8,128)(2,1)S(1)}, u32[]{:S(2)}) copy-start(bf16[1024,768]{1,0:T(8,128)(2,1)S(1)} %multiply_convert_fusion.3) | copy-start | bytes 4718596
  118.8 6.7 %slice-start = ((s8[4718592]{0:T(1024)(128)(4,1)}), s8[4194304]{0:T(1024)(128)(4,1)S(1)}, s32[]{:S(2)}) async-start(s8[4718592]{0:T(1024)(128)(4,1)} %bitcast.107), calls=%async_computation.14 | async-start | bytes 8388608
  124.9 32.3 %copy-start = (f32[1024,768]{1,0:T(8,128)}, f32[1024,768]{1,0:T(8,128)S(1)}, u32[]{:S(2)}) copy-start(f32[1024,768]{1,0:T(8,128)S(1)} %get-tuple-element.100) | copy-start | bytes 9437188
  125.0 12.6 %slice-start.2 = ((s8[4718592]{0:T(1024)(128)(4,1)}), s8[4194304]{0:T(1024)(128)(4,1)S(1)}, s32[]{:S(2)}) async-start(s8[4718592]{0:T(1024)(128)(4,1)} %bitcast.109), calls=%async_computation.16 | async-start | bytes 8388608
  125.7 11.9 %slice-start.3 = ((s8[4718592]{0:T(1024)(128)(4,1)}), s8[524288]{0:T(1024)(128)(4,1)S(1)}, s32[]{:S(2)}) async-start(s8[4718592]{0:T(1024)(128)(4,1)} %bitcast.109), calls=%async_computation.17 | async-start | bytes 1048576
  161.5 2.4 collective-permute-start.2
  230.4 4.9 collective-permute-start.3
  259.9 105.7 %reduce-scatter.7.cloned.1.call-start = ((), (), s32[]{:S(2)}) async-start(), calls=%async_computation.9 | async-start | bytes 1474560 | tf_op jit(solution)/shard_map/reduce_scatter | solution.py:513
  264.5 161.1 %reduce-scatter.9.cloned.1.call-start = ((), (), s32[]{:S(2)}) async-start(), calls=%async_computation.10 | async-start | bytes 5898240 | tf_op jit(solution)/shard_map/reduce_scatter | solution.py:513
  275.1 210.3 %reduce-scatter.11.cloned.1.call-start = ((), (), s32[]{:S(2)}) async-start(), calls=%async_computation.11 | async-start | bytes 5898240 | tf_op jit(solution)/shard_map/reduce_scatter | solution.py:513
  284.6 9.4 %copy-start.3 = (f32[1024,768]{1,0:T(8,128)S(1)}, f32[1024,768]{1,0:T(8,128)}, u32[]{:S(2)}) copy-start(f32[1024,768]{1,0:T(8,128)} %copy-done.2) | copy-start | bytes 9437188
  284.6 9.4 %copy-start.25 = (f32[1024,768]{1,0:T(8,128)S(1)}, f32[1024,768]{1,0:T(8,128)}, u32[]{:S(2)}) copy-start(f32[1024,768]{1,0:T(8,128)} %get-tuple-element.127) | copy-start | bytes 9437188
  345.3 190.9 %all-to-all-start.4 = ((bf16[8,128,768]{2,1,0:T(8,128)(2,1)}), bf16[8,128,768]{2,1,0:T(8,128)(2,1)}, u32[]{:S(2)}, u32[]{:S(2)}) async-start(bf16[8,128,768]{2,1,0:T(8,128)(2,1)} %bitcast.96), calls=%async_computation.4 | async-start | bytes 3145728 | tf_op jit(solution)/shard_map/all_to_all | solution.py:402
  349.6 135.9 %copy-start.24 = (u32[32]{0:T(128)S(1)}, u32[32]{0:T(128)}, u32[]{:S(2)}) copy-start(u32[32]{0:T(128)} %constant.131) | copy-start | bytes 388
  349.6 229.7 %all-reduce.4.cloned.1.call-start = ((), (), s32[]{:S(2)}) async-start(), calls=%async_computation.13 | async-start | bytes 7667712 | tf_op jit(solution)/shard_map/psum | solution.py:514
  (20 other events, 57.1 us)
Sparse Core Ops, SparseCore 0:
  260.1 73.2 reduce-scatter.12
  336.9 28.6 reduce-scatter.6
  368.6 56.9 reduce-scatter.8
  428.5 56.9 reduce-scatter.10
  488.5 90.7 all-reduce.3

commit v3 on v2

--- a/solution.py
+++ b/solution.py
@@ -344,6 +344,147 @@
     )(table, *qkv_parts, *grad_parts, *mixed_parts, lse, key_marks, query_marks)
 
 
+def flipped(place, k):
+    bits = [place // 2**b % 2 for b in range(6)]
+    return sum((1 - bit if k >> b & 1 else bit) * 2**b for b, bit in enumerate(bits))
+
+
+def reduce_kernel(wide, peers, narrow, count, *refs):
+    sources, outs = refs[:count], refs[count : 2 * count]
+    firsts, partials, seconds, gathers = (
+        refs[(2 + k) * count : (3 + k) * count] for k in range(4)
+    )
+    send_sems, recv_sems = refs[6 * count :]
+    row = lax.axis_index("narrow")
+    mine = lax.axis_index("wide")
+    chip, peer = mine // peers, mine % peers
+
+    barrier = pltpu.get_barrier_semaphore()
+    for k in range(1, narrow):
+        pl.semaphore_signal(
+            barrier,
+            inc=1,
+            device_id={"narrow": flipped(row, k)},
+            device_id_type=pl.DeviceIdType.MESH,
+        )
+    for k in range(1, wide):
+        pl.semaphore_signal(
+            barrier,
+            inc=1,
+            device_id={"wide": flipped(mine, k)},
+            device_id_type=pl.DeviceIdType.MESH,
+        )
+    pl.semaphore_wait(barrier, narrow - 1 + wide - 1)
+
+    def copy(job, index, source, target, device):
+        return pltpu.make_async_remote_copy(
+            src_ref=source,
+            dst_ref=target,
+            send_sem=send_sems.at[job, index],
+            recv_sem=recv_sems.at[job, index],
+            device_id=device,
+            device_id_type=pl.DeviceIdType.MESH,
+        )
+
+    def to_row(job, k):
+        target = flipped(row, k)
+        return copy(
+            job, k - 1, sources[job].at[target], firsts[job].at[k - 1], {"narrow": target}
+        )
+
+    def to_chip(job, k):
+        target = flipped(chip, k)
+        return copy(
+            job,
+            narrow - 2 + k,
+            partials[job].at[target],
+            seconds[job].at[k - 1],
+            {"wide": target * peers + peer},
+        )
+
+    def spread(job, k):
+        place = gathers[job].at[peer, chip]
+        target = flipped(chip, k) * peers + peer
+        return copy(job, narrow + GROUPS - 3 + k, place, place, {"wide": target})
+
+    def to_peer(job, k, other):
+        place = gathers[job].at[peer, flipped(chip, k)]
+        index = narrow + 2 * GROUPS - 3 + k * (peers - 1) + other - 1
+        return copy(job, index, place, place, {"wide": chip * peers + flipped(peer, other)})
+
+    jobs = range(count)
+    rows, chips, others = range(1, narrow), range(1, GROUPS), range(1, peers)
+    started = [[to_row(job, k) for k in rows] for job in jobs]
+    for copies in started:
+        for c in copies:
+            c.start()
+    sent = [c for copies in started for c in copies]
+    second = []
+    for job in jobs:
+        for c in started[job]:
+            c.wait_recv()
+        acc = sources[job][row].astype(F32)
+        for k in rows:
+            acc = acc + firsts[job][k - 1].astype(F32)
+        partials[job][...] = acc.astype(partials[job].dtype)
+        second.append([to_chip(job, k) for k in chips])
+        for c in second[job]:
+            c.start()
+        sent += second[job]
+    third, fourth = [], []
+    for job in jobs:
+        for c in second[job]:
+            c.wait_recv()
+        acc = partials[job][chip].astype(F32)
+        for k in chips:
+            acc = acc + seconds[job][k - 1].astype(F32)
+        gathers[job][peer, chip] = acc.astype(gathers[job].dtype)
+        third.append([spread(job, k) for k in chips])
+        fourth.append([to_peer(job, 0, other) for other in others])
+        for c in third[job] + fourth[job]:
+            c.start()
+    for job in jobs:
+        for k in chips:
+            third[job][k - 1].wait_recv()
+            passed = [to_peer(job, k, other) for other in others]
+            for c in passed:
+                c.start()
+            fourth[job] += passed
+    for job in jobs:
+        for c in fourth[job]:
+            c.wait_recv()
+        outs[job][...] = gathers[job][...]
+        sent += third[job] + fourth[job]
+    for c in sent:
+        c.wait_send()
+
+
+def reduce_everywhere(wide, peers, narrow, arrays):
+    count = len(arrays)
+
+    def scratch(*lead):
+        return [pltpu.VMEM((*lead, *a.shape[2:]), a.dtype) for a in arrays]
+
+    copies = narrow - 1 + 2 * (GROUPS - 1) + GROUPS * (peers - 1)
+    in_vmem = pl.BlockSpec(memory_space=pltpu.VMEM)
+    return pl.pallas_call(
+        functools.partial(reduce_kernel, wide, peers, narrow, count),
+        name="reduce_everywhere",
+        out_shape=[jax.ShapeDtypeStruct((peers, *a.shape[1:]), a.dtype) for a in arrays],
+        in_specs=[in_vmem] * count,
+        out_specs=[in_vmem] * count,
+        scratch_shapes=scratch(narrow - 1, GROUPS)
+        + scratch(GROUPS)
+        + scratch(GROUPS - 1)
+        + scratch(peers, GROUPS)
+        + [pltpu.SemaphoreType.DMA((count, copies)), pltpu.SemaphoreType.DMA((count, copies))],
+        compiler_params=pltpu.CompilerParams(collective_id=1, has_side_effects=True),
+        cost_estimate=pl.CostEstimate(
+            flops=10**6, bytes_accessed=10**6, transcendentals=0
+        ),
+    )(*arrays)
+
+
 def marks_of(block_ids, geo):
     lane = lax.broadcasted_iota(jnp.int32, (geo.slots, LANES), 1) % HEAD
     number = block_ids[:, None] + 1
@@ -401,10 +542,12 @@
     def regroup(array):
         return lax.all_to_all(array, "wide", split_axis=0, concat_axis=0, tiled=True)
 
+    token_rows = regroup(tokens.reshape(wide, chunk, D)).reshape(rows, D)
+    cotangent, segment_ids, token_rows = lax.optimization_barrier(
+        (cotangent, segment_ids, token_rows)
+    )
     ids_out = jnp.broadcast_to(segment_ids.reshape(GROUPS, 1, geo.piece), (GROUPS, peers, geo.piece))
     block_ids = regroup(ids_out.reshape(wide, geo.piece)).reshape(geo.slots)
-    token_rows = regroup(tokens.reshape(wide, chunk, D)).reshape(rows, D)
-    cotangent, token_rows = lax.optimization_barrier((cotangent, token_rows))
     cotangent_rows = regroup(cotangent.reshape(wide, chunk, D)).reshape(rows, D)
 
     my_ids = lax.dynamic_index_in_dim(
@@ -420,35 +563,82 @@
     o_heads = w_out.reshape(peers, geo.real_cols, D)
     spare = cols - geo.real_cols
 
-    def heads_of(step):
-        group = (own + step) % peers
-        w = lax.dynamic_index_in_dim(w_heads, group, 2, keepdims=False)
-        b = lax.dynamic_index_in_dim(b_heads, group, 1, keepdims=False)
-        o = lax.dynamic_index_in_dim(o_heads, group, 0, keepdims=False)
-        w = jnp.pad(w, ((0, 0), (0, 0), (0, spare))).reshape(D, 3 * cols)
-        b = jnp.pad(b, ((0, 0), (0, spare))).reshape(3 * cols)
-        return w, b, jnp.pad(o, ((0, spare), (0, 0)))
-
-    weights = [heads_of(step) for step in range(peers)]
+    w_own = lax.dynamic_index_in_dim(w_heads, own, 2, keepdims=False)
+    w_own = jnp.pad(w_own, ((0, 0), (0, 0), (0, spare))).reshape(D, 3 * cols)
+    b_own = lax.dynamic_index_in_dim(b_heads, own, 1, keepdims=False)
+    b_own = jnp.pad(b_own, ((0, 0), (0, spare))).reshape(3 * cols)
+
+    def outward_of(step):
+        o = lax.dynamic_index_in_dim(o_heads, (own + step) % peers, 0, keepdims=False)
+        return jnp.pad(o, ((0, spare), (0, 0)))
+
+    o_parts = [outward_of(step) for step in range(peers)]
 
     def send(array, step):
         return lax.ppermute(array, "wide", ahead(wide, peers, step % peers))
+
+    def peer_share(left, right):
+        width = right.shape[1] // peers
+
+        def product(step):
+            start = (own + step) % peers * width
+            some = lax.dynamic_slice_in_dim(right, start, width, 1)
+            return lax.dot_general(left, some, (((0,), (0,)), ((), ())), preferred_element_type=F32)
+
+        travels = [send(product(step).astype(BF16), step) for step in range(1, peers)]
+        return (product(0) + sum(t.astype(F32) for t in travels)).astype(BF16)
+
+    def scattered(array):
+        return lax.psum_scatter(array, "narrow", scatter_dimension=0, tiled=True)
+
+    def over_chips(array):
+        return lax.psum(array, "wide", axis_index_groups=[
+            list(range(p, wide, peers)) for p in range(peers)
+        ])
+
+    def swap_chips(array, k):
+        pairs = [(w, (w // peers ^ k) * peers + w % peers) for w in range(wide)]
+        return lax.ppermute(array, "wide", pairs)
+
+    def paired(place, mine, theirs, axis):
+        low, high = jnp.where(place == 0, mine, theirs), jnp.where(place == 0, theirs, mine)
+        return jnp.stack([low, high], axis)
+
+    def in_order(parts, place):
+        bit = 1
+        while bit < len(parts):
+            odd = place // bit % 2 == 1
+            parts = [jnp.where(odd, parts[k ^ bit], parts[k]) for k in range(len(parts))]
+            bit *= 2
+        return parts
+
+    def added(a, b):
+        return (a.astype(F32) + b.astype(F32)).astype(BF16)
+
+    def held(*values):
+        return lax.optimization_barrier(values)
+
+    def over_peers(array):
+        return lax.all_gather(array, "wide", axis_index_groups=[
+            list(range(g, g + peers)) for g in range(0, wide, peers)
+        ])
 
     inputs = token_rows.astype(F32)
     normed, norm_first_back = jax.vjp(layer_norm, inputs, ln1_gain, ln1_bias)
     normed_low = normed.astype(BF16)
-    qkv_parts = [None] * peers
-    for step in [*range(1, peers), 0]:
-        w, b, _ = weights[step]
-        made = (dot_nn(normed_low, w) + b).astype(BF16).reshape(wide, chunk, 3 * cols)
-        qkv_parts[step] = send(made, step) if step else made
+    normed_parts = [normed_low] + [send(normed_low, step) for step in range(1, peers)]
+    qkv_parts = [
+        (dot_nn(part, w_own) + b_own).astype(BF16).reshape(wide, chunk, 3 * cols)
+        for part in normed_parts
+    ]
     *mixed_parts, lse = attend(geo, table, qkv_parts, key_marks, query_marks)
+    mixed_parts, cotangent_rows = lax.optimization_barrier((mixed_parts, cotangent_rows))
     mixed_home = [
         (send(part, -step) if step else part).reshape(rows, cols)
         for step, part in enumerate(mixed_parts)
     ]
     mixed_rows = jnp.concatenate(mixed_home, 1)
-    w_out_rel = jnp.concatenate([o for _, _, o in weights], 0)
+    w_out_rel = jnp.concatenate(o_parts, 0)
     projected = dot_nn(mixed_rows, w_out_rel) + b_out
     hidden = inputs + ls_attn * projected
     second, norm_second_back = jax.vjp(layer_norm, hidden, ln2_gain, ln2_bias)
@@ -463,57 +653,91 @@
     grad_ls_mlp = jnp.sum(grad_out * mlp_out, 0)
     grad_mlp = (ls_mlp * grad_out).astype(BF16)
     grad_b_fc2 = jnp.sum(grad_mlp.astype(F32), 0)
-    grad_w_fc2 = jnp.einsum("tf,td->fd", act_low, grad_mlp, preferred_element_type=F32)
+    grad_w_fc2 = peer_share(act_low, grad_mlp)
     grad_act = jnp.dot(grad_mlp, w_fc2.T, preferred_element_type=F32)
     grad_pre = gelu_back(grad_act)[0].astype(BF16)
+    grad_pre, grad_w_fc2 = lax.optimization_barrier((grad_pre, grad_w_fc2))
+    sums_fc2 = scattered(grad_w_fc2)
     grad_b_fc1 = jnp.sum(grad_pre.astype(F32), 0)
-    grad_w_fc1 = jnp.einsum("td,tf->df", second_low, grad_pre, preferred_element_type=F32)
+    grad_w_fc1 = peer_share(second_low, grad_pre)
     grad_second = jnp.dot(grad_pre, w_fc1.T, preferred_element_type=F32)
     grad_hidden_norm, grad_ln2_gain, grad_ln2_bias = norm_second_back(grad_second)
     grad_hidden = grad_out + grad_hidden_norm
     grad_ls_attn = jnp.sum(grad_hidden * projected, 0)
     grad_proj = (ls_attn * grad_hidden).astype(BF16)
     grad_b_out = jnp.sum(grad_proj.astype(F32), 0)
-    grad_parts = [None] * peers
-    for step in [*range(1, peers), 0]:
-        made = jnp.dot(grad_proj, weights[step][2].T, preferred_element_type=F32)
-        made = made.astype(BF16).reshape(wide, chunk, cols)
-        grad_parts[step] = send(made, step) if step else made
-    grad_w_out_rel = jnp.einsum("td,te->de", mixed_rows, grad_proj, preferred_element_type=F32)
-    grad_w_out_parts = [
-        grad_w_out_rel[step * cols : step * cols + geo.real_cols].astype(BF16)
-        for step in range(peers)
+    proj_parts = [grad_proj] + [send(grad_proj, step) for step in range(1, peers)]
+    mixed_plain = jnp.concatenate(
+        [pick([m[:, : geo.real_cols] for m in mixed_home], own, g) for g in range(peers)], 1
+    )
+    grad_w_out = peer_share(mixed_plain, grad_proj)
+    grad_parts = [
+        jnp.dot(part, o_parts[0].T, preferred_element_type=F32)
+        .astype(BF16)
+        .reshape(wide, chunk, cols)
+        for part in proj_parts
     ]
-    grad_w_out = jnp.concatenate([pick(grad_w_out_parts, own, g) for g in range(peers)], 0)
+    narrow = lax.axis_size("narrow")
+    wide_half = grad_w_fc1.shape[1]
+    grad_w_both = jnp.concatenate(
+        [
+            grad_w_fc1.reshape(narrow, -1, wide_half),
+            grad_w_out.reshape(narrow, -1, wide_half),
+        ],
+        1,
+    ).reshape(-1, wide_half)
+    grad_parts, grad_w_both, sums_fc2, output = lax.optimization_barrier(
+        (grad_parts, grad_w_both, sums_fc2, output)
+    )
+    sums_both = scattered(grad_w_both)
 
     dqkv_parts = attend_back(
         geo, table, qkv_parts, grad_parts, mixed_parts, lse, key_marks, query_marks
     )
-    dqkv_home = [
-        (send(part, -step) if step else part).reshape(rows, 3 * cols)
-        for step, part in enumerate(dqkv_parts)
+    share, step_width = D // narrow, D // peers
+    chip = lax.axis_index("wide") // peers
+    near, far = chip % 2, chip // 2
+    quarters = jnp.stack(
+        [sums_both[:, k * step_width : (k + 1) * step_width] for k in range(GROUPS)]
+    )
+    quarters = jnp.concatenate([sums_fc2.reshape(GROUPS, share, step_width), quarters], 1)
+    quarters, dqkv_parts = held(quarters, dqkv_parts)
+    quarters = quarters.reshape(2, 2, -1, step_width)
+    going = lax.dynamic_index_in_dim(quarters, 1 - near, 1, keepdims=False)
+    staying = lax.dynamic_index_in_dim(quarters, near, 1, keepdims=False)
+    going, staying, dqkv_parts = held(going, staying, dqkv_parts)
+    came = swap_chips(going, 1)
+    dqkv_parts = [part.reshape(rows, 3 * cols) for part in dqkv_parts]
+    partial = [
+        jnp.dot(part, w_own.T, preferred_element_type=F32) for part in dqkv_parts
     ]
-    grad_qkv = jnp.concatenate(dqkv_home, 1)
-    w_qkv_rel = jnp.concatenate([w for w, _, _ in weights], 1)
-    grad_normed = jnp.dot(grad_qkv, w_qkv_rel.T, preferred_element_type=F32)
-    sums_rel = jnp.sum(grad_qkv.astype(F32), 0).reshape(peers, 3, cols)[:, :, : geo.real_cols]
-    sums = jnp.stack([pick(list(sums_rel), own, g) for g in range(peers)], 1).reshape(3, D)
-    grad_b_qv = jnp.concatenate([sums[0], sums[2]])
-    grad_w_rel = jnp.einsum("td,te->de", normed_low, grad_qkv, preferred_element_type=F32)
-    grad_w_rel = grad_w_rel.astype(BF16).reshape(D, peers, 3, cols)[..., : geo.real_cols]
-    grad_w_qkv = jnp.stack(
-        [pick([grad_w_rel[:, k] for k in range(peers)], own, g) for g in range(peers)], 2
-    ).reshape(D, 3 * D)
+    for step in range(1, peers):
+        partial[step] = send(partial[step].astype(BF16), -step)
+    partial, came = held(partial, came)
+    halves = added(staying, came)
+    going = lax.dynamic_index_in_dim(halves, 1 - far, 0, keepdims=False)
+    staying = lax.dynamic_index_in_dim(halves, far, 0, keepdims=False)
+    going, staying, partial = held(going, staying, partial)
+    came = swap_chips(going, 2)
+    grad_normed = partial[0]
+    for step in range(1, peers):
+        grad_normed = grad_normed + partial[step].astype(F32)
+    grad_w_qkv = sum(
+        jnp.einsum("td,te->de", a, b, preferred_element_type=F32)
+        for a, b in zip(normed_parts, dqkv_parts)
+    ).astype(BF16)
+    sums = sum(jnp.sum(part.astype(F32), 0) for part in dqkv_parts)
+    sums = sums.reshape(3, 1, cols)[:, :, : geo.real_cols]
+    sums = jnp.where(jnp.arange(peers)[:, None] == own, sums, 0.0)
+    grad_b_qv = sums[::2].reshape(2 * D)
     grad_inputs_norm, grad_ln1_gain, grad_ln1_bias = norm_first_back(grad_normed)
-    grad_tokens = regroup(
-        (grad_hidden + grad_inputs_norm).astype(BF16).reshape(wide, chunk, D)
-    ).reshape(tokens.shape)
-
-    def reduced(array):
-        share = lax.psum_scatter(array.astype(BF16), "narrow", scatter_dimension=0, tiled=True)
-        return lax.psum(share, "wide").astype(F32)
-
-    narrow = lax.axis_size("narrow")
+    grad_rows = (grad_hidden + grad_inputs_norm).astype(BF16)
+    came, _ = held(came, grad_rows)
+    quarter = added(staying, came)
+    quarter, grad_w_qkv = held(quarter, grad_w_qkv)
+    came = swap_chips(quarter, 2)
+    grad_tokens = regroup(grad_rows.reshape(wide, chunk, D)).reshape(tokens.shape)
+
     vectors = [
         grad_b_qv,
         grad_b_out,
@@ -526,29 +750,67 @@
         grad_b_fc2,
         grad_ls_mlp,
     ]
-    packed = jnp.concatenate([v.reshape(narrow, -1) for v in vectors], 1)
-    packed = lax.psum_scatter(packed, "narrow", scatter_dimension=0, tiled=False)
-    packed = lax.psum(packed, "wide")
+    flat = jnp.concatenate([v.reshape(narrow, -1) for v in vectors], 1)
+    flat = jnp.pad(flat, ((0, 0), (0, -flat.shape[1] % (GROUPS * 8 * LANES))))
+    flat = flat.reshape(narrow, GROUPS, -1, LANES)
+    thirds = [
+        grad_w_qkv[:, t * cols : (t + 1) * cols].reshape(narrow, GROUPS, -1, cols)
+        for t in range(3)
+    ]
+    came, flat, thirds = held(came, flat, thirds)
+    pair = paired(far, quarter, came, 0)
+    pair, flat, thirds = held(pair, flat, thirds)
+    came = swap_chips(pair, 1)
+    if narrow <= GROUPS:
+        flat, *thirds = reduce_everywhere(wide, peers, narrow, [flat, *thirds])
+    else:
+        flat, *thirds = (
+            over_peers(over_chips(scattered(a))).reshape(peers, *a.shape[1:])
+            for a in (flat, *thirds)
+        )
+
+    came, flat, thirds = held(came, flat, thirds)
+    whole_share = paired(near, pair, came, 1).reshape(GROUPS, -1, step_width)
+    parts = [whole_share]
+    for k in range(1, peers):
+        parts.append(lax.ppermute(whole_share, "wide", [(w, w ^ k) for w in range(wide)]))
+    everything = jnp.stack(in_order(parts, own))
+    flat = sum(flat[p] for p in range(peers)).reshape(-1)
     small, start = [], 0
     for v in vectors:
         size = v.shape[0] // narrow
-        small.append(packed[start : start + size])
+        small.append(flat[start : start + size])
         start += size
+    sums_fc2 = everything[:, :, :share].reshape(peers, GROUPS * share, step_width)
+    sums_both = jnp.concatenate([everything[:, k, share:] for k in range(GROUPS)], 2)
+    sums_out = sums_both[:, share:].reshape(peers, share, step_width)
+    done_qkv = jnp.concatenate(
+        [
+            third[p].reshape(share, cols)[:, : geo.real_cols]
+            for third in thirds
+            for p in range(peers)
+        ],
+        1,
+    ).astype(F32)
+
+    def side_by_side(array):
+        return array.transpose(1, 0, 2).reshape(array.shape[1], -1).astype(F32)
+
     return (
         output,
         grad_tokens,
-        reduced(grad_w_qkv),
+        done_qkv,
         small[0],
-        reduced(grad_w_out),
+        side_by_side(sums_out),
         small[1],
         small[2],
         small[3],
         small[4],
         small[5],
         small[6],
-        reduced(grad_w_fc1),
+        side_by_side(sums_both[:, :share]),
         small[7],
-        reduced(grad_w_fc2),
+        side_by_side(sums_fc2),
         small[8],
         small[9],
     )

time: 590 us -> 486 us (0.82); the launches traced: 598 us -> 476 us
  waiting for transfers between devices: 209 us -> 70.9 us
  blocking collectives: 83.5 us -> 0 us
  Pallas kernels: 106 us -> 176 us
  matrix products: 98.5 us -> 114 us
  other arithmetic: 22.1 us -> 35 us
    reduce_scatter x3 -> x2, waiting for transfers between devices: 133 us -> 0.02 us  [scattered(): return lax.psum_scatter(array, 'narrow', scatter_dimension=0, tiled=True)]
    pallas_call x0 -> x1, Pallas kernels: none -> 69.4 us  [reduce_everywhere(): pl.pallas_call(functools.partial(reduce_kernel, wide, peers, narrow, coun...]
    psum x1 -> x0, waiting for transfers between devices: 43.1 us -> none  [reduced(): return lax.psum(share, 'wide').astype(F32)]
    all_to_all x1 -> x0, blocking collectives: 40.2 us -> none  [regroup(): lax.all_to_all(array, 'wide', split_axis=0, concat_axis=0, tiled=True)]
    psum x1 -> x0, blocking collectives: 27.5 us -> none  [per_device(): packed = lax.psum(packed, 'wide')]
    ppermute x0 -> x5, waiting for transfers between devices: none -> 27 us  [the longest x4 27 us: swap_chips(): return lax.ppermute(array, 'wide', pairs)]
    all_to_all x4 -> x5, waiting for transfers between devices: 27.1 us -> 43.6 us  [regroup(): lax.all_to_all(array, 'wide', split_axis=0, concat_axis=0, tiled=True)]
    unnamed x1 -> x0, blocking collectives: 15.7 us -> none
  transfers between devices with their start and end apart: 13 -> 19, of which waited for: 7 -> 6; matrix products, arithmetic and copies ran while one was open for 14% -> 26% of each run, Pallas kernels for 7% -> 37%
where the time goes in v3:
time: 486 us; the launch traced here: 476 us
  Pallas kernels  176 us (36%)
  matrix products  114 us (23%)
  waiting for transfers between devices  70.9 us (15%)
  local copies, waits for them, and re-layouts  39.7 us (8%)
  other arithmetic  35 us (7%)
  starting transfers between devices  24.7 us (5%)
  between operations  15.5 us (3%)
    pallas_call x1, Pallas kernels, reduce_everywhere(): pl.pallas_call(functools.partial(reduce_kernel, wide, peers, narrow, coun...  69.4 us
    pallas_call x1, Pallas kernels, attend_back(): pl.pallas_call(functools.partial(attend_back_kernel, geo), name='attend_b...  65.5 us
    all_to_all x5, waiting for transfers between devices, regroup(): lax.all_to_all(array, 'wide', split_axis=0, concat_axis=0, tiled=True)  43.6 us
    pallas_call x1, Pallas kernels, attend(): pl.pallas_call(functools.partial(attend_kernel, geo), name='attend', out_...  41 us
    dot_general x5, matrix products, dot_nn(): return jnp.dot(a, b, preferred_element_type=F32)  36.2 us
    ppermute x4, waiting for transfers between devices, swap_chips(): return lax.ppermute(array, 'wide', pairs)  27 us
    dot_general x6, matrix products, product(): lax.dot_general(left, some, (((0,), (0,)), ((), ())), preferred_element_t...  24.7 us
    all_to_all x5, starting transfers between devices, regroup(): lax.all_to_all(array, 'wide', split_axis=0, concat_axis=0, tiled=True)  21.9 us
  transfers between devices with their start and end apart: 19, of which 6 were waited for; matrix products, arithmetic and copies ran while one was open for 26% of the time, Pallas kernels for 37%

profile of v3, /device:TPU:0, one launch (start us, length us, event | category | flops | bytes accessed | tf_op | source)
XLA Modules:
  0.0 476.0 jit_solution(15689183867973350515)
XLA Ops:
  7.2 6.4 %all-to-all-start = ((bf16[8,128,768]{2,1,0:T(8,128)(2,1)}), bf16[8,128,768]{2,1,0:T(8,128)(2,1)S(1)}, u32[]{:S(2)}, u32[]{:S(2)}) async-start(bf16[8,128,768]{2,1,0:T(8,128)(2,1)} %bitcast.171), calls=%async_computation | async-start | bytes 3145728 | tf_op jit(solution)/shard_map/all_to_all | solution.py:543
  13.6 5.7 %copy.59 = bf16[768,2304]{0,1:T(8,128)(2,1)} copy(bf16[768,2304]{1,0:T(8,128)(2,1)} %param.20) | data formatting | bytes 7077888 | tf_op args[3]
  22.4 29.0 %all-to-all-done = bf16[8,128,768]{2,1,0:T(8,128)(2,1)S(1)} async-done(((bf16[8,128,768]{2,1,0:T(8,128)(2,1)}), bf16[8,128,768]{2,1,0:T(8,128)(2,1)S(1)}, u32[]{:S(2)}, u32[]{:S(2)}) %all-to-all-start) | async-done | bytes 1572896 | tf_op jit(solution)/shard_map/all_to_all | solution.py:543
  64.5 5.6 %add_convert_fusion.4 = bf16[1024,1152]{1,0:T(8,128)(2,1)} fusion(bf16[1024,768]{1,0:T(8,128)(2,1)} %fusion.8, bf16[768,1152]{0,1:T(8,128)(2,1)} %bitcast.167, f32[1152]{0:T(1024)S(1)} %add.269), kind=kOutput, calls=%fused_computation.18 | convolution fusion | flops 1814298624 | bytes 5706240 | tf_op jit(solution)/shard_map/dot_general | solution.py:39
  73.8 5.6 %add_convert_fusion.3 = bf16[1024,1152]{1,0:T(8,128)(2,1)} fusion(bf16[1024,768]{1,0:T(8,128)(2,1)} %collective-permute-done, bf16[768,1152]{0,1:T(8,128)(2,1)} %bitcast.168, f32[1152]{0:T(1024)S(1)} %add.269), kind=kOutput, calls=%fused_computation.17 | convolution fusion | flops 1814298624 | bytes 5706240 | tf_op jit(solution)/shard_map/dot_general | solution.py:39
  79.4 41.0 %attend.1 = (bf16[8,128,384]{2,1,0:T(8,128)(2,1)}, bf16[8,128,384]{2,1,0:T(8,128)(2,1)}, f32[3,8,2048]{2,1,0:T(8,128)}) custom-call(s32[9]{0:T(128)} %pad_add_fusion.table, bf16[8,128,1152]{2,1,0:T(8,128)(2,1)} %bitcast.197, bf16[8,128,1152]{2,1,0:T(8,128)(2,1)} %bitcast.199, bf16[2048,128]{1,0:T(8,128)(2,1)} %fusion.25.refs_2_.refs_7_, ...), custom_call_target="tpu_custom_call" | custom-call | flops 6442450944 | bytes 6291456 | tf_op jit(solution)/shard_map/attend/pallas_call | solution.py:288
  123.2 4.8 %fusion.51 = (f32[1024]{0:T(1024)S(1)}, f32[1024,768]{1,0:T(8,128)S(1)}, f32[1024,768]{1,0:T(8,128)}) fusion(f32[768]{0:T(1024)S(1)} %copy-done.39, f32[768]{0:T(1024)S(1)} %copy-done.38, bf16[1024,768]{1,0:T(8,128)(2,1)S(1)} %bitcast.146, bf16[384,768]{1,0:T(8,128)(2,1)S(1)} %get-tuple-element.162, bf16[384,768]{1,0:T(8,128)(2,1)S(1)} %get-tuple-element.161, ...), kind=kOutput, calls=%fused_computation.159 | convolution fusion | flops 1217395712 | bytes 10627072 | tf_op jit(solution)/shard_map/dot_general | solution.py:39
  130.3 8.6 %multiply_convert_fusion = (bf16[1024,3072]{1,0:T(8,128)(2,1)S(1)}, f32[1024,3072]{1,0:T(8,128)}) fusion(f32[3072]{0:T(1024)S(1)} %copy-done.42, bf16[1024,768]{1,0:T(8,128)(2,1)S(1)} %add_convert_fusion.6, bf16[768,3072]{1,0:T(8,128)(2,1)S(1)} %bitcast.194), kind=kOutput, calls=%fused_computation.1 | convolution fusion | flops 4850712576 | bytes 25178112 | tf_op jit(solution)/shard_map/dot_general | solution.py:39
  142.9 13.8 %add_convert_fusion = bf16[1024,3072]{1,0:T(8,128)(2,1)} fusion(f32[1024,3072]{1,0:T(8,128)} %get-tuple-element.191, f32[3072]{0:T(1024)S(1)} %copy-done.42, bf16[1024,768]{1,0:T(8,128)(2,1)S(1)} %get-tuple-element.135, bf16[3072,768]{1,0:T(8,128)(2,1)S(1)} %bitcast.196), kind=kOutput, calls=%fused_computation.2 | convolution fusion | flops 4875878400 | bytes 25178112 | tf_op jit(solution)/shard_map/dot_general | solution.py:657
  156.7 5.0 %add_convert_fusion.2 = bf16[3072,384]{1,0:T(8,128)(2,1)} fusion(bf16[3072,384]{1,0:T(8,128)(2,1)S(1)} %collective-permute-done.2, bf16[1024,3072]{1,0:T(8,128)(2,1)S(1)} %get-tuple-element.190, bf16[1024,768]{1,0:T(8,128)(2,1)S(1)} %get-tuple-element.135, s32[]{:T(128)S(6)} %select_n.177), kind=kOutput, calls=%fused_computation.16 | convolution fusion | flops 2419458048 | bytes 11796484 | tf_op jit(solution)/shard_map/dot_general | solution.py:586
  161.7 10.8 %multiply_reduce_fusion.1 = (f32[768]{0:T(1024)S(1)}, f32[1024]{0:T(1024)S(1)}, f32[768]{0:T(1024)S(1)}, f32[1024,768]{1,0:T(8,128)}) fusion(f32[1024,768]{1,0:T(8,128)} %copy-done, f32[1024]{0:T(1024)S(1)} %fusion.45, f32[1024]{0:T(1024)S(1)} %broadcast_multiply_fusion, f32[768]{0:T(1024)S(1)} %copy-done.36, bf16[1024,3072]{1,0:T(8,128)(2,1)} %add_convert_fusion, ...), kind=kOutput, calls=%fused_computation.32 | convolution fusion | flops 4838126592 | bytes 17323008 | tf_op jit(solution)/shard_map/dot_general | solution.py:663
  172.6 4.0 convolution_convert_fusion.1
  177.0 11.5 %fusion.50 = (f32[1024]{0:T(1024)S(1)}, f32[1024,768]{1,0:T(8,128)S(1)}, bf16[1024,768]{1,0:T(8,128)(2,1)}, f32[1024,768]{1,0:T(8,128)}) fusion(f32[1024]{0:T(1024)S(1)} %multiply_multiply_fusion.1, f32[1024,768]{1,0:T(8,128)} %copy-done, f32[1024]{0:T(1024)S(1)} %broadcast_multiply_fusion, f32[1024]{0:T(1024)S(1)} %fusion.45, ...), kind=kOutput, calls=%fused_computation.158 | convolution fusion | flops 4841274368 | bytes 25195520 | tf_op jit(solution)/shard_map/dot_general | solution.py:39
  190.8 4.3 all-to-all-start.3
  213.6 5.2 %add_convert_fusion.1 = bf16[768,1536]{1,0:T(8,128)(2,1)S(1)} fusion(bf16[768,1536]{1,0:T(8,128)(2,1)} %collective-permute-done.4, bf16[1024,768]{1,0:T(8,128)(2,1)S(1)} %copy-done.16, bf16[1024,3072]{1,0:T(8,128)(2,1)} %add_convert_fusion, s32[]{:T(128)S(6)} %select_n.179), kind=kOutput, calls=%fused_computation.15 | convolution fusion | flops 2419458048 | bytes 9437188 | tf_op jit(solution)/shard_map/dot_general | solution.py:586
  220.6 12.3 %all-to-all-done.3 = bf16[8,128,768]{2,1,0:T(8,128)(2,1)} async-done(((bf16[8,128,768]{2,1,0:T(8,128)(2,1)}), bf16[8,128,768]{2,1,0:T(8,128)(2,1)}, u32[]{:S(2)}, u32[]{:S(2)}) %all-to-all-start.3) | async-done | bytes 1572896 | tf_op jit(solution)/shard_map/all_to_all | solution.py:543
  237.0 65.5 %attend_back.1 = (bf16[8,128,1152]{2,1,0:T(8,128)(2,1)}, bf16[8,128,1152]{2,1,0:T(8,128)(2,1)}) custom-call(s32[9]{0:T(128)} %pad_add_fusion.table, bf16[8,128,1152]{2,1,0:T(8,128)(2,1)} %bitcast.198, bf16[8,128,1152]{2,1,0:T(8,128)(2,1)} %bitcast.200, bf16[8,128,384]{2,1,0:T(8,128)(2,1)} %bitcast.201, bf16[8,128,384]{2,1,0:T(8,128)(2,1)} %bitcast.202, ...), custom_call_target="tpu_custom_call" | custom-call | flops 16106127360 | bytes 18874368 | tf_op jit(solution)/shard_map/attend_back/pallas_call | solution.py:319
  310.3 5.4 %fusion.59 = f32[768,1152]{1,0:T(8,128)} fusion(bf16[1024,768]{1,0:T(8,128)(2,1)} %fusion.8, bf16[1024,1152]{1,0:T(8,128)(2,1)S(1)} %bitcast.154), kind=kOutput, calls=%fused_computation.167 | convolution fusion | flops 1811939328 | bytes 7471104 | tf_op jit(solution)/shard_map/td,te->de/dot_general | solution.py:726
  316.1 6.1 %fusion.58 = f32[1024,768]{1,0:T(8,128)} fusion(bf16[1024,1152]{1,0:T(8,128)(2,1)} %bitcast.153, bf16[768,1152]{0,1:T(8,128)(2,1)} %bitcast.169), kind=kOutput, calls=%fused_computation.166 | convolution fusion | flops 1811939328 | bytes 7274496 | tf_op jit(solution)/shard_map/dot_general | solution.py:712
  322.4 6.7 %fusion.6 = bf16[768,1152]{1,0:T(8,128)(2,1)} fusion(f32[768,1152]{1,0:T(8,128)} %fusion.59, bf16[1024,768]{1,0:T(8,128)(2,1)} %collective-permute-done, bf16[1024,1152]{1,0:T(8,128)(2,1)} %bitcast.161), kind=kOutput, calls=%fused_computation.24 | convolution fusion | flops 1813708800 | bytes 9240576 | tf_op jit(solution)/shard_map/td,te->de/dot_general | solution.py:726
  341.8 14.0 %collective-permute-done.8 = bf16[432,384]{1,0:T(8,128)(2,1)S(1)} collective-permute-done((bf16[432,384]{1,0:T(8,128)(2,1)}, bf16[432,384]{1,0:T(8,128)(2,1)S(1)}, u32[]{:S(2)}, u32[]{:S(2)}) %collective-permute-start.8) | collective-permute-done | bytes 331808 | tf_op jit(solution)/shard_map/ppermute | solution.py:601
  359.2 13.0 %collective-permute-done.9 = bf16[432,384]{1,0:T(8,128)(2,1)S(1)} collective-permute-done((bf16[432,384]{1,0:T(8,128)(2,1)S(1)}, bf16[432,384]{1,0:T(8,128)(2,1)S(1)}, u32[]{:S(2)}, u32[]{:S(2)}) %collective-permute-start.9) | collective-permute-done | bytes 331808 | tf_op jit(solution)/shard_map/ppermute | solution.py:601
  372.5 4.3 all-to-all-start.4
  376.8 69.4 %reduce_everywhere.1 = (f32[2,4,8,128]{3,2,1,0:T(8,128)}, bf16[2,4,48,384]{3,2,1,0:T(8,128)(2,1)}, bf16[2,4,48,384]{3,2,1,0:T(8,128)(2,1)}, bf16[2,4,48,384]{3,2,1,0:T(8,128)(2,1)}) custom-call(f32[4,4,8,128]{3,2,1,0:T(8,128)} %bitcast.184, bf16[4,4,48,384]{3,2,1,0:T(8,128)(2,1)} %bitcast.160, bf16[4,4,48,384]{3,2,1,0:T(8,128)(2,1)} %bitcast.159, ...), custom_call_target="tpu_custom_call" | custom-call | flops 1000000 | bytes 1000000 | tf_op jit(solution)/shard_map/reduce_everywhere/pallas_call | solution.py:470
  (240 shorter events, 102.5 us)
Async XLA Ops:
  7.2 44.2 %all-to-all-start = ((bf16[8,128,768]{2,1,0:T(8,128)(2,1)}), bf16[8,128,768]{2,1,0:T(8,128)(2,1)S(1)}, u32[]{:S(2)}, u32[]{:S(2)}) async-start(bf16[8,128,768]{2,1,0:T(8,128)(2,1)} %bitcast.171), calls=%async_computation | async-start | bytes 3145728 | tf_op jit(solution)/shard_map/all_to_all | solution.py:543
  19.3 32.0 %copy-start.41 = (s32[1,1,4,256]{3,2,1,0:T(4,128)S(1)}, s32[1,1,4,256]{3,2,1,0:T(4,128)}, u32[]{:S(2)}) copy-start(s32[1,1,4,256]{3,2,1,0:T(4,128)} %param.18) | copy-start | bytes 12292
  19.6 36.7 %copy-start.29 = (f32[768]{0:T(1024)S(1)}, f32[768]{0:T(1024)}, u32[]{:S(2)}) copy-start(f32[768]{0:T(1024)} %param.25) | copy-start | bytes 9220
  19.6 36.7 %copy-start.34 = (f32[768]{0:T(1024)S(1)}, f32[768]{0:T(1024)}, u32[]{:S(2)}) copy-start(f32[768]{0:T(1024)} %param.26) | copy-start | bytes 9220
  52.0 8.9 %all-to-all-start.1 = ((s32[8,1,256]{2,1,0:T(1,128)}), s32[8,1,256]{2,1,0:T(1,128)S(1)}, u32[]{:S(2)}, u32[]{:S(2)}) async-start(s32[8,1,256]{2,1,0:T(1,128)} %all_to_all.19), calls=%async_computation.1 | async-start | bytes 16384 | tf_op jit(solution)/shard_map/all_to_all | solution.py:543
  58.1 15.8 %collective-permute-start = (bf16[1024,768]{1,0:T(8,128)(2,1)}, bf16[1024,768]{1,0:T(8,128)(2,1)}, u32[]{:S(2)}, u32[]{:S(2)}) collective-permute-start(bf16[1024,768]{1,0:T(8,128)(2,1)} %fusion.8), channel_id=1, source_target_pairs={{0,4},{4,0},{8,12},{12,8},{16,20},{20,16},{24,28},{28,24},{1,5},{5... | collective-permute-start | bytes 4718600 | tf_op jit(solution)/shard_map/ppermute | solution.py:578
  60.9 59.6 %all-to-all-start.2 = ((bf16[8,128,768]{2,1,0:T(8,128)(2,1)}), bf16[8,128,768]{2,1,0:T(8,128)(2,1)S(1)}, u32[]{:S(2)}, u32[]{:S(2)}) async-start(bf16[8,128,768]{2,1,0:T(8,128)(2,1)} %bitcast.172), calls=%async_computation.2 | async-start | bytes 3145728 | tf_op jit(solution)/shard_map/all_to_all | solution.py:543
  64.4 168.5 %reduce-scatter.3.cloned.1.call-start = ((), (), s32[]{:S(2)}) async-start(), calls=%async_computation.7 | async-start | bytes 2949120 | tf_op jit(solution)/shard_map/reduce_scatter | solution.py:592
  79.4 42.9 %copy-start.37 = (f32[768]{0:T(1024)S(1)}, f32[768]{0:T(1024)}, u32[]{:S(2)}) copy-start(f32[768]{0:T(1024)} %param.33) | copy-start | bytes 9220
  120.4 2.7 collective-permute-start.1
  139.0 17.8 %copy-start.43 = (bf16[1024,3072]{1,0:T(8,128)(2,1)}, bf16[1024,3072]{1,0:T(8,128)(2,1)S(1)}, u32[]{:S(2)}) copy-start(bf16[1024,3072]{1,0:T(8,128)(2,1)S(1)} %get-tuple-element.190) | copy-start | bytes 18874372
  142.7 14.0 %collective-permute-start.2 = (bf16[3072,384]{1,0:T(8,128)(2,1)S(1)}, bf16[3072,384]{1,0:T(8,128)(2,1)S(1)}, u32[]{:S(2)}, u32[]{:S(2)}) collective-permute-start(bf16[3072,384]{1,0:T(8,128)(2,1)S(1)} %convolution_convert_fusion), channel_id=1, source_target_pairs={{0,4},{4,0},{8,12},{12,8},{16,20},{20,16},{24,28},{28,24},{1,5},{5... | collective-permute-start | bytes 7077896 | tf_op jit(solution)/shard_map/ppermute | solution.py:578
  176.6 37.0 %collective-permute-start.4 = (bf16[768,1536]{1,0:T(8,128)(2,1)}, bf16[768,1536]{1,0:T(8,128)(2,1)}, u32[]{:S(2)}, u32[]{:S(2)}) collective-permute-start(bf16[768,1536]{1,0:T(8,128)(2,1)} %convolution_convert_fusion.1), channel_id=1, source_target_pairs={{0,4},{4,0},{8,12},{12,8},{16,20},{20,16},{24,28},{28,24},{1,5},{5... | collective-permute-start | bytes 7077896 | tf_op jit(solution)/shard_map/ppermute | solution.py:578
  190.6 19.4 %collective-permute-start.3 = (bf16[1024,768]{1,0:T(8,128)(2,1)}, bf16[1024,768]{1,0:T(8,128)(2,1)}, u32[]{:S(2)}, u32[]{:S(2)}) collective-permute-start(bf16[1024,768]{1,0:T(8,128)(2,1)} %get-tuple-element.137), channel_id=1, source_target_pairs={{0,4},{4,0},{8,12},{12,8},{16,20},{20,16},{24,28},{28,24},{1,5},{5... | collective-permute-start | bytes 4718600 | tf_op jit(solution)/shard_map/ppermute | solution.py:578
  190.8 42.1 %all-to-all-start.3 = ((bf16[8,128,768]{2,1,0:T(8,128)(2,1)}), bf16[8,128,768]{2,1,0:T(8,128)(2,1)}, u32[]{:S(2)}, u32[]{:S(2)}) async-start(bf16[8,128,768]{2,1,0:T(8,128)(2,1)} %bitcast.173), calls=%async_computation.4 | async-start | bytes 3145728 | tf_op jit(solution)/shard_map/all_to_all | solution.py:543
  195.1 107.5 %reduce-scatter.5.cloned.1.call-start = ((), (), s32[]{:S(2)}) async-start(), calls=%async_computation.8 | async-start | bytes 3686400 | tf_op jit(solution)/shard_map/reduce_scatter | solution.py:592
  200.3 4.2 collective-permute-start.5
  309.9 19.2 %collective-permute-start.6 = (bf16[1024,768]{1,0:T(8,128)(2,1)}, bf16[1024,768]{1,0:T(8,128)(2,1)}, u32[]{:S(2)}, u32[]{:S(2)}) collective-permute-start(bf16[1024,768]{1,0:T(8,128)(2,1)} %convolution_convert_fusion.2), channel_id=1, source_target_pairs={{0,4},{4,0},{8,12},{12,8},{16,20},{20,16},{24,28},{28,24},{1,5},{5... | collective-permute-start | bytes 4718600 | tf_op jit(solution)/shard_map/ppermute | solution.py:578
  309.9 19.2 %collective-permute-start.7 = (bf16[2,432,384]{2,1,0:T(8,128)(2,1)}, bf16[2,432,384]{2,1,0:T(8,128)(2,1)}, u32[]{:S(2)}, u32[]{:S(2)}) collective-permute-start(bf16[2,432,384]{2,1,0:T(8,128)(2,1)} %get-tuple-element.94), channel_id=1, source_target_pairs={{0,8},{4,12},{8,0},{12,4},{16,24},{20,28},{24,16},{28,20},{1,9},{5... | collective-permute-start | bytes 1990664 | tf_op jit(solution)/shard_map/ppermute | solution.py:601
  337.2 18.5 %collective-permute-start.8 = (bf16[432,384]{1,0:T(8,128)(2,1)}, bf16[432,384]{1,0:T(8,128)(2,1)S(1)}, u32[]{:S(2)}, u32[]{:S(2)}) collective-permute-start(bf16[432,384]{1,0:T(8,128)(2,1)} %get-tuple-element.101), channel_id=1, source_target_pairs={{0,16},{4,20},{8,24},{12,28},{16,0},{20,4},{24,8},{28,12},{1,17},{... | collective-permute-start | bytes 995336 | tf_op jit(solution)/shard_map/ppermute | solution.py:601
  355.8 16.4 %collective-permute-start.9 = (bf16[432,384]{1,0:T(8,128)(2,1)S(1)}, bf16[432,384]{1,0:T(8,128)(2,1)S(1)}, u32[]{:S(2)}, u32[]{:S(2)}) collective-permute-start(bf16[432,384]{1,0:T(8,128)(2,1)S(1)} %add_convert_fusion.8), channel_id=1, source_target_pairs={{0,16},{4,20},{8,24},{12,28},{16,0},{20,4},{24,8},{28,12},{1,17},{... | collective-permute-start | bytes 995336 | tf_op jit(solution)/shard_map/ppermute | solution.py:601
  372.4 73.8 %collective-permute-start.10 = (bf16[2,432,384]{2,1,0:T(8,128)(2,1)S(1)}, bf16[2,432,384]{2,1,0:T(8,128)(2,1)S(1)}, u32[]{:S(2)}, u32[]{:S(2)}) collective-permute-start(bf16[2,432,384]{2,1,0:T(8,128)(2,1)S(1)} %pad_maximum_fusion.9), channel_id=1, source_target_pairs={{0,8},{4,12},{8,0},{12,4},{16,24},{20,28},{24,16},{28,20},{1,9},{5... | collective-permute-start | bytes 1990664 | tf_op jit(solution)/shard_map/ppermute | solution.py:601
  372.5 90.9 %all-to-all-start.4 = ((bf16[8,128,768]{2,1,0:T(8,128)(2,1)}), bf16[8,128,768]{2,1,0:T(8,128)(2,1)}, u32[]{:S(2)}, u32[]{:S(2)}) async-start(bf16[8,128,768]{2,1,0:T(8,128)(2,1)} %bitcast.36), calls=%async_computation.6 | async-start | bytes 3145728 | tf_op jit(solution)/shard_map/all_to_all | solution.py:543
  448.3 4.0 collective-permute-start.11
  (43 other events, 182.5 us)
Sparse Core Ops, SparseCore 0:
  177.1 45.4 reduce-scatter.2
  233.0 49.1 reduce-scatter.4

commit v4 on v3

--- a/solution.py
+++ b/solution.py
@@ -176,7 +176,7 @@
     scatter_rows(geo, own, mixed, pair * LANES, ob)
 
 
-def attend_back_kernel(geo, table, *refs):
+def attend_back_kernel(geo, begin, count, table, *refs):
     peers = geo.peers
     qkv = refs[:peers]
     grads = refs[peers : 2 * peers]
@@ -184,7 +184,8 @@
     lse, key_marks, query_marks = refs[3 * peers : 3 * peers + 3]
     outs = refs[3 * peers + 3 : 4 * peers + 3]
     ka, qa, vn, qm, dm, kn, kt, dk, dv, ob, inner = refs[4 * peers + 3 :]
-    pair = pl.program_id(0)
+    step_pair = pl.program_id(0)
+    pair = begin + step_pair
     own = table[0]
     lane = lax.broadcasted_iota(jnp.int32, (geo.chunk, LANES), 1)
     first = lane < HEAD
@@ -270,11 +271,11 @@
         return 0
 
     lax.fori_loop(0, geo.tiles, query_tile, 0)
-    scatter_rows(geo, own, outs, pair * LANES, ob)
+    scatter_rows(geo, own, outs, step_pair * LANES, ob)
     ob[...] = dk[...].astype(BF16)
-    scatter_rows(geo, own, outs, geo.cols + pair * LANES, ob)
+    scatter_rows(geo, own, outs, (count + step_pair) * LANES, ob)
     ob[...] = dv[...].astype(BF16)
-    scatter_rows(geo, own, outs, 2 * geo.cols + pair * LANES, ob)
+    scatter_rows(geo, own, outs, (2 * count + step_pair) * LANES, ob)
 
 
 def whole_spec(shape):
@@ -312,19 +313,19 @@
     )(table, *qkv_parts, key_marks, query_marks)
 
 
-def attend_back(geo, table, qkv_parts, grad_parts, mixed_parts, lse, key_marks, query_marks):
-    wide_shape = (geo.wide, geo.chunk, 3 * geo.cols)
+def attend_back(geo, begin, count, table, qkv_parts, grad_parts, mixed_parts, lse, key_marks, query_marks):
+    wide_shape = (geo.wide, geo.chunk, 3 * count * LANES)
     two = pltpu.VMEM((2, geo.slots, LANES), BF16)
     one = pltpu.VMEM((geo.slots, LANES), BF16)
     return pl.pallas_call(
-        functools.partial(attend_back_kernel, geo),
-        name="attend_back",
+        functools.partial(attend_back_kernel, geo, begin, count),
+        name=f"attend_back_{begin}",
         out_shape=[jax.ShapeDtypeStruct(wide_shape, BF16) for _ in range(geo.peers)],
         grid_spec=pltpu.PrefetchScalarGridSpec(
             num_scalar_prefetch=1,
-            grid=(geo.pairs,),
+            grid=(count,),
             in_specs=[whole_spec(a.shape) for a in (*qkv_parts, *grad_parts, *mixed_parts)]
-            + [pl.BlockSpec((1, 8, geo.slots), lambda pair, table: (pair, 0, 0))]
+            + [pl.BlockSpec((1, 8, geo.slots), lambda pair, table: (begin + pair, 0, 0))]
             + [whole_spec((geo.slots, LANES))] * 2,
             out_specs=[whole_spec(wide_shape)] * geo.peers,
             scratch_shapes=[two, two, one, two, two, one]
@@ -337,8 +338,8 @@
             ],
         ),
         cost_estimate=pl.CostEstimate(
-            flops=10 * geo.slots * geo.slots * geo.real_cols,
-            transcendentals=geo.slots * geo.slots * 6,
+            flops=10 * geo.slots * geo.slots * count * LANES,
+            transcendentals=geo.slots * geo.slots * 2 * count,
             bytes_accessed=12 * geo.slots * geo.cols * 2,
         ),
     )(table, *qkv_parts, *grad_parts, *mixed_parts, lse, key_marks, query_marks)
@@ -350,11 +351,12 @@
 
 
 def reduce_kernel(wide, peers, narrow, count, *refs):
-    sources, outs = refs[:count], refs[count : 2 * count]
-    firsts, partials, seconds, gathers = (
-        refs[(2 + k) * count : (3 + k) * count] for k in range(4)
-    )
-    send_sems, recv_sems = refs[6 * count :]
+    sources, given = refs[:count], refs[count]
+    outs = refs[count + 1 : 2 * count + 2]
+    scratch = refs[2 * count + 2 :]
+    firsts, partials, seconds = (scratch[k * count : (k + 1) * count] for k in range(3))
+    gathers = scratch[3 * count : 4 * count + 1]
+    send_sems, recv_sems = scratch[4 * count + 1 :]
     row = lax.axis_index("narrow")
     mine = lax.axis_index("wide")
     chip, peer = mine // peers, mine % peers
@@ -402,36 +404,81 @@
             {"wide": target * peers + peer},
         )
 
-    def spread(job, k):
-        place = gathers[job].at[peer, chip]
-        target = flipped(chip, k) * peers + peer
-        return copy(job, narrow + GROUPS - 3 + k, place, place, {"wide": target})
-
-    def to_peer(job, k, other):
-        place = gathers[job].at[peer, flipped(chip, k)]
-        index = narrow + 2 * GROUPS - 3 + k * (peers - 1) + other - 1
-        return copy(job, index, place, place, {"wide": chip * peers + flipped(peer, other)})
-
-    jobs = range(count)
     rows, chips, others = range(1, narrow), range(1, GROUPS), range(1, peers)
-    started = [[to_row(job, k) for k in rows] for job in jobs]
-    for copies in started:
+    after_chips = narrow + GROUPS - 2
+    near, far = flipped(chip, 1), flipped(chip, 2)
+
+    def place(job, k):
+        return gathers[job].at[peer, flipped(chip, k)]
+
+    def own(job):
+        return given if job == count else place(job, 0)
+
+    def to_far(job):
+        return copy(job, after_chips, own(job), place(job, 0), {"wide": far * peers + peer})
+
+    def to_near(job):
+        return copy(job, after_chips + 1, own(job), place(job, 0), {"wide": near * peers + peer})
+
+    def relay(job):
+        target = {"wide": near * peers + peer}
+        return copy(job, after_chips + 2, place(job, 2), place(job, 2), target)
+
+    sent, passed = [], [[] for _ in gathers]
+
+    def go(copies):
         for c in copies:
             c.start()
-    sent = [c for copies in started for c in copies]
+        sent.extend(copies)
+        return copies
+
+    def to_peers(job, k):
+        source = place(job, k) if k else own(job)
+        passed[job] += go(
+            [
+                copy(
+                    job,
+                    after_chips + 3 + k * (peers - 1) + other - 1,
+                    source,
+                    place(job, k),
+                    {"wide": chip * peers + flipped(peer, other)},
+                )
+                for other in others
+            ]
+        )
+
+    jobs = range(count)
+    offers = {}
+
+    def offer(job):
+        offers[job] = go([to_far(job), to_near(job)])
+        to_peers(job, 0)
+
+    def from_far(job):
+        offers[job][0].wait_recv()
+        offers[job] += go([relay(job)])
+        to_peers(job, 2)
+
+    def from_near(job):
+        offers[job][1].wait_recv()
+        to_peers(job, 1)
+        offers[job][2].wait_recv()
+        to_peers(job, 3)
+
+    offer(count)
+    gathers[count][peer, chip] = given[...]
+    first = [go([to_row(job, k) for k in rows]) for job in jobs]
     second = []
     for job in jobs:
-        for c in started[job]:
+        for c in first[job]:
             c.wait_recv()
         acc = sources[job][row].astype(F32)
         for k in rows:
             acc = acc + firsts[job][k - 1].astype(F32)
         partials[job][...] = acc.astype(partials[job].dtype)
-        second.append([to_chip(job, k) for k in chips])
-        for c in second[job]:
-            c.start()
-        sent += second[job]
-    third, fourth = [], []
+        second.append(go([to_chip(job, k) for k in chips]))
+        if job == 0:
+            from_far(count)
     for job in jobs:
         for c in second[job]:
             c.wait_recv()
@@ -439,50 +486,104 @@
         for k in chips:
             acc = acc + seconds[job][k - 1].astype(F32)
         gathers[job][peer, chip] = acc.astype(gathers[job].dtype)
-        third.append([spread(job, k) for k in chips])
-        fourth.append([to_peer(job, 0, other) for other in others])
-        for c in third[job] + fourth[job]:
-            c.start()
+        offer(job)
+    from_near(count)
     for job in jobs:
-        for k in chips:
-            third[job][k - 1].wait_recv()
-            passed = [to_peer(job, k, other) for other in others]
-            for c in passed:
-                c.start()
-            fourth[job] += passed
+        from_far(job)
     for job in jobs:
-        for c in fourth[job]:
+        from_near(job)
+    for job in (count, *jobs):
+        for c in passed[job]:
             c.wait_recv()
         outs[job][...] = gathers[job][...]
-        sent += third[job] + fourth[job]
     for c in sent:
         c.wait_send()
 
 
-def reduce_everywhere(wide, peers, narrow, arrays):
+def reduce_everywhere(wide, peers, narrow, arrays, quarter):
     count = len(arrays)
 
     def scratch(*lead):
         return [pltpu.VMEM((*lead, *a.shape[2:]), a.dtype) for a in arrays]
 
-    copies = narrow - 1 + 2 * (GROUPS - 1) + GROUPS * (peers - 1)
+    copies = narrow + 2 * GROUPS - 2 + GROUPS * (peers - 1)
     in_vmem = pl.BlockSpec(memory_space=pltpu.VMEM)
+    whole = (peers, GROUPS, *quarter.shape)
     return pl.pallas_call(
         functools.partial(reduce_kernel, wide, peers, narrow, count),
         name="reduce_everywhere",
-        out_shape=[jax.ShapeDtypeStruct((peers, *a.shape[1:]), a.dtype) for a in arrays],
-        in_specs=[in_vmem] * count,
-        out_specs=[in_vmem] * count,
+        out_shape=[jax.ShapeDtypeStruct((peers, *a.shape[1:]), a.dtype) for a in arrays]
+        + [jax.ShapeDtypeStruct(whole, quarter.dtype)],
+        in_specs=[in_vmem] * (count + 1),
+        out_specs=[in_vmem] * (count + 1),
         scratch_shapes=scratch(narrow - 1, GROUPS)
         + scratch(GROUPS)
         + scratch(GROUPS - 1)
         + scratch(peers, GROUPS)
-        + [pltpu.SemaphoreType.DMA((count, copies)), pltpu.SemaphoreType.DMA((count, copies))],
+        + [pltpu.VMEM(whole, quarter.dtype)]
+        + [pltpu.SemaphoreType.DMA((count + 1, copies))] * 2,
         compiler_params=pltpu.CompilerParams(collective_id=1, has_side_effects=True),
         cost_estimate=pl.CostEstimate(
             flops=10**6, bytes_accessed=10**6, transcendentals=0
         ),
-    )(*arrays)
+    )(*arrays, quarter)
+
+
+def assembled(blocks, peers, share, pieces, everything):
+    def rows_of(array):
+        return array.reshape(-1, array.shape[-1])
+
+    columns = [
+        rows_of(pieces[array][p])[:, start : start + width]
+        for third in range(3)
+        for p in range(peers)
+        for array, start, width, which in blocks
+        if which == third
+    ]
+    fc1 = [
+        everything[p, k, share : 2 * share] for p in range(peers) for k in range(GROUPS)
+    ]
+    out = [rows_of(everything[p, :, 2 * share :]) for p in range(peers)]
+    fc2 = [rows_of(everything[p, :, :share]) for p in range(peers)]
+    return [jnp.concatenate(parts, 1).astype(F32) for parts in (columns, out, fc1, fc2)]
+
+
+def finish_kernel(blocks, peers, share, count, *refs):
+    pieces, everything = refs[:count], refs[count]
+    qkv, out, fc1, fc2 = refs[count + 1 :]
+    step, width = share // GROUPS, everything.shape[-1]
+    for p in range(peers):
+        for k in range(GROUPS):
+            some = slice(k * step, (k + 1) * step)
+            columns = slice(p * width, (p + 1) * width)
+            fc2[k * share : (k + 1) * share, columns] = everything[p, k, :share].astype(F32)
+            start = (p * GROUPS + k) * width
+            fc1[:, start : start + width] = everything[p, k, share : 2 * share].astype(F32)
+            out[some, columns] = everything[p, k, 2 * share :].astype(F32)
+            for third in range(3):
+                place = third * D + p * (D // peers)
+                for array, column, size, which in blocks:
+                    if which == third:
+                        qkv[some, place : place + size] = pieces[array][
+                            p, k, :, column : column + size
+                        ].astype(F32)
+                        place += size
+
+
+def finish(blocks, peers, share, pieces, everything):
+    count = len(pieces)
+    in_vmem = pl.BlockSpec(memory_space=pltpu.VMEM)
+    shapes = [(share, 3 * D), (share, D), (share, 4 * D), (GROUPS * share, D)]
+    return pl.pallas_call(
+        functools.partial(finish_kernel, blocks, peers, share, count),
+        name="finish",
+        out_shape=[jax.ShapeDtypeStruct(shape, F32) for shape in shapes],
+        in_specs=[in_vmem] * (count + 1),
+        out_specs=[in_vmem] * 4,
+        cost_estimate=pl.CostEstimate(
+            flops=10**6, bytes_accessed=10**7, transcendentals=0
+        ),
+    )(*pieces, everything)
 
 
 def marks_of(block_ids, geo):
@@ -603,14 +704,6 @@
     def paired(place, mine, theirs, axis):
         low, high = jnp.where(place == 0, mine, theirs), jnp.where(place == 0, theirs, mine)
         return jnp.stack([low, high], axis)
-
-    def in_order(parts, place):
-        bit = 1
-        while bit < len(parts):
-            odd = place // bit % 2 == 1
-            parts = [jnp.where(odd, parts[k ^ bit], parts[k]) for k in range(len(parts))]
-            bit *= 2
-        return parts
 
     def added(a, b):
         return (a.astype(F32) + b.astype(F32)).astype(BF16)
@@ -647,7 +740,7 @@
     activation, gelu_back = jax.vjp(gelu_exact, pre_act)
     act_low = activation.astype(BF16)
     mlp_out = dot_nn(act_low, w_fc2) + b_fc2
-    result = ((hidden + ls_mlp * mlp_out) * valid_rows).astype(BF16)
+    result = (hidden + ls_mlp * mlp_out).astype(BF16)
     output = regroup(result.reshape(wide, chunk, D)).reshape(tokens.shape)
     grad_out = cotangent_rows.astype(F32) * valid_rows
     grad_ls_mlp = jnp.sum(grad_out * mlp_out, 0)
@@ -679,63 +772,95 @@
     ]
     narrow = lax.axis_size("narrow")
     wide_half = grad_w_fc1.shape[1]
+
+    def side_by_side(array):
+        return jnp.concatenate([array[:, k] for k in range(array.shape[1])], -1)
+
     grad_w_both = jnp.concatenate(
         [
             grad_w_fc1.reshape(narrow, -1, wide_half),
-            grad_w_out.reshape(narrow, -1, wide_half),
+            side_by_side(grad_w_out.reshape(narrow, GROUPS, -1, grad_w_out.shape[1])),
         ],
         1,
     ).reshape(-1, wide_half)
-    grad_parts, grad_w_both, sums_fc2, output = lax.optimization_barrier(
-        (grad_parts, grad_w_both, sums_fc2, output)
+    grad_parts, grad_w_both, sums_fc2 = lax.optimization_barrier(
+        (grad_parts, grad_w_both, sums_fc2)
     )
     sums_both = scattered(grad_w_both)
 
-    dqkv_parts = attend_back(
-        geo, table, qkv_parts, grad_parts, mixed_parts, lse, key_marks, query_marks
-    )
     share, step_width = D // narrow, D // peers
     chip = lax.axis_index("wide") // peers
     near, far = chip % 2, chip // 2
+    begins = [0, geo.pairs - 1] if geo.pairs > 1 else [0]
+    counts = [end - begin for begin, end in zip(begins, [*begins[1:], geo.pairs])]
+
+    def back(index):
+        return attend_back(
+            geo,
+            begins[index],
+            counts[index],
+            table,
+            qkv_parts,
+            grad_parts,
+            mixed_parts,
+            lse,
+            key_marks,
+            query_marks,
+        )
+
+    calls = [back(0)]
     quarters = jnp.stack(
         [sums_both[:, k * step_width : (k + 1) * step_width] for k in range(GROUPS)]
     )
     quarters = jnp.concatenate([sums_fc2.reshape(GROUPS, share, step_width), quarters], 1)
-    quarters, dqkv_parts = held(quarters, dqkv_parts)
+    quarters, calls = held(quarters, calls)
     quarters = quarters.reshape(2, 2, -1, step_width)
     going = lax.dynamic_index_in_dim(quarters, 1 - near, 1, keepdims=False)
     staying = lax.dynamic_index_in_dim(quarters, near, 1, keepdims=False)
-    going, staying, dqkv_parts = held(going, staying, dqkv_parts)
+    going, staying, grad_parts, calls = held(going, staying, grad_parts, calls)
     came = swap_chips(going, 1)
-    dqkv_parts = [part.reshape(rows, 3 * cols) for part in dqkv_parts]
+    calls += [back(index) for index in range(1, len(begins))]
+    came, calls, output = held(came, calls, output)
+    halves = added(staying, came)
+    going = lax.dynamic_index_in_dim(halves, 1 - far, 0, keepdims=False)
+    staying = lax.dynamic_index_in_dim(halves, far, 0, keepdims=False)
+    going, staying, calls = held(going, staying, calls)
+    came = swap_chips(going, 2)
+    output = jnp.where(segment_ids[..., None] >= 0, output, jnp.zeros_like(output))
+    calls = [[part.reshape(rows, -1) for part in made] for made in calls]
+    w_split = w_own.reshape(D, 3, geo.pairs, LANES)
+    w_calls = [
+        w_split[:, :, begin : begin + count].reshape(D, -1)
+        for begin, count in zip(begins, counts)
+    ]
     partial = [
-        jnp.dot(part, w_own.T, preferred_element_type=F32) for part in dqkv_parts
+        sum(
+            jnp.dot(made[back], w.T, preferred_element_type=F32)
+            for made, w in zip(calls, w_calls)
+        )
+        for back in range(peers)
     ]
     for step in range(1, peers):
         partial[step] = send(partial[step].astype(BF16), -step)
-    partial, came = held(partial, came)
-    halves = added(staying, came)
-    going = lax.dynamic_index_in_dim(halves, 1 - far, 0, keepdims=False)
-    staying = lax.dynamic_index_in_dim(halves, far, 0, keepdims=False)
-    going, staying, partial = held(going, staying, partial)
-    came = swap_chips(going, 2)
     grad_normed = partial[0]
     for step in range(1, peers):
         grad_normed = grad_normed + partial[step].astype(F32)
-    grad_w_qkv = sum(
-        jnp.einsum("td,te->de", a, b, preferred_element_type=F32)
-        for a, b in zip(normed_parts, dqkv_parts)
-    ).astype(BF16)
-    sums = sum(jnp.sum(part.astype(F32), 0) for part in dqkv_parts)
-    sums = sums.reshape(3, 1, cols)[:, :, : geo.real_cols]
+    sums = [
+        sum(jnp.sum(part.astype(F32), 0) for part in made).reshape(3, 1, -1) for made in calls
+    ]
+    sums = jnp.concatenate(sums, 2)[:, :, : geo.real_cols]
     sums = jnp.where(jnp.arange(peers)[:, None] == own, sums, 0.0)
     grad_b_qv = sums[::2].reshape(2 * D)
     grad_inputs_norm, grad_ln1_gain, grad_ln1_bias = norm_first_back(grad_normed)
     grad_rows = (grad_hidden + grad_inputs_norm).astype(BF16)
-    came, _ = held(came, grad_rows)
-    quarter = added(staying, came)
-    quarter, grad_w_qkv = held(quarter, grad_w_qkv)
-    came = swap_chips(quarter, 2)
+    grad_rows, calls = held(grad_rows, calls)
+    grad_w_qkv = []
+    for made, count in zip(calls, counts):
+        weight = sum(
+            jnp.einsum("td,te->de", a, b, preferred_element_type=F32)
+            for a, b in zip(normed_parts, made)
+        ).astype(BF16)
+        grad_w_qkv += [weight[:, k * 3 * LANES : (k + 1) * 3 * LANES] for k in range(count)]
     grad_tokens = regroup(grad_rows.reshape(wide, chunk, D)).reshape(tokens.shape)
 
     vectors = [
@@ -753,64 +878,58 @@
     flat = jnp.concatenate([v.reshape(narrow, -1) for v in vectors], 1)
     flat = jnp.pad(flat, ((0, 0), (0, -flat.shape[1] % (GROUPS * 8 * LANES))))
     flat = flat.reshape(narrow, GROUPS, -1, LANES)
-    thirds = [
-        grad_w_qkv[:, t * cols : (t + 1) * cols].reshape(narrow, GROUPS, -1, cols)
-        for t in range(3)
-    ]
+    thirds = [w.reshape(narrow, GROUPS, -1, 3 * LANES) for w in grad_w_qkv]
     came, flat, thirds = held(came, flat, thirds)
-    pair = paired(far, quarter, came, 0)
-    pair, flat, thirds = held(pair, flat, thirds)
-    came = swap_chips(pair, 1)
+    quarter = added(staying, came)
     if narrow <= GROUPS:
-        flat, *thirds = reduce_everywhere(wide, peers, narrow, [flat, *thirds])
+        flat, *thirds, everything = reduce_everywhere(
+            wide, peers, narrow, [flat, *thirds], quarter
+        )
     else:
+        came = swap_chips(quarter, 2)
+        pair = paired(far, quarter, came, 0)
+        whole_share = paired(near, pair, swap_chips(pair, 1), 1)
+        whole_share = whole_share.reshape(GROUPS, -1, step_width)
+        everything = over_peers(whole_share)
         flat, *thirds = (
             over_peers(over_chips(scattered(a))).reshape(peers, *a.shape[1:])
             for a in (flat, *thirds)
         )
 
-    came, flat, thirds = held(came, flat, thirds)
-    whole_share = paired(near, pair, came, 1).reshape(GROUPS, -1, step_width)
-    parts = [whole_share]
-    for k in range(1, peers):
-        parts.append(lax.ppermute(whole_share, "wide", [(w, w ^ k) for w in range(wide)]))
-    everything = jnp.stack(in_order(parts, own))
     flat = sum(flat[p] for p in range(peers)).reshape(-1)
     small, start = [], 0
     for v in vectors:
         size = v.shape[0] // narrow
         small.append(flat[start : start + size])
         start += size
-    sums_fc2 = everything[:, :, :share].reshape(peers, GROUPS * share, step_width)
-    sums_both = jnp.concatenate([everything[:, k, share:] for k in range(GROUPS)], 2)
-    sums_out = sums_both[:, share:].reshape(peers, share, step_width)
-    done_qkv = jnp.concatenate(
-        [
-            third[p].reshape(share, cols)[:, : geo.real_cols]
-            for third in thirds
-            for p in range(peers)
-        ],
-        1,
-    ).astype(F32)
-
-    def side_by_side(array):
-        return array.transpose(1, 0, 2).reshape(array.shape[1], -1).astype(F32)
+    blocks = []
+    for third in range(3):
+        for begin, count in zip(begins, counts):
+            for pair in range(begin, begin + count):
+                array, column = divmod(third * count + pair - begin, 3)
+                width = min(LANES, geo.real_cols - pair * LANES)
+                blocks.append((begin + array, column * LANES, width, third))
+    if narrow <= GROUPS:
+        matrices = finish(blocks, peers, share, thirds, everything)
+    else:
+        matrices = assembled(blocks, peers, share, thirds, everything)
+    done_qkv, done_out, done_fc1, done_fc2 = matrices
 
     return (
         output,
         grad_tokens,
         done_qkv,
         small[0],
-        side_by_side(sums_out),
+        done_out,
         small[1],
         small[2],
         small[3],
         small[4],
         small[5],
         small[6],
-        side_by_side(sums_both[:, :share]),
+        done_fc1,
         small[7],
-        side_by_side(sums_fc2),
+        done_fc2,
         small[8],
         small[9],
     )

time: 486 us -> 448 us (0.922); the launches traced: 476 us -> 444 us
  waiting for transfers between devices: 70.9 us -> 41.1 us
  local copies, waits for them, and re-layouts: 39.7 us -> 29.3 us
  Pallas kernels: 176 us -> 182 us
    ppermute x4 -> x2, waiting for transfers between devices: 27 us -> 0.01 us  [swap_chips(): return lax.ppermute(array, 'wide', pairs)]
    all_to_all x5, waiting for transfers between devices: 43.6 us -> 31.3 us  [regroup(): lax.all_to_all(array, 'wide', split_axis=0, concat_axis=0, tiled=True)]
    pallas_call x1 -> x3, Pallas kernels: 65.5 us -> 75.9 us  [the longest x2 70.6 us: attend_back(): pl.pallas_call(functools.partial(attend_back_kernel, geo, begin, count),...]
    reduce_scatter x2, waiting for transfers between devices: 0.02 us -> 9.41 us  [scattered(): return lax.psum_scatter(array, 'narrow', scatter_dimension=0, tiled=True)]
    convert_element_type x4 -> x0, local copies, waits for them, and re-layouts: 7.11 us -> none  [side_by_side(): return array.transpose(1, 0, 2).reshape(array.shape[1], -1).astype(F32)]
    unnamed x106 -> x104, local copies, waits for them, and re-layouts: 15.2 us -> 9.11 us
    dot_general x2 -> x4, matrix products: 9.47 us -> 9.87 us  [per_device(): jnp.dot(made[back], w.T, preferred_element_type=F32)]
    dot_general x2 -> x4, matrix products: 12.1 us -> 11.7 us  [per_device(): jnp.einsum('td,te->de', a, b, preferred_element_type=F32)]
  transfers between devices with their start and end apart: 19 -> 16, of which waited for: 6 -> 4; matrix products, arithmetic and copies ran while one was open for 26% -> 29% of each run, Pallas kernels for 37% -> 41%
where the time goes in v4:
time: 448 us; the launch traced here: 444 us
  Pallas kernels  182 us (41%)
  matrix products  114 us (25%)
  waiting for transfers between devices  41.1 us (9%)
  other arithmetic  34.3 us (8%)
  local copies, waits for them, and re-layouts  29.3 us (7%)
  starting transfers between devices  28.4 us (6%)
  between operations  15.1 us (3%)
    pallas_call x2, Pallas kernels, attend_back(): pl.pallas_call(functools.partial(attend_back_kernel, geo, begin, count),...  70.6 us
    pallas_call x1, Pallas kernels, reduce_everywhere(): pl.pallas_call(functools.partial(reduce_kernel, wide, peers, narrow, coun...  64.8 us
    pallas_call x1, Pallas kernels, attend(): pl.pallas_call(functools.partial(attend_kernel, geo), name='attend', out_...  41 us
    dot_general x5, matrix products, dot_nn(): return jnp.dot(a, b, preferred_element_type=F32)  36.7 us
    all_to_all x5, waiting for transfers between devices, regroup(): lax.all_to_all(array, 'wide', split_axis=0, concat_axis=0, tiled=True)  31.3 us
    dot_general x6, matrix products, product(): lax.dot_general(left, some, (((0,), (0,)), ((), ())), preferred_element_t...  23.8 us
    all_to_all x5, starting transfers between devices, regroup(): lax.all_to_all(array, 'wide', split_axis=0, concat_axis=0, tiled=True)  22.1 us
    dot_general x1, matrix products, per_device(): grad_act = jnp.dot(grad_mlp, w_fc2.T, preferred_element_type=F32)  13.8 us
  transfers between devices with their start and end apart: 16, of which 4 were waited for; matrix products, arithmetic and copies ran while one was open for 29% of the time, Pallas kernels for 41%

profile of v4, /device:TPU:0, one launch (start us, length us, event | category | flops | bytes accessed | tf_op | source)
XLA Modules:
  0.0 443.6 jit_solution(5400027777012990235)
XLA Ops:
  7.2 6.4 %all-to-all-start = ((bf16[8,128,768]{2,1,0:T(8,128)(2,1)}), bf16[8,128,768]{2,1,0:T(8,128)(2,1)S(1)}, u32[]{:S(2)}, u32[]{:S(2)}) async-start(bf16[8,128,768]{2,1,0:T(8,128)(2,1)} %bitcast.157), calls=%async_computation | async-start | bytes 3145728 | tf_op jit(solution)/shard_map/all_to_all | solution.py:644
  13.6 5.8 %copy.53 = bf16[768,2304]{0,1:T(8,128)(2,1)} copy(bf16[768,2304]{1,0:T(8,128)(2,1)} %param.20) | data formatting | bytes 7077888 | tf_op args[3]
  22.4 28.9 %all-to-all-done = bf16[8,128,768]{2,1,0:T(8,128)(2,1)S(1)} async-done(((bf16[8,128,768]{2,1,0:T(8,128)(2,1)}), bf16[8,128,768]{2,1,0:T(8,128)(2,1)S(1)}, u32[]{:S(2)}, u32[]{:S(2)}) %all-to-all-start) | async-done | bytes 1572896 | tf_op jit(solution)/shard_map/all_to_all | solution.py:644
  64.5 5.6 %add_convert_fusion.4 = bf16[1024,1152]{1,0:T(8,128)(2,1)} fusion(bf16[1024,768]{1,0:T(8,128)(2,1)} %fusion.7, bf16[768,1152]{0,1:T(8,128)(2,1)} %bitcast.139, f32[1152]{0:T(1024)S(1)} %add.292), kind=kOutput, calls=%fused_computation.16 | convolution fusion | flops 1814298624 | bytes 5706240 | tf_op jit(solution)/shard_map/dot_general | solution.py:39
  73.8 5.6 %add_convert_fusion.3 = bf16[1024,1152]{1,0:T(8,128)(2,1)} fusion(bf16[1024,768]{1,0:T(8,128)(2,1)} %collective-permute-done, bf16[768,1152]{0,1:T(8,128)(2,1)} %bitcast.140, f32[1152]{0:T(1024)S(1)} %add.292), kind=kOutput, calls=%fused_computation.15 | convolution fusion | flops 1814298624 | bytes 5706240 | tf_op jit(solution)/shard_map/dot_general | solution.py:39
  79.4 41.0 %attend.1 = (bf16[8,128,384]{2,1,0:T(8,128)(2,1)}, bf16[8,128,384]{2,1,0:T(8,128)(2,1)}, f32[3,8,2048]{2,1,0:T(8,128)}) custom-call(s32[9]{0:T(128)} %pad_add_fusion.table, bf16[8,128,1152]{2,1,0:T(8,128)(2,1)} %bitcast.183, bf16[8,128,1152]{2,1,0:T(8,128)(2,1)} %bitcast.186, bf16[2048,128]{1,0:T(8,128)(2,1)} %fusion.25.refs_2_.refs_7_, ...), custom_call_target="tpu_custom_call" | custom-call | flops 6442450944 | bytes 6291456 | tf_op jit(solution)/shard_map/attend/pallas_call | solution.py:289
  123.1 4.9 %fusion.51 = (f32[1024]{0:T(1024)S(1)}, f32[1024,768]{1,0:T(8,128)S(1)}, f32[1024,768]{1,0:T(8,128)}) fusion(f32[768]{0:T(1024)S(1)} %copy-done.37, f32[768]{0:T(1024)S(1)} %copy-done.36, bf16[1024,768]{1,0:T(8,128)(2,1)S(1)} %bitcast.130, bf16[384,768]{1,0:T(8,128)(2,1)S(1)} %get-tuple-element.162, bf16[384,768]{1,0:T(8,128)(2,1)S(1)} %get-tuple-element.161, ...), kind=kOutput, calls=%fused_computation.145 | convolution fusion | flops 1217395712 | bytes 10627072 | tf_op jit(solution)/shard_map/dot_general | solution.py:39
  130.4 8.7 %multiply_convert_fusion = (bf16[1024,3072]{1,0:T(8,128)(2,1)S(1)}, f32[1024,3072]{1,0:T(8,128)}) fusion(f32[3072]{0:T(1024)S(1)} %copy-done.42, bf16[1024,768]{1,0:T(8,128)(2,1)S(1)} %add_convert_fusion.8, bf16[768,3072]{1,0:T(8,128)(2,1)S(1)} %bitcast.180), kind=kOutput, calls=%fused_computation.1 | convolution fusion | flops 4850712576 | bytes 25178112 | tf_op jit(solution)/shard_map/dot_general | solution.py:39
  139.0 3.7 convolution_convert_fusion
  143.0 13.8 %add_convert_fusion = bf16[1024,3072]{1,0:T(8,128)(2,1)} fusion(f32[1024,3072]{1,0:T(8,128)} %get-tuple-element.187, f32[3072]{0:T(1024)S(1)} %copy-done.42, bf16[1024,768]{1,0:T(8,128)(2,1)S(1)} %get-tuple-element.146, bf16[3072,768]{1,0:T(8,128)(2,1)S(1)} %bitcast.182), kind=kOutput, calls=%fused_computation.2 | convolution fusion | flops 4875878400 | bytes 25178112 | tf_op jit(solution)/shard_map/dot_general | solution.py:750
  156.8 5.1 %add_convert_fusion.2 = bf16[3072,384]{1,0:T(8,128)(2,1)} fusion(bf16[3072,384]{1,0:T(8,128)(2,1)S(1)} %collective-permute-done.2, bf16[1024,3072]{1,0:T(8,128)(2,1)S(1)} %get-tuple-element.186, bf16[1024,768]{1,0:T(8,128)(2,1)S(1)} %get-tuple-element.146, s32[]{:T(128)S(6)} %select_n.142), kind=kOutput, calls=%fused_computation.14 | convolution fusion | flops 2419458048 | bytes 11796484 | tf_op jit(solution)/shard_map/dot_general | solution.py:687
  161.9 10.8 %multiply_reduce_fusion.1 = (f32[768]{0:T(1024)S(1)}, f32[1024]{0:T(1024)S(1)}, f32[768]{0:T(1024)S(1)}, f32[1024,768]{1,0:T(8,128)}) fusion(f32[1024,768]{1,0:T(8,128)} %copy-done, f32[1024]{0:T(1024)S(1)} %fusion.44, f32[1024]{0:T(1024)S(1)} %broadcast_multiply_fusion, f32[768]{0:T(1024)S(1)} %copy-done.34, bf16[1024,3072]{1,0:T(8,128)(2,1)} %add_convert_fusion, ...), kind=kOutput, calls=%fused_computation.28 | convolution fusion | flops 4838126592 | bytes 17323008 | tf_op jit(solution)/shard_map/dot_general | solution.py:756
  172.8 4.1 convolution_convert_fusion.1
  177.3 12.0 %fusion.50 = (f32[1024]{0:T(1024)S(1)}, f32[1024,768]{1,0:T(8,128)S(1)}, bf16[1024,768]{1,0:T(8,128)(2,1)}, f32[1024,768]{1,0:T(8,128)}) fusion(f32[1024]{0:T(1024)S(1)} %multiply_multiply_fusion.1, f32[1024,768]{1,0:T(8,128)} %copy-done, f32[1024]{0:T(1024)S(1)} %broadcast_multiply_fusion, f32[1024]{0:T(1024)S(1)} %fusion.44, ...), kind=kOutput, calls=%fused_computation.144 | convolution fusion | flops 4840487936 | bytes 25191424 | tf_op jit(solution)/shard_map/dot_general | solution.py:39
  207.5 4.2 add_convert_fusion.1
  213.5 9.4 %reduce-scatter.3.cloned.1.call-done = bf16[768,384]{1,0:T(8,128)(2,1)} async-done(((bf16[3072,384]{1,0:T(8,128)(2,1)}), bf16[768,384]{1,0:T(8,128)(2,1)}) %reduce-scatter.3.cloned.1.call-update) | async-done | bytes 589840 | tf_op jit(solution)/shard_map/reduce_scatter | solution.py:693
  222.9 4.9 %all-to-all-start.3 = ((bf16[8,128,768]{2,1,0:T(8,128)(2,1)}), bf16[8,128,768]{2,1,0:T(8,128)(2,1)}, u32[]{:S(2)}, u32[]{:S(2)}) async-start(bf16[8,128,768]{2,1,0:T(8,128)(2,1)} %bitcast.159), calls=%async_computation.5 | async-start | bytes 3145728 | tf_op jit(solution)/shard_map/all_to_all | solution.py:644
  232.8 45.2 %attend_back_0.1 = (bf16[8,128,768]{2,1,0:T(8,128)(2,1)}, bf16[8,128,768]{2,1,0:T(8,128)(2,1)}) custom-call(s32[9]{0:T(128)} %pad_add_fusion.table, bf16[8,128,1152]{2,1,0:T(8,128)(2,1)} %bitcast.184, bf16[8,128,1152]{2,1,0:T(8,128)(2,1)} %bitcast.187, bf16[8,128,384]{2,1,0:T(8,128)(2,1)} %bitcast.189, bf16[8,128,384]{2,1,0:T(8,128)(2,1)} %bitcast.191, ...), custom_call_target="tpu_custom_call" | custom-call | flops 10737418240 | bytes 18874368 | tf_op jit(solution)/shard_map/attend_back_0/pallas_call | solution.py:320
  281.8 3.7 convert_reduce_fusion
  286.3 25.4 %attend_back_2.1 = (bf16[8,128,384]{2,1,0:T(8,128)(2,1)}, bf16[8,128,384]{2,1,0:T(8,128)(2,1)}) custom-call(s32[9]{0:T(128)} %pad_add_fusion.table, bf16[8,128,1152]{2,1,0:T(8,128)(2,1)} %bitcast.185, bf16[8,128,1152]{2,1,0:T(8,128)(2,1)} %bitcast.188, bf16[8,128,384]{2,1,0:T(8,128)(2,1)} %bitcast.190, bf16[8,128,384]{2,1,0:T(8,128)(2,1)} %bitcast.192, ...), custom_call_target="tpu_custom_call" | custom-call | flops 5368709120 | bytes 18874368 | tf_op jit(solution)/shard_map/attend_back_2/pallas_call | solution.py:320
  318.3 3.8 collective-permute-start.8
  337.3 3.9 all-to-all-start.4
  362.8 64.8 %reduce_everywhere.1 = (f32[2,4,8,128]{3,2,1,0:T(8,128)}, bf16[2,4,48,384]{3,2,1,0:T(8,128)(2,1)}, bf16[2,4,48,384]{3,2,1,0:T(8,128)(2,1)}, bf16[2,4,48,384]{3,2,1,0:T(8,128)(2,1)}, bf16[2,4,432,384]{3,2,1,0:T(8,128)(2,1)}) custom-call(f32[4,4,8,128]{3,2,1,0:T(8,128)} %bitcast.171, bf16[4,4,48,384]{3,2,1,0:T(8,128)(2,1)} %bitcast.156, ...), custom_call_target="tpu_custom_call" | custom-call | flops 1000000 | bytes 1000000 | tf_op jit(solution)/shard_map/reduce_everywhere/pallas_call | solution.py:512
  429.6 5.2 %finish.1 = (f32[192,2304]{1,0:T(8,128)}, f32[192,768]{1,0:T(8,128)}, f32[192,3072]{1,0:T(8,128)}, f32[768,768]{1,0:T(8,128)}) custom-call(bf16[2,4,48,384]{3,2,1,0:T(8,128)(2,1)} %get-tuple-element.125.refs_0_, bf16[2,4,48,384]{3,2,1,0:T(8,128)(2,1)} %get-tuple-element.126.refs_1_, bf16[2,4,48,384]{3,2,1,0:T(8,128)(2,1)} %get-tuple-element.127.refs_2_, ...), custom_call_target="tpu_custom_call" | custom-call | flops 1000000 | bytes 10000000 | tf_op jit(solution)/shard_map/finish/pallas_call | solution.py:577
  (227 shorter events, 101.6 us)
Async XLA Ops:
  7.2 44.2 %all-to-all-start = ((bf16[8,128,768]{2,1,0:T(8,128)(2,1)}), bf16[8,128,768]{2,1,0:T(8,128)(2,1)S(1)}, u32[]{:S(2)}, u32[]{:S(2)}) async-start(bf16[8,128,768]{2,1,0:T(8,128)(2,1)} %bitcast.157), calls=%async_computation | async-start | bytes 3145728 | tf_op jit(solution)/shard_map/all_to_all | solution.py:644
  19.3 32.0 %copy-start.30 = (s32[1,1,4,256]{3,2,1,0:T(4,128)S(1)}, s32[1,1,4,256]{3,2,1,0:T(4,128)}, u32[]{:S(2)}) copy-start(s32[1,1,4,256]{3,2,1,0:T(4,128)} %param.18) | copy-start | bytes 12292
  19.6 36.6 %copy-start.25 = (f32[768]{0:T(1024)S(1)}, f32[768]{0:T(1024)}, u32[]{:S(2)}) copy-start(f32[768]{0:T(1024)} %param.25) | copy-start | bytes 9220
  19.6 36.6 %copy-start.32 = (f32[768]{0:T(1024)S(1)}, f32[768]{0:T(1024)}, u32[]{:S(2)}) copy-start(f32[768]{0:T(1024)} %param.26) | copy-start | bytes 9220
  52.0 8.9 %all-to-all-start.1 = ((s32[8,1,256]{2,1,0:T(1,128)}), s32[8,1,256]{2,1,0:T(1,128)S(1)}, u32[]{:S(2)}, u32[]{:S(2)}) async-start(s32[8,1,256]{2,1,0:T(1,128)} %all_to_all.19), calls=%async_computation.1 | async-start | bytes 16384 | tf_op jit(solution)/shard_map/all_to_all | solution.py:644
  58.0 15.7 %collective-permute-start = (bf16[1024,768]{1,0:T(8,128)(2,1)}, bf16[1024,768]{1,0:T(8,128)(2,1)}, u32[]{:S(2)}, u32[]{:S(2)}) collective-permute-start(bf16[1024,768]{1,0:T(8,128)(2,1)} %fusion.7), channel_id=1, source_target_pairs={{0,4},{4,0},{8,12},{12,8},{16,20},{20,16},{24,28},{28,24},{1,5},{5... | collective-permute-start | bytes 4718600 | tf_op jit(solution)/shard_map/ppermute | solution.py:679
  60.9 59.5 %all-to-all-start.2 = ((bf16[8,128,768]{2,1,0:T(8,128)(2,1)}), bf16[8,128,768]{2,1,0:T(8,128)(2,1)S(1)}, u32[]{:S(2)}, u32[]{:S(2)}) async-start(bf16[8,128,768]{2,1,0:T(8,128)(2,1)} %bitcast.158), calls=%async_computation.2 | async-start | bytes 3145728 | tf_op jit(solution)/shard_map/all_to_all | solution.py:644
  64.5 158.4 %reduce-scatter.3.cloned.1.call-start = ((), (), s32[]{:S(2)}) async-start(), calls=%async_computation.7 | async-start | bytes 2949120 | tf_op jit(solution)/shard_map/reduce_scatter | solution.py:693
  79.4 42.9 %copy-start.35 = (f32[768]{0:T(1024)S(1)}, f32[768]{0:T(1024)}, u32[]{:S(2)}) copy-start(f32[768]{0:T(1024)} %param.33) | copy-start | bytes 9220
  120.4 2.7 collective-permute-start.1
  129.8 13.3 %slice-start.4 = ((s8[4718592]{0:T(1024)(128)(4,1)}), s8[4194304]{0:T(1024)(128)(4,1)S(1)}, s32[]{:S(2)}) async-start(s8[4718592]{0:T(1024)(128)(4,1)} %bitcast.181), calls=%async_computation.13 | async-start | bytes 8388608
  130.4 12.7 %slice-start.5 = ((s8[4718592]{0:T(1024)(128)(4,1)}), s8[524288]{0:T(1024)(128)(4,1)S(1)}, s32[]{:S(2)}) async-start(s8[4718592]{0:T(1024)(128)(4,1)} %bitcast.181), calls=%async_computation.14 | async-start | bytes 1048576
  139.0 17.8 %copy-start.43 = (bf16[1024,3072]{1,0:T(8,128)(2,1)}, bf16[1024,3072]{1,0:T(8,128)(2,1)S(1)}, u32[]{:S(2)}) copy-start(bf16[1024,3072]{1,0:T(8,128)(2,1)S(1)} %get-tuple-element.186) | copy-start | bytes 18874372
  142.8 14.0 %collective-permute-start.2 = (bf16[3072,384]{1,0:T(8,128)(2,1)S(1)}, bf16[3072,384]{1,0:T(8,128)(2,1)S(1)}, u32[]{:S(2)}, u32[]{:S(2)}) collective-permute-start(bf16[3072,384]{1,0:T(8,128)(2,1)S(1)} %convolution_convert_fusion), channel_id=1, source_target_pairs={{0,4},{4,0},{8,12},{12,8},{16,20},{20,16},{24,28},{28,24},{1,5},{5... | collective-permute-start | bytes 7077896 | tf_op jit(solution)/shard_map/ppermute | solution.py:679
  161.9 10.9 %copy-start.17 = (bf16[1024,768]{1,0:T(8,128)(2,1)S(1)}, bf16[1024,768]{1,0:T(8,128)(2,1)}, u32[]{:S(2)}) copy-start(bf16[1024,768]{1,0:T(8,128)(2,1)} %copy-done.16) | copy-start | bytes 4718596
  176.9 30.6 %collective-permute-start.4 = (bf16[768,1536]{1,0:T(8,128)(2,1)}, bf16[768,1536]{1,0:T(8,128)(2,1)}, u32[]{:S(2)}, u32[]{:S(2)}) collective-permute-start(bf16[768,1536]{1,0:T(8,128)(2,1)} %convolution_convert_fusion.1), channel_id=1, source_target_pairs={{0,4},{4,0},{8,12},{12,8},{16,20},{20,16},{24,28},{28,24},{1,5},{5... | collective-permute-start | bytes 7077896 | tf_op jit(solution)/shard_map/ppermute | solution.py:679
  177.2 100.8 %reduce-scatter.5.cloned.1.call-start = ((), (), s32[]{:S(2)}) async-start(), calls=%async_computation.8 | async-start | bytes 3686400 | tf_op jit(solution)/shard_map/reduce_scatter | solution.py:693
  191.5 12.5 %collective-permute-start.3 = (bf16[1024,768]{1,0:T(8,128)(2,1)}, bf16[1024,768]{1,0:T(8,128)(2,1)}, u32[]{:S(2)}, u32[]{:S(2)}) collective-permute-start(bf16[1024,768]{1,0:T(8,128)(2,1)} %get-tuple-element.148), channel_id=1, source_target_pairs={{0,4},{4,0},{8,12},{12,8},{16,20},{20,16},{24,28},{28,24},{1,5},{5... | collective-permute-start | bytes 4718600 | tf_op jit(solution)/shard_map/ppermute | solution.py:679
  196.9 3.9 collective-permute-start.5
  222.9 88.8 %all-to-all-start.3 = ((bf16[8,128,768]{2,1,0:T(8,128)(2,1)}), bf16[8,128,768]{2,1,0:T(8,128)(2,1)}, u32[]{:S(2)}, u32[]{:S(2)}) async-start(bf16[8,128,768]{2,1,0:T(8,128)(2,1)} %bitcast.159), calls=%async_computation.5 | async-start | bytes 3145728 | tf_op jit(solution)/shard_map/all_to_all | solution.py:644
  281.8 30.0 %collective-permute-start.6 = (bf16[2,432,384]{2,1,0:T(8,128)(2,1)}, bf16[2,432,384]{2,1,0:T(8,128)(2,1)}, u32[]{:S(2)}, u32[]{:S(2)}) collective-permute-start(bf16[2,432,384]{2,1,0:T(8,128)(2,1)} %get-tuple-element.95), channel_id=1, source_target_pairs={{0,8},{4,12},{8,0},{12,4},{16,24},{20,28},{24,16},{28,20},{1,9},{5... | collective-permute-start | bytes 1990664 | tf_op jit(solution)/shard_map/ppermute | solution.py:702
  317.8 10.9 %collective-permute-start.7 = (bf16[1024,768]{1,0:T(8,128)(2,1)}, bf16[1024,768]{1,0:T(8,128)(2,1)}, u32[]{:S(2)}, u32[]{:S(2)}) collective-permute-start(bf16[1024,768]{1,0:T(8,128)(2,1)} %add_convert_fusion.6), channel_id=1, source_target_pairs={{0,4},{4,0},{8,12},{12,8},{16,20},{20,16},{24,28},{28,24},{1,5},{5... | collective-permute-start | bytes 4718600 | tf_op jit(solution)/shard_map/ppermute | solution.py:679
  318.3 42.7 %collective-permute-start.8 = (bf16[432,384]{1,0:T(8,128)(2,1)}, bf16[432,384]{1,0:T(8,128)(2,1)}, u32[]{:S(2)}, u32[]{:S(2)}) collective-permute-start(bf16[432,384]{1,0:T(8,128)(2,1)} %get-tuple-element.114), channel_id=1, source_target_pairs={{0,16},{4,20},{8,24},{12,28},{16,0},{20,4},{24,8},{28,12},{1,17},{... | collective-permute-start | bytes 995336 | tf_op jit(solution)/shard_map/ppermute | solution.py:702
  337.3 98.2 %all-to-all-start.4 = ((bf16[8,128,768]{2,1,0:T(8,128)(2,1)}), bf16[8,128,768]{2,1,0:T(8,128)(2,1)S(1)}, u32[]{:S(2)}, u32[]{:S(2)}) async-start(bf16[8,128,768]{2,1,0:T(8,128)(2,1)} %bitcast.143), calls=%async_computation.6 | async-start | bytes 3145728 | tf_op jit(solution)/shard_map/all_to_all | solution.py:644
  (42 other events, 175.5 us)
Sparse Core Ops, SparseCore 0:
  177.3 45.4 reduce-scatter.2
  225.9 42.2 reduce-scatter.4
